TPU v7x, 512 devices: a whole 4x4x16 slice. The times are simulated.
512 devices in a mesh: gx: 16 (over z_lo, core), gy: 32 (over x, z_hi, y).
Axes of the slice: x: 4, y: 4, z: 16 (z_hi: 2, z_lo: 8; z = z_hi * 8 + z_lo), core: 2. Of those that a mesh axis runs over, the one named last changes fastest.
Arguments:
- positions: float32 [3, 16, 32, 128], P(None, 'gx', 'gy'), may hold values from 0 to 20
- spring: float32 [16, 32, 128], P('gx', 'gy'), may hold values from 0.25 to 4
- border: int32 [16, 32, 32], P('gx', 'gy'), may hold values from 0 to 127, as said below
- neighbours: int32 [16, 32, 64, 128], P('gx', 'gy'), may hold values from -1 to 1055, as said below
- vec_prev: float32 [3, 8, 16, 32, 128], P(None, None, 'gx', 'gy'), may hold values from -6 to 6
- vec_now: float32 [3, 8, 16, 32, 128], P(None, None, 'gx', 'gy'), may hold values from -6 to 6
- heat_prev: float32 [3, 8, 16, 32, 128], P(None, None, 'gx', 'gy'), may hold values from -6 to 6
- heat_now: float32 [3, 8, 16, 32, 128], P(None, None, 'gx', 'gy'), may hold values from -6 to 6
Outputs:
- vec_next: float32 [3, 8, 16, 32, 128], P(None, None, 'gx', 'gy')
- vec_after: float32 [3, 8, 16, 32, 128], P(None, None, 'gx', 'gy')
- heat_next: float32 [3, 8, 16, 32, 128], P(None, None, 'gx', 'gy')
- heat_after: float32 [3, 8, 16, 32, 128], P(None, None, 'gx', 'gy')
Inputs may be any that keep to these rules, and one draw needn't show every extreme that they name: `border`: each column's row lists 32 different atoms of that column. `neighbours`: -1 marks an empty slot, and empty slots follow the used ones; an entry o * 128 + k names for o = 4 the column's own atom k, else entry k (k < 32) of the border table of the column o // 3 - 1 steps along x and o % 3 - 1 steps along y (periodic); every atom uses at least 32 slots and some atom of every column uses all 64.
All inputs are finite; a program needn't handle non-finite values.
Results may differ from a plain program's by a relative error of at most 0.0003.
Values sent between devices are 32-bit elements; how exact they have to be, the bound alone decides.
No kernel may reach another device: no remote copies, remote signals or barrier semaphores. Data moves between devices by JAX's collectives and lax.ppermute only.
A program may use at most 64 MiB of HBM per device.

v0:
```python
import jax
import jax.numpy as jnp
from jax import lax
from jax.sharding import PartitionSpec as P

column_edge = 20.0
reach_sq = 64.0
block_slots = 8


def padded(cells, sides, width):
    for axis, dim in sides:
        count = lax.axis_size(axis)
        head = lax.slice_in_dim(cells, 0, width, axis=dim)
        tail = lax.slice_in_dim(cells, cells.shape[dim] - width, cells.shape[dim], axis=dim)
        cells = jnp.concatenate(
            [
                lax.ppermute(tail, axis, [(i, (i + 1) % count) for i in range(count)]),
                cells,
                lax.ppermute(head, axis, [((i + 1) % count, i) for i in range(count)]),
            ],
            axis=dim,
        )
    return cells


def select_columns(source, index):
    one_hot = (
        lax.broadcasted_iota(jnp.int32, (source.shape[1], index.shape[0]), 0) == index[None, :]
    ).astype(jnp.float32)
    return jnp.dot(source, one_hot, precision=lax.Precision.HIGHEST)


def surround(values):
    widened = padded(values, (("gx", 1), ("gy", 2)), 1)
    return widened.reshape(values.shape[0], -1)


def shards(positions, spring, border, neighbours, vec_prev, vec_now, heat_prev, heat_now):
    n_atoms = spring.shape[-1]
    n_slots = neighbours.shape[2]
    n_border = border.shape[-1]
    n_vec = vec_prev.shape[1]
    n_blocks = n_slots // block_slots
    entries = neighbours[0, 0]
    usable = entries >= 0
    entry_safe = jnp.maximum(entries, 0)
    offset = entry_safe // n_atoms
    within = entry_safe % n_atoms
    at_home = offset == 4
    tables = padded(border, (("gx", 0), ("gy", 1)), 1).reshape(1, -1)
    table_values = tables.astype(jnp.float32)
    keyed = (offset * n_border + jnp.minimum(within, n_border - 1)).reshape(
        n_blocks, block_slots * n_atoms
    )
    remote = lax.map(lambda keys: select_columns(table_values, keys)[0], keyed)
    remote = remote.reshape(n_slots, n_atoms).astype(jnp.int32)
    source_index = offset * n_atoms + jnp.where(at_home, within, remote)

    def spread(values):
        return surround(values)

    index_blocks = source_index.reshape(n_blocks, block_slots * n_atoms)
    geometry = jnp.concatenate([positions, spring[None]], axis=0)
    geo_source = spread(geometry)
    remote_geo = lax.map(lambda keys: select_columns(geo_source, keys), index_blocks)
    remote_geo = jnp.moveaxis(remote_geo.reshape(n_blocks, 4, block_slots, n_atoms), 1, 0).reshape(
        4, n_slots, n_atoms
    )
    local_geo = geometry[:, 0, 0]
    delta_x = remote_geo[0] + (offset // 3 - 1).astype(jnp.float32) * column_edge - local_geo[0]
    delta_y = remote_geo[1] + (offset % 3 - 1).astype(jnp.float32) * column_edge - local_geo[1]
    delta_z = remote_geo[2] - local_geo[2]
    dist_sq = delta_x * delta_x + delta_y * delta_y + delta_z * delta_z
    coupling = jnp.where(
        usable,
        jnp.sqrt(local_geo[3] * remote_geo[3]) / (n_slots * (1.0 + dist_sq / reach_sq)),
        jnp.float32(0.0),
    )
    bending = 2.0 / (dist_sq + 1.0)
    displace = jnp.stack([delta_x, delta_y, delta_z])
    identity = jnp.eye(3, dtype=jnp.float32)[:, :, None, None]
    blocks = coupling[None, None] * (
        identity + bending[None, None] * displace[:, None] * displace[None, :]
    )
    self_block = jnp.sum(blocks, axis=2)

    def operate_on(current):
        n_rows = current.shape[1]
        source = spread(current.reshape(3 * n_rows, 1, 1, n_atoms))
        local_rows = current[:, :, 0, 0]
        local_term = jnp.einsum(
            "abn,brn->arn", self_block, local_rows, precision=lax.Precision.HIGHEST
        )

        def add_block(block_turn, total):
            slot_index = lax.dynamic_index_in_dim(index_blocks, block_turn, 0, keepdims=False)
            far_rows = select_columns(source, slot_index).reshape(3, n_rows, block_slots, n_atoms)
            part_blocks = lax.dynamic_slice_in_dim(blocks, block_turn * block_slots, block_slots, 2)
            return total + jnp.einsum(
                "abkn,brkn->arn", part_blocks, far_rows, precision=lax.Precision.HIGHEST
            )

        far_sum = lax.fori_loop(0, n_blocks, add_block, jnp.zeros_like(local_rows))
        return (local_term - far_sum - local_rows)[:, :, None, None]

    state_zero = jnp.concatenate([vec_prev, heat_prev], axis=1)
    state_one = jnp.concatenate([vec_now, heat_now], axis=1)
    state_two = 2.0 * operate_on(state_one) - state_zero
    state_three = 2.0 * operate_on(state_two) - state_one
    return (
        state_two[:, :n_vec],
        state_three[:, :n_vec],
        state_two[:, n_vec:],
        state_three[:, n_vec:],
    )


def solution(mesh):
    return jax.shard_map(
        shards,
        mesh=mesh,
        in_specs=(
            P(None, "gx", "gy", None),
            P("gx", "gy", None),
            P("gx", "gy", None),
            P("gx", "gy", None, None),
            P(None, None, "gx", "gy", None),
            P(None, None, "gx", "gy", None),
            P(None, None, "gx", "gy", None),
            P(None, None, "gx", "gy", None),
        ),
        out_specs=(
            P(None, None, "gx", "gy", None),
            P(None, None, "gx", "gy", None),
            P(None, None, "gx", "gy", None),
            P(None, None, "gx", "gy", None),
        ),
        check_vma=False,
    )
```

profile of v0, /device:TPU:511, one launch (start us, length us, event | category | flops | bytes accessed | tf_op | source)
XLA Modules:
  0.0 381.6 jit_solution(6089658358856776760)
XLA Ops:
  43.3 12.6 %collective-permute-done.3 = s32[3,1,32]{2,1,0:T(1,128)S(1)} collective-permute-done((s32[3,1,32]{2,1,0:T(1,128)S(1)}, s32[3,1,32]{2,1,0:T(1,128)S(1)}, u32[]{:S(2)}, u32[]{:S(2)}) %collective-permute-start.3) | collective-permute-done | bytes 416 | tf_op jit(solution)/shard_map/ppermute | solution.py:20
  66.6 15.3 %collective-permute-done.7 = f32[4,3,1,128]{3,2,1,0:T(1,128)S(1)} collective-permute-done((f32[4,3,1,128]{3,2,1,0:T(1,128)S(1)}, f32[4,3,1,128]{3,2,1,0:T(1,128)S(1)}, u32[]{:S(2)}, u32[]{:S(2)}) %collective-permute-start.7) | collective-permute-done | bytes 6176 | tf_op jit(solution)/shard_map/ppermute | solution.py:20
  82.0 12.5 %while.49 = (s32[]{:T(128)}, f32[8,4,1024]{2,1,0:T(4,128)S(1)}, s32[8,1024]{1,0:T(8,128)S(1)}, f32[4,1152]{1,0:T(4,128)S(1)}, s32[]{:T(128)}) while((s32[]{:T(128)}, f32[8,4,1024]{2,1,0:T(4,128)S(1)}, s32[8,1024]{1,0:T(8,128)S(1)}, f32[4,1152]{1,0:T(4,128)S(1)}, s32[]{:T(128)}) %tuple.108), condition=%wide.region_3.4_spmd, body=%wide.region_2.3_spmd.sunk | while | flops 57802752 | bytes 47173 | solution.py:66
  101.2 13.9 %collective-permute-done.11 = f32[48,3,1,128]{3,0,2,1:T(8,128)S(1)} collective-permute-done((f32[48,3,1,128]{3,0,2,1:T(8,128)S(1)}, f32[48,3,1,128]{3,0,2,1:T(8,128)S(1)}, u32[]{:S(2)}, u32[]{:S(2)}) %collective-permute-start.11) | collective-permute-done | bytes 73760 | tf_op jit(solution)/shard_map/ppermute | solution.py:20
  115.5 107.6 %while.50 = (s32[]{:T(128)}, f32[3,16,128]{1,0,2:T(4,128)S(1)}, s32[8,1024]{1,0:T(8,128)S(1)}, f32[48,1152]{1,0:T(8,128)S(1)}, f32[3,3,64,128]{2,0,1,3:T(4,128)S...) while((s32[]{:T(128)}, f32[3,16,128]{1,0,2:T(4,128)S(1)}, s32[8,1024]{1,0:T(8,128)S(1)}, ...), condition=%wide.region_6.7_spmd.clone, body=%wide.region_5.6_spmd.clone.sunk | while | flops 682438656 | bytes 3526869 | solution.py:104
  118.6 10.4 %fusion.96 = f32[3,16,128]{1,0,2:T(4,128)S(1)} fusion(f32[3,16,8,128]{1,2,0,3:T(8,128)S(1)} %copy.97, f32[3,3,64,128]{2,0,1,3:T(4,128)S(1)} %get-tuple-element.515, s32[]{:T(128)S(6)} %select_n.201, f32[3,16,128]{1,0,2:T(4,128)S(1)} %get-tuple-element.503, pred[]{:T(512)S(6)} %compare.21), kind=kOutput, calls=%fused_computation.15.clone.1 | convolution fusion | flops 1781760 | bytes 540677 | tf_op jit(solution)/shard_map/while/body/eval_jaxpr/abkn,brkn->arn/dot_general | solution.py:100
  132.0 10.4 %fusion.96 = f32[3,16,128]{1,0,2:T(4,128)S(1)} fusion(f32[3,16,8,128]{1,2,0,3:T(8,128)S(1)} %copy.97, f32[3,3,64,128]{2,0,1,3:T(4,128)S(1)} %get-tuple-element.515, s32[]{:T(128)S(6)} %select_n.201, f32[3,16,128]{1,0,2:T(4,128)S(1)} %get-tuple-element.503, pred[]{:T(512)S(6)} %compare.21), kind=kOutput, calls=%fused_computation.15.clone.1 | convolution fusion | flops 1781760 | bytes 540677 | tf_op jit(solution)/shard_map/while/body/eval_jaxpr/abkn,brkn->arn/dot_general | solution.py:100
  145.5 10.4 %fusion.96 = f32[3,16,128]{1,0,2:T(4,128)S(1)} fusion(f32[3,16,8,128]{1,2,0,3:T(8,128)S(1)} %copy.97, f32[3,3,64,128]{2,0,1,3:T(4,128)S(1)} %get-tuple-element.515, s32[]{:T(128)S(6)} %select_n.201, f32[3,16,128]{1,0,2:T(4,128)S(1)} %get-tuple-element.503, pred[]{:T(512)S(6)} %compare.21), kind=kOutput, calls=%fused_computation.15.clone.1 | convolution fusion | flops 1781760 | bytes 540677 | tf_op jit(solution)/shard_map/while/body/eval_jaxpr/abkn,brkn->arn/dot_general | solution.py:100
  158.9 10.4 %fusion.96 = f32[3,16,128]{1,0,2:T(4,128)S(1)} fusion(f32[3,16,8,128]{1,2,0,3:T(8,128)S(1)} %copy.97, f32[3,3,64,128]{2,0,1,3:T(4,128)S(1)} %get-tuple-element.515, s32[]{:T(128)S(6)} %select_n.201, f32[3,16,128]{1,0,2:T(4,128)S(1)} %get-tuple-element.503, pred[]{:T(512)S(6)} %compare.21), kind=kOutput, calls=%fused_computation.15.clone.1 | convolution fusion | flops 1781760 | bytes 540677 | tf_op jit(solution)/shard_map/while/body/eval_jaxpr/abkn,brkn->arn/dot_general | solution.py:100
  172.4 10.4 %fusion.96 = f32[3,16,128]{1,0,2:T(4,128)S(1)} fusion(f32[3,16,8,128]{1,2,0,3:T(8,128)S(1)} %copy.97, f32[3,3,64,128]{2,0,1,3:T(4,128)S(1)} %get-tuple-element.515, s32[]{:T(128)S(6)} %select_n.201, f32[3,16,128]{1,0,2:T(4,128)S(1)} %get-tuple-element.503, pred[]{:T(512)S(6)} %compare.21), kind=kOutput, calls=%fused_computation.15.clone.1 | convolution fusion | flops 1781760 | bytes 540677 | tf_op jit(solution)/shard_map/while/body/eval_jaxpr/abkn,brkn->arn/dot_general | solution.py:100
  185.8 10.4 %fusion.96 = f32[3,16,128]{1,0,2:T(4,128)S(1)} fusion(f32[3,16,8,128]{1,2,0,3:T(8,128)S(1)} %copy.97, f32[3,3,64,128]{2,0,1,3:T(4,128)S(1)} %get-tuple-element.515, s32[]{:T(128)S(6)} %select_n.201, f32[3,16,128]{1,0,2:T(4,128)S(1)} %get-tuple-element.503, pred[]{:T(512)S(6)} %compare.21), kind=kOutput, calls=%fused_computation.15.clone.1 | convolution fusion | flops 1781760 | bytes 540677 | tf_op jit(solution)/shard_map/while/body/eval_jaxpr/abkn,brkn->arn/dot_general | solution.py:100
  199.3 10.4 %fusion.96 = f32[3,16,128]{1,0,2:T(4,128)S(1)} fusion(f32[3,16,8,128]{1,2,0,3:T(8,128)S(1)} %copy.97, f32[3,3,64,128]{2,0,1,3:T(4,128)S(1)} %get-tuple-element.515, s32[]{:T(128)S(6)} %select_n.201, f32[3,16,128]{1,0,2:T(4,128)S(1)} %get-tuple-element.503, pred[]{:T(512)S(6)} %compare.21), kind=kOutput, calls=%fused_computation.15.clone.1 | convolution fusion | flops 1781760 | bytes 540677 | tf_op jit(solution)/shard_map/while/body/eval_jaxpr/abkn,brkn->arn/dot_general | solution.py:100
  212.7 10.4 %fusion.96 = f32[3,16,128]{1,0,2:T(4,128)S(1)} fusion(f32[3,16,8,128]{1,2,0,3:T(8,128)S(1)} %copy.97, f32[3,3,64,128]{2,0,1,3:T(4,128)S(1)} %get-tuple-element.515, s32[]{:T(128)S(6)} %select_n.201, f32[3,16,128]{1,0,2:T(4,128)S(1)} %get-tuple-element.503, pred[]{:T(512)S(6)} %compare.21), kind=kOutput, calls=%fused_computation.15.clone.1 | convolution fusion | flops 1781760 | bytes 540677 | tf_op jit(solution)/shard_map/while/body/eval_jaxpr/abkn,brkn->arn/dot_general | solution.py:100
  225.4 12.8 %collective-permute-start.12 = (f32[48,1,1,128]{3,0,2,1:T(8,128)S(1)}, f32[48,1,1,128]{3,0,2,1:T(8,128)S(1)}, u32[]{:S(2)}, u32[]{:S(2)}) collective-permute-start(f32[48,1,1,128]{3,0,2,1:T(8,128)S(1)} %bitcast.197), channel_id=1, source_target_pairs={{0,32},{32,64},{64,96},{96,128},{128,160},{160,192},{192,224},{224... | collective-permute-start | bytes 73736 | tf_op jit(solution)/shard_map/ppermute | solution.py:18
  257.1 12.9 %collective-permute-done.15 = f32[48,3,1,128]{3,0,2,1:T(8,128)S(1)} collective-permute-done((f32[48,3,1,128]{3,0,2,1:T(8,128)S(1)}, f32[48,3,1,128]{3,0,2,1:T(8,128)S(1)}, u32[]{:S(2)}, u32[]{:S(2)}) %collective-permute-start.15) | collective-permute-done | bytes 73760 | tf_op jit(solution)/shard_map/ppermute | solution.py:20
  270.2 107.6 %while.51 = (s32[]{:T(128)}, f32[3,16,128]{1,0,2:T(4,128)S(1)}, s32[8,1024]{1,0:T(8,128)S(1)}, f32[48,1152]{1,0:T(8,128)S(1)}, f32[3,3,64,128]{2,0,1,3:T(4,128)S...) while((s32[]{:T(128)}, f32[3,16,128]{1,0,2:T(4,128)S(1)}, s32[8,1024]{1,0:T(8,128)S(1)}, ...), condition=%wide.region_8.9_spmd.clone, body=%wide.region_7.8_spmd.clone.sunk | while | flops 682438656 | bytes 3526869 | solution.py:104
  273.3 10.4 %fusion.101 = f32[3,16,128]{1,0,2:T(4,128)S(1)} fusion(f32[3,16,8,128]{1,2,0,3:T(8,128)S(1)} %copy.99, f32[3,3,64,128]{2,0,1,3:T(4,128)S(1)} %get-tuple-element.542, s32[]{:T(128)S(6)} %select_n.202, f32[3,16,128]{1,0,2:T(4,128)S(1)} %get-tuple-element.530, pred[]{:T(512)S(6)} %compare.22), kind=kOutput, calls=%fused_computation.24.clone.1 | convolution fusion | flops 1781760 | bytes 540677 | tf_op jit(solution)/shard_map/while/body/eval_jaxpr/abkn,brkn->arn/dot_general | solution.py:100
  286.7 10.4 %fusion.101 = f32[3,16,128]{1,0,2:T(4,128)S(1)} fusion(f32[3,16,8,128]{1,2,0,3:T(8,128)S(1)} %copy.99, f32[3,3,64,128]{2,0,1,3:T(4,128)S(1)} %get-tuple-element.542, s32[]{:T(128)S(6)} %select_n.202, f32[3,16,128]{1,0,2:T(4,128)S(1)} %get-tuple-element.530, pred[]{:T(512)S(6)} %compare.22), kind=kOutput, calls=%fused_computation.24.clone.1 | convolution fusion | flops 1781760 | bytes 540677 | tf_op jit(solution)/shard_map/while/body/eval_jaxpr/abkn,brkn->arn/dot_general | solution.py:100
  300.2 10.4 %fusion.101 = f32[3,16,128]{1,0,2:T(4,128)S(1)} fusion(f32[3,16,8,128]{1,2,0,3:T(8,128)S(1)} %copy.99, f32[3,3,64,128]{2,0,1,3:T(4,128)S(1)} %get-tuple-element.542, s32[]{:T(128)S(6)} %select_n.202, f32[3,16,128]{1,0,2:T(4,128)S(1)} %get-tuple-element.530, pred[]{:T(512)S(6)} %compare.22), kind=kOutput, calls=%fused_computation.24.clone.1 | convolution fusion | flops 1781760 | bytes 540677 | tf_op jit(solution)/shard_map/while/body/eval_jaxpr/abkn,brkn->arn/dot_general | solution.py:100
  313.7 10.4 %fusion.101 = f32[3,16,128]{1,0,2:T(4,128)S(1)} fusion(f32[3,16,8,128]{1,2,0,3:T(8,128)S(1)} %copy.99, f32[3,3,64,128]{2,0,1,3:T(4,128)S(1)} %get-tuple-element.542, s32[]{:T(128)S(6)} %select_n.202, f32[3,16,128]{1,0,2:T(4,128)S(1)} %get-tuple-element.530, pred[]{:T(512)S(6)} %compare.22), kind=kOutput, calls=%fused_computation.24.clone.1 | convolution fusion | flops 1781760 | bytes 540677 | tf_op jit(solution)/shard_map/while/body/eval_jaxpr/abkn,brkn->arn/dot_general | solution.py:100
  327.1 10.4 %fusion.101 = f32[3,16,128]{1,0,2:T(4,128)S(1)} fusion(f32[3,16,8,128]{1,2,0,3:T(8,128)S(1)} %copy.99, f32[3,3,64,128]{2,0,1,3:T(4,128)S(1)} %get-tuple-element.542, s32[]{:T(128)S(6)} %select_n.202, f32[3,16,128]{1,0,2:T(4,128)S(1)} %get-tuple-element.530, pred[]{:T(512)S(6)} %compare.22), kind=kOutput, calls=%fused_computation.24.clone.1 | convolution fusion | flops 1781760 | bytes 540677 | tf_op jit(solution)/shard_map/while/body/eval_jaxpr/abkn,brkn->arn/dot_general | solution.py:100
  340.6 10.4 %fusion.101 = f32[3,16,128]{1,0,2:T(4,128)S(1)} fusion(f32[3,16,8,128]{1,2,0,3:T(8,128)S(1)} %copy.99, f32[3,3,64,128]{2,0,1,3:T(4,128)S(1)} %get-tuple-element.542, s32[]{:T(128)S(6)} %select_n.202, f32[3,16,128]{1,0,2:T(4,128)S(1)} %get-tuple-element.530, pred[]{:T(512)S(6)} %compare.22), kind=kOutput, calls=%fused_computation.24.clone.1 | convolution fusion | flops 1781760 | bytes 540677 | tf_op jit(solution)/shard_map/while/body/eval_jaxpr/abkn,brkn->arn/dot_general | solution.py:100
  354.0 10.4 %fusion.101 = f32[3,16,128]{1,0,2:T(4,128)S(1)} fusion(f32[3,16,8,128]{1,2,0,3:T(8,128)S(1)} %copy.99, f32[3,3,64,128]{2,0,1,3:T(4,128)S(1)} %get-tuple-element.542, s32[]{:T(128)S(6)} %select_n.202, f32[3,16,128]{1,0,2:T(4,128)S(1)} %get-tuple-element.530, pred[]{:T(512)S(6)} %compare.22), kind=kOutput, calls=%fused_computation.24.clone.1 | convolution fusion | flops 1781760 | bytes 540677 | tf_op jit(solution)/shard_map/while/body/eval_jaxpr/abkn,brkn->arn/dot_general | solution.py:100
  367.5 10.4 %fusion.101 = f32[3,16,128]{1,0,2:T(4,128)S(1)} fusion(f32[3,16,8,128]{1,2,0,3:T(8,128)S(1)} %copy.99, f32[3,3,64,128]{2,0,1,3:T(4,128)S(1)} %get-tuple-element.542, s32[]{:T(128)S(6)} %select_n.202, f32[3,16,128]{1,0,2:T(4,128)S(1)} %get-tuple-element.530, pred[]{:T(512)S(6)} %compare.22), kind=kOutput, calls=%fused_computation.24.clone.1 | convolution fusion | flops 1781760 | bytes 540677 | tf_op jit(solution)/shard_map/while/body/eval_jaxpr/abkn,brkn->arn/dot_general | solution.py:100
  (268 shorter events, 150.5 us)
Async XLA Ops:
  0.6 34.3 %copy-start.7 = (f32[3,1,1,128]{3,2,1,0:T(1,128)S(1)}, f32[3,1,1,128]{3,2,1,0:T(1,128)}, u32[]{:S(2)}) copy-start(f32[3,1,1,128]{3,2,1,0:T(1,128)} %param.16) | copy-start | bytes 4612
  0.6 34.5 %copy-start.11 = (s32[1,1,32]{2,1,0:T(1,128)S(1)}, s32[1,1,32]{2,1,0:T(1,128)}, u32[]{:S(2)}) copy-start(s32[1,1,32]{2,1,0:T(1,128)} %param.18) | copy-start | bytes 388
  0.7 34.2 %copy-start = (s32[1,1,64,128]{3,2,1,0:T(8,128)S(1)}, s32[1,1,64,128]{3,2,1,0:T(8,128)}, u32[]{:S(2)}) copy-start(s32[1,1,64,128]{3,2,1,0:T(8,128)} %param.19) | copy-start | bytes 98308
  0.7 34.4 %copy-start.9 = (f32[3,8,1,1,128]{4,3,2,1,0:T(1,128)S(1)}, f32[3,8,1,1,128]{4,3,2,1,0:T(1,128)}, u32[]{:S(2)}) copy-start(f32[3,8,1,1,128]{4,3,2,1,0:T(1,128)} %param.20) | copy-start | bytes 36868
  0.7 34.4 %copy-start.8 = (f32[3,8,1,1,128]{4,3,2,1,0:T(1,128)S(1)}, f32[3,8,1,1,128]{4,3,2,1,0:T(1,128)}, u32[]{:S(2)}) copy-start(f32[3,8,1,1,128]{4,3,2,1,0:T(1,128)} %param.22) | copy-start | bytes 36868
  1.4 59.4 %collective-permute-start.4 = (f32[4,1,1,128]{3,2,1,0:T(1,128)S(1)}, f32[4,1,1,128]{3,2,1,0:T(1,128)S(1)}, u32[]{:S(2)}, u32[]{:S(2)}) collective-permute-start(f32[4,1,1,128]{3,2,1,0:T(1,128)S(1)} %pad_maximum_fusion.11), channel_id=1, source_target_pairs={{0,32},{32,64},{64,96},{96,128},{128,160},{160,192},{192,224},{224... | collective-permute-start | bytes 6152 | tf_op jit(solution)/shard_map/ppermute | solution.py:18
  8.5 52.4 %collective-permute-start.5 = (f32[4,1,1,128]{3,2,1,0:T(1,128)S(1)}, f32[4,1,1,128]{3,2,1,0:T(1,128)S(1)}, u32[]{:S(2)}, u32[]{:S(2)}) collective-permute-start(f32[4,1,1,128]{3,2,1,0:T(1,128)S(1)} %pad_maximum_fusion.11), channel_id=1, source_target_pairs={{32,0},{64,32},{96,64},{128,96},{160,128},{192,160},{224,192},{256... | collective-permute-start | bytes 6152 | tf_op jit(solution)/shard_map/ppermute | solution.py:20
  10.4 24.7 %collective-permute-start = (s32[1,1,32]{2,1,0:T(1,128)}, s32[1,1,32]{2,1,0:T(1,128)S(1)}, u32[]{:S(2)}, u32[]{:S(2)}) collective-permute-start(s32[1,1,32]{2,1,0:T(1,128)} %param.18), channel_id=1, source_target_pairs={{0,32},{32,64},{64,96},{96,128},{128,160},{160,192},{192,224},{224... | collective-permute-start | bytes 392 | tf_op jit(solution)/shard_map/ppermute | solution.py:18
  20.7 14.5 %collective-permute-start.1 = (s32[1,1,32]{2,1,0:T(1,128)}, s32[1,1,32]{2,1,0:T(1,128)S(1)}, u32[]{:S(2)}, u32[]{:S(2)}) collective-permute-start(s32[1,1,32]{2,1,0:T(1,128)} %param.18), channel_id=1, source_target_pairs={{32,0},{64,32},{96,64},{128,96},{160,128},{192,160},{224,192},{256... | collective-permute-start | bytes 392 | tf_op jit(solution)/shard_map/ppermute | solution.py:20
  24.5 36.3 %copy-start.10 = (f32[1,1,128]{2,1,0:T(1,128)S(1)}, f32[1,1,128]{2,1,0:T(1,128)}, u32[]{:S(2)}) copy-start(f32[1,1,128]{2,1,0:T(1,128)} %param.17) | copy-start | bytes 1540
  24.6 70.6 %collective-permute-start.8 = (f32[48,1,1,128]{3,0,2,1:T(8,128)S(1)}, f32[48,1,1,128]{3,0,2,1:T(8,128)S(1)}, u32[]{:S(2)}, u32[]{:S(2)}) collective-permute-start(f32[48,1,1,128]{3,0,2,1:T(8,128)S(1)} %bitcast.193), channel_id=1, source_target_pairs={{0,32},{32,64},{64,96},{96,128},{128,160},{160,192},{192,224},{224... | collective-permute-start | bytes 73736 | tf_op jit(solution)/shard_map/ppermute | solution.py:18
  35.2 6.2 %collective-permute-start.2 = (s32[3,1,32]{2,1,0:T(1,128)S(1)}, s32[3,1,32]{2,1,0:T(1,128)S(1)}, u32[]{:S(2)}, u32[]{:S(2)}) collective-permute-start(s32[3,1,32]{2,1,0:T(1,128)S(1)} %constant_dynamic-update-slice_fusion), channel_id=1, source_target_pairs={{0,1},{1,2},{2,3},{3,4},{4,5},{5,6},{6,7},{7,8},{8,9},{9,10},{10,1... | collective-permute-start | bytes 1160 | tf_op jit(solution)/shard_map/ppermute | solution.py:18
  38.7 17.3 %collective-permute-start.3 = (s32[3,1,32]{2,1,0:T(1,128)S(1)}, s32[3,1,32]{2,1,0:T(1,128)S(1)}, u32[]{:S(2)}, u32[]{:S(2)}) collective-permute-start(s32[3,1,32]{2,1,0:T(1,128)S(1)} %constant_dynamic-update-slice_fusion), channel_id=1, source_target_pairs={{1,0},{2,1},{3,2},{4,3},{5,4},{6,5},{7,6},{8,7},{9,8},{10,9},{11,1... | collective-permute-start | bytes 1160 | tf_op jit(solution)/shard_map/ppermute | solution.py:20
  41.4 53.8 %collective-permute-start.9 = (f32[48,1,1,128]{3,0,2,1:T(8,128)S(1)}, f32[48,1,1,128]{3,0,2,1:T(8,128)S(1)}, u32[]{:S(2)}, u32[]{:S(2)}) collective-permute-start(f32[48,1,1,128]{3,0,2,1:T(8,128)S(1)} %bitcast.194), channel_id=1, source_target_pairs={{32,0},{64,32},{96,64},{128,96},{160,128},{192,160},{224,192},{256... | collective-permute-start | bytes 73736 | tf_op jit(solution)/shard_map/ppermute | solution.py:20
  60.9 5.7 %collective-permute-start.6 = (f32[4,3,1,128]{3,2,1,0:T(1,128)S(1)}, f32[4,3,1,128]{3,2,1,0:T(1,128)S(1)}, u32[]{:S(2)}, u32[]{:S(2)}) collective-permute-start(f32[4,3,1,128]{3,2,1,0:T(1,128)S(1)} %pad_maximum_fusion.10), channel_id=1, source_target_pairs={{0,1},{1,2},{2,3},{3,4},{4,5},{5,6},{6,7},{7,8},{8,9},{9,10},{10,1... | collective-permute-start | bytes 18440 | tf_op jit(solution)/shard_map/ppermute | solution.py:18
  64.6 17.3 %collective-permute-start.7 = (f32[4,3,1,128]{3,2,1,0:T(1,128)S(1)}, f32[4,3,1,128]{3,2,1,0:T(1,128)S(1)}, u32[]{:S(2)}, u32[]{:S(2)}) collective-permute-start(f32[4,3,1,128]{3,2,1,0:T(1,128)S(1)} %pad_maximum_fusion.10), channel_id=1, source_target_pairs={{1,0},{2,1},{3,2},{4,3},{5,4},{6,5},{7,6},{8,7},{9,8},{10,9},{11,1... | collective-permute-start | bytes 18440 | tf_op jit(solution)/shard_map/ppermute | solution.py:20
  95.2 6.0 %collective-permute-start.10 = (f32[48,3,1,128]{3,0,2,1:T(8,128)S(1)}, f32[48,3,1,128]{3,0,2,1:T(8,128)S(1)}, u32[]{:S(2)}, u32[]{:S(2)}) collective-permute-start(f32[48,3,1,128]{3,0,2,1:T(8,128)S(1)} %pad_maximum_fusion.5), channel_id=1, source_target_pairs={{0,1},{1,2},{2,3},{3,4},{4,5},{5,6},{6,7},{7,8},{8,9},{9,10},{10,1... | collective-permute-start | bytes 221192 | tf_op jit(solution)/shard_map/ppermute | solution.py:18
  97.2 18.0 %collective-permute-start.11 = (f32[48,3,1,128]{3,0,2,1:T(8,128)S(1)}, f32[48,3,1,128]{3,0,2,1:T(8,128)S(1)}, u32[]{:S(2)}, u32[]{:S(2)}) collective-permute-start(f32[48,3,1,128]{3,0,2,1:T(8,128)S(1)} %pad_maximum_fusion.5), channel_id=1, source_target_pairs={{1,0},{2,1},{3,2},{4,3},{5,4},{6,5},{7,6},{8,7},{9,8},{10,9},{11,1... | collective-permute-start | bytes 221192 | tf_op jit(solution)/shard_map/ppermute | solution.py:20
  223.1 17.0 %copy-start.5 = (f32[3,8,1,1,128]{4,3,2,1,0:T(1,128)S(1)}, f32[3,8,1,1,128]{4,3,2,1,0:T(1,128)}, u32[]{:S(2)}) copy-start(f32[3,8,1,1,128]{4,3,2,1,0:T(1,128)} %param.23) | copy-start | bytes 36868
  223.1 17.0 %copy-start.6 = (f32[3,8,1,1,128]{4,3,2,1,0:T(1,128)S(1)}, f32[3,8,1,1,128]{4,3,2,1,0:T(1,128)}, u32[]{:S(2)}) copy-start(f32[3,8,1,1,128]{4,3,2,1,0:T(1,128)} %param.21) | copy-start | bytes 36868
  225.4 15.6 %collective-permute-start.12 = (f32[48,1,1,128]{3,0,2,1:T(8,128)S(1)}, f32[48,1,1,128]{3,0,2,1:T(8,128)S(1)}, u32[]{:S(2)}, u32[]{:S(2)}) collective-permute-start(f32[48,1,1,128]{3,0,2,1:T(8,128)S(1)} %bitcast.197), channel_id=1, source_target_pairs={{0,32},{32,64},{64,96},{96,128},{128,160},{160,192},{192,224},{224... | collective-permute-start | bytes 73736 | tf_op jit(solution)/shard_map/ppermute | solution.py:18
  238.2 11.8 %collective-permute-start.13 = (f32[48,1,1,128]{3,0,2,1:T(8,128)S(1)}, f32[48,1,1,128]{3,0,2,1:T(8,128)S(1)}, u32[]{:S(2)}, u32[]{:S(2)}) collective-permute-start(f32[48,1,1,128]{3,0,2,1:T(8,128)S(1)} %bitcast.198), channel_id=1, source_target_pairs={{32,0},{64,32},{96,64},{128,96},{160,128},{192,160},{224,192},{256... | collective-permute-start | bytes 73736 | tf_op jit(solution)/shard_map/ppermute | solution.py:20
  250.0 7.1 %collective-permute-start.14 = (f32[48,3,1,128]{3,0,2,1:T(8,128)S(1)}, f32[48,3,1,128]{3,0,2,1:T(8,128)S(1)}, u32[]{:S(2)}, u32[]{:S(2)}) collective-permute-start(f32[48,3,1,128]{3,0,2,1:T(8,128)S(1)} %pad_maximum_fusion.6), channel_id=1, source_target_pairs={{0,1},{1,2},{2,3},{3,4},{4,5},{5,6},{6,7},{7,8},{8,9},{9,10},{10,1... | collective-permute-start | bytes 221192 | tf_op jit(solution)/shard_map/ppermute | solution.py:18
  251.9 18.0 %collective-permute-start.15 = (f32[48,3,1,128]{3,0,2,1:T(8,128)S(1)}, f32[48,3,1,128]{3,0,2,1:T(8,128)S(1)}, u32[]{:S(2)}, u32[]{:S(2)}) collective-permute-start(f32[48,3,1,128]{3,0,2,1:T(8,128)S(1)} %pad_maximum_fusion.6), channel_id=1, source_target_pairs={{1,0},{2,1},{3,2},{4,3},{5,4},{6,5},{7,6},{8,7},{9,8},{10,9},{11,1... | collective-permute-start | bytes 221192 | tf_op jit(solution)/shard_map/ppermute | solution.py:20
  (32 other events, 176.9 us)
where the time goes:
time: 382 us
  matrix products  214 us (56%)
  starting transfers between devices  69.9 us (18%)
  waiting for transfers between devices  63.7 us (17%)
  local copies, waits for them, and re-layouts  29 us (8%)
    dot_general x16, matrix products, add_block(): jnp.einsum('abkn,brkn->arn', part_blocks, far_rows, precision=lax.Precisi...  166 us
    ppermute x8, waiting for transfers between devices, padded(): lax.ppermute(head, axis, [((i + 1) % count, i) for i in range(count)])  63.7 us
    ppermute x8, starting transfers between devices, padded(): lax.ppermute(tail, axis, [(i, (i + 1) % count) for i in range(count)])  51.5 us
    dot_general x32, matrix products, select_columns(): return jnp.dot(source, one_hot, precision=lax.Precision.HIGHEST)  44.5 us
    ppermute x8, starting transfers between devices, padded(): lax.ppermute(head, axis, [((i + 1) % count, i) for i in range(count)])  18.4 us
    while x80, local copies, waits for them, and re-layouts  11.1 us
    reshape x16, local copies, waits for them, and re-layouts, add_block(): select_columns(source, slot_index).reshape(3, n_rows, block_slots, n_atoms)  8.93 us
  transfers between devices with their start and end apart: 16, of which 5 were waited for; matrix products, arithmetic and copies ran while one was open for 6% of the time, Pallas kernels for 0%

commit v1 on v0

v1 whole, which is shorter than its diff:
```python
import jax
import jax.numpy as jnp
from jax import lax
from jax.experimental import pallas as pl
from jax.experimental.pallas import tpu as pltpu
from jax.sharding import PartitionSpec as P

column_edge = 20.0
reach_sq = 64.0
A = 128
G = 32
NB = 64
F = 16
OWN = 3 * A
FAR = 8 * A
F32 = jnp.float32
BF16 = jnp.bfloat16
KEYS = ((0, 0), (0, 1), (0, 2), (1, 1), (1, 2), (2, 2))


def steps_of_slots():
    e = 1 - 2 * lax.rem(lax.axis_index("gy"), 2)
    f = 1 - 2 * lax.rem(lax.axis_index("gx"), 2)
    return [(0, e), (0, -e)] + [(s, t) for s in (f, -f) for t in (e, 0, -e)]


def gather_slots(near, row_one, row_two):
    return [near[0][...], near[1][...]] + [r[j] for r in (row_one, row_two) for j in range(3)]


def split(x):
    high = x.astype(BF16)
    return high, (x - high.astype(F32)).astype(BF16)


def border_lanes(border, values):
    index = jnp.concatenate([border[...]] * (A // G), axis=1)
    return jnp.take_along_axis(values, jnp.broadcast_to(index, values.shape), axis=1)


def pack_fields(border, parts, last):
    group = lax.broadcasted_iota(jnp.int32, (F, A), 1) // G
    out = last
    for b in range(3):
        out = jnp.where(group == b, border_lanes(border, parts[b]), out)
    return out


def stacked(vec, heat):
    return [jnp.concatenate([vec[b], heat[b]], axis=0) for b in range(3)]


def pack_kernel(pos, spring, border, vec, heat, out):
    geometry = jnp.concatenate(
        [pos[0], pos[1], pos[2], spring[...], jnp.zeros((F - 4, A), F32)], axis=0
    )
    out[...] = pack_fields(border, stacked(vec, heat), border_lanes(border, geometry))


def count_slots(entries, groups):
    sub = lax.broadcasted_iota(jnp.int32, (8, A), 0)
    counters = [jnp.zeros((8, A), jnp.int32) for _ in groups]
    for n in range(NB):
        e = jnp.broadcast_to(entries[n : n + 1, :], (8, A))
        mark = jnp.where(sub == (e & 7), jnp.left_shift(jnp.int32(1), e & 24), 0)
        which = lax.shift_right_arithmetic(e, 5)
        for i, g in enumerate(groups):
            counters[i] += jnp.where(which == g, mark, 0)
    return counters


def pair_terms(counter, source, home, root_home):
    tiles = [lax.shift_right_logical(counter, 8 * q) & 255 for q in range(4)]
    count = jnp.concatenate(tiles, axis=0).astype(F32)
    d = [source[a] - home[a] for a in range(3)]
    r2 = d[0] * d[0] + d[1] * d[1] + d[2] * d[2]
    near = r2 + 1.0
    inverse = (count * (root_home * source[3])) / ((reach_sq + r2) * near)
    c = inverse * near * (reach_sq / NB)
    bend = inverse * (2.0 * reach_sq / NB)
    g = [bend * d[a] for a in range(3)]
    return {(a, b): (g[a] * d[b] + c if a == b else g[a] * d[b]) for a, b in KEYS}


def put_terms(w_high, w_low, sums, rows, terms):
    for (a, b), value in terms.items():
        part = value[0:8] + value[8:16] + value[16:24] + value[24:32]
        sums[(a, b)] = sums[(a, b)] + part if (a, b) in sums else part
        high, low = split(value)
        for p, q in sorted({(a, b), (b, a)}):
            w_high[rows[q] : rows[q] + G, p * A : (p + 1) * A] = high
            w_low[rows[q] : rows[q] + G, p * A : (p + 1) * A] = low


def apply_weights(w_high, w_low, lhs):
    high, low = split(lhs)
    both = jnp.concatenate([high, low], axis=0)
    main = jnp.dot(both, w_high[...], preferred_element_type=F32)
    rest = jnp.dot(high, w_low[...], preferred_element_type=F32)
    return main[:F] + main[F:] + rest


def home_of(pos, root):
    home = [jnp.broadcast_to(pos[a], (G, A)) for a in range(3)]
    return home, jnp.broadcast_to(root, (G, A))


def own_kernel(pos, spring, entries, vec, heat, w_high, w_low, far, counts, sums_out):
    groups = [4 * (3 * (sx + 1) + sy + 1) for sx, sy in steps_of_slots()]
    counters = count_slots(entries[...], groups + [16, 17, 18, 19])
    for i in range(8):
        counts[i] = counters[i]
    root = jnp.sqrt(spring[...])
    home, root_home = home_of(pos, root)
    geo = jnp.concatenate([pos[0], pos[1], pos[2], root, jnp.zeros((4, A), F32)], axis=0).T
    sums = {}
    for t in range(4):
        source = [
            jnp.broadcast_to(geo[t * G : (t + 1) * G, c : c + 1], (G, A)) for c in range(4)
        ]
        terms = pair_terms(counters[8 + t], source, home, root_home)
        put_terms(w_high, w_low, sums, [b * A + t * G for b in range(3)], terms)
    for i, key in enumerate(KEYS):
        sums_out[i] = sums[key]
    far[...] = apply_weights(w_high, w_low, jnp.concatenate(stacked(vec, heat), axis=1))


def local_term(far, self_terms, current, previous, a):
    total = -far[:, a * A : (a + 1) * A] - current[a]
    for b in range(3):
        total += self_terms[(min(a, b), max(a, b))] * current[b]
    return 2.0 * total - previous[a]


def first_kernel(pos, spring, border, vec, heat, vec0, heat0, far_in, counts, sums_in,
                 near_one, near_two, row_one, row_two,
                 next_v, next_h, payload, w_high, w_low, self_out):
    slots = gather_slots((near_one, near_two), row_one, row_two)
    root = jnp.sqrt(spring[...])
    home, root_home = home_of(pos, root)
    geo = jnp.concatenate([s[0:4] for s in slots], axis=0).T
    sums = {key: sums_in[i] for i, key in enumerate(KEYS)}
    for j, (sx, sy) in enumerate(steps_of_slots()):
        cols = [geo[3 * G :, 4 * j + c : 4 * j + c + 1] for c in range(4)]
        source = [
            jnp.broadcast_to(cols[0] + column_edge * jnp.asarray(sx, F32), (G, A)),
            jnp.broadcast_to(cols[1] + column_edge * jnp.asarray(sy, F32), (G, A)),
            jnp.broadcast_to(cols[2], (G, A)),
            jnp.broadcast_to(jnp.sqrt(cols[3]), (G, A)),
        ]
        terms = pair_terms(counts[j], source, home, root_home)
        put_terms(w_high, w_low, sums, [j * A + b * G for b in range(3)], terms)
        w_high[j * A + 3 * G : (j + 1) * A, :] = jnp.zeros((G, OWN), BF16)
        w_low[j * A + 3 * G : (j + 1) * A, :] = jnp.zeros((G, OWN), BF16)
    self_terms = {}
    for i, key in enumerate(KEYS):
        self_terms[key] = jnp.sum(sums[key], axis=0, keepdims=True)
        self_out[i : i + 1, :] = self_terms[key]
    far = far_in[...] + apply_weights(w_high, w_low, jnp.concatenate(slots, axis=1))
    current, previous = stacked(vec, heat), stacked(vec0, heat0)
    result = [local_term(far, self_terms, current, previous, a) for a in range(3)]
    payload[...] = pack_fields(border, result, jnp.zeros((F, A), F32))
    for a in range(3):
        next_v[a] = result[a][:8]
        next_h[a] = result[a][8:]


def again_kernel(w_high, w_low, self_in, vec, heat, vec1, heat1, out):
    self_terms = {key: self_in[i : i + 1, :] for i, key in enumerate(KEYS)}
    current, previous = stacked(vec, heat), stacked(vec1, heat1)
    far = apply_weights(w_high, w_low, jnp.concatenate(current, axis=1))
    for a in range(3):
        out[a] = local_term(far, self_terms, current, previous, a)


def last_kernel(w_high, w_low, partial, near_one, near_two, row_one, row_two, out_v, out_h):
    slots = gather_slots((near_one, near_two), row_one, row_two)
    far = apply_weights(w_high, w_low, jnp.concatenate(slots, axis=1))
    for a in range(3):
        result = partial[a] - 2.0 * far[:, a * A : (a + 1) * A]
        out_v[a] = result[:8]
        out_h[a] = result[8:]


def pairs(count, first):
    out = []
    for i in range(first, count + first, 2):
        a, b = i % count, (i + 1) % count
        out += [(a, b), (b, a)]
    return out


def swaps(values, axis):
    count = lax.axis_size(axis)
    return [lax.ppermute(values, axis, pairs(count, first)) for first in (0, 1)]


def surround(payload):
    near_one, near_two = swaps(payload, "gy")
    row_one, row_two = swaps(jnp.stack([near_one, payload, near_two]), "gx")
    return near_one, near_two, row_one, row_two


def call(kernel, out_shape, *args):
    size = sum(x.size * x.dtype.itemsize for x in (*args, *out_shape))
    return pl.pallas_call(
        kernel,
        out_shape=out_shape,
        name=kernel.__name__,
        cost_estimate=pl.CostEstimate(flops=2**20, bytes_accessed=size, transcendentals=0),
        compiler_params=pltpu.CompilerParams(vmem_limit_bytes=16 * 2**20),
    )(*args)


def shards(positions, spring, border, neighbours, vec_prev, vec_now, heat_prev, heat_now):
    def fields(x):
        return x.reshape(3, 8, A)

    shape = jax.ShapeDtypeStruct
    vector = shape((3, 8, A), F32)
    pos = positions.reshape(3, 1, A)
    stiff = spring.reshape(1, A)
    index = border.reshape(1, G)
    entries = neighbours.reshape(NB, A)
    v0, v1, h0, h1 = map(fields, (vec_prev, vec_now, heat_prev, heat_now))
    (payload,) = call(pack_kernel, (shape((F, A), F32),), pos, stiff, index, v1, h1)
    received = surround(payload)
    own_high, own_low, far, counts, sums = call(
        own_kernel,
        (
            shape((OWN, OWN), BF16),
            shape((OWN, OWN), BF16),
            shape((F, OWN), F32),
            shape((8, 8, A), jnp.int32),
            shape((6, 8, A), F32),
        ),
        pos, stiff, entries, v1, h1,
    )
    v2, h2, payload, far_high, far_low, self_terms = call(
        first_kernel,
        (
            vector,
            vector,
            shape((F, A), F32),
            shape((FAR, OWN), BF16),
            shape((FAR, OWN), BF16),
            shape((6, A), F32),
        ),
        pos, stiff, index, v1, h1, v0, h0, far, counts, sums, *received,
    )
    received = surround(payload)
    (partial,) = call(
        again_kernel, (shape((3, F, A), F32),), own_high, own_low, self_terms, v2, h2, v1, h1
    )
    v3, h3 = call(last_kernel, (vector, vector), far_high, far_low, partial, *received)
    whole = vec_prev.shape
    return v2.reshape(whole), v3.reshape(whole), h2.reshape(whole), h3.reshape(whole)


def solution(mesh):
    wide = P(None, None, "gx", "gy", None)
    return jax.shard_map(
        shards,
        mesh=mesh,
        in_specs=(
            P(None, "gx", "gy", None),
            P("gx", "gy", None),
            P("gx", "gy", None),
            P("gx", "gy", None, None),
            wide, wide, wide, wide,
        ),
        out_specs=(wide, wide, wide, wide),
        check_vma=False,
    )
```

time: 382 us -> 72.4 us (0.19)
  the two profiles are of different devices: /device:TPU:511 before, /device:TPU:8 now
where the time goes in v1:
time: 72.4 us; the launch traced here: 71.9 us
  starting transfers between devices  50.4 us (70%)
  waiting for transfers between devices  15 us (21%)
  Pallas kernels  3.52 us (5%)
  local copies, waits for them, and re-layouts  2.11 us (3%)
  between operations  0.82 us (1%)
    ppermute x8, starting transfers between devices, swaps(): return [lax.ppermute(values, axis, pairs(count, first)) for first in (0, 1)]  50.4 us
    ppermute x8, waiting for transfers between devices, swaps(): return [lax.ppermute(values, axis, pairs(count, first)) for first in (0, 1)]  15 us
    pallas_call x5, Pallas kernels, call(): pl.pallas_call(kernel, out_shape=out_shape, name=kernel.__name__, cost_es...  3.52 us
    unnamed x24, local copies, waits for them, and re-layouts  2.11 us
  transfers between devices with their start and end apart: 8, of which 4 were waited for; matrix products, arithmetic and copies ran while one was open for 0% of the time, Pallas kernels for 1%

profile of v1, /device:TPU:8, one launch (start us, length us, event | category | flops | bytes accessed | tf_op | source)
XLA Modules:
  0.0 71.9 jit_solution(4811735706963925668)
XLA Ops:
  0.7 0.7 copy-done.5
  1.3 0.0 copy-done.11
  1.3 0.7 copy-done
  2.0 0.7 copy-done.2
  2.7 0.1 pack_kernel.1
  2.9 3.5 %collective-permute-start.1 = (f32[16,128]{1,0:T(8,128)S(1)}, f32[16,128]{1,0:T(8,128)S(1)}, u32[]{:S(2)}, u32[]{:S(2)}) collective-permute-start(f32[16,128]{1,0:T(8,128)S(1)} %pack_kernel.1), channel_id=1, source_target_pairs={{1,2},{2,1},{3,4},{4,3},{5,6},{6,5},{7,8},{8,7},{9,10},{10,9},{11,... | collective-permute-start | bytes 24584 | tf_op jit(solution)/shard_map/ppermute | solution.py:195
  6.4 19.2 %collective-permute-start = (f32[16,128]{1,0:T(8,128)S(1)}, f32[16,128]{1,0:T(8,128)S(1)}, u32[]{:S(2)}, u32[]{:S(2)}) collective-permute-start(f32[16,128]{1,0:T(8,128)S(1)} %pack_kernel.1), channel_id=1, source_target_pairs={{0,1},{1,0},{2,3},{3,2},{4,5},{5,4},{6,7},{7,6},{8,9},{9,8},{10,11... | collective-permute-start | bytes 24584 | tf_op jit(solution)/shard_map/ppermute | solution.py:195
  25.6 0.0 collective-permute-done.1.near_two
  25.6 1.6 %collective-permute-done.near_one = f32[16,128]{1,0:T(8,128)S(1)} collective-permute-done((f32[16,128]{1,0:T(8,128)S(1)}, f32[16,128]{1,0:T(8,128)S(1)}, u32[]{:S(2)}, u32[]{:S(2)}) %collective-permute-start) | collective-permute-done | bytes 8224 | tf_op jit(solution)/shard_map/ppermute | solution.py:195
  27.2 4.1 %collective-permute-start.3 = (f32[3,16,128]{2,1,0:T(8,128)S(1)}, f32[3,16,128]{2,1,0:T(8,128)S(1)}, u32[]{:S(2)}, u32[]{:S(2)}) collective-permute-start(f32[3,16,128]{2,1,0:T(8,128)S(1)} %pad_maximum_fusion), channel_id=1, source_target_pairs={{32,64},{64,32},{96,128},{128,96},{160,192},{192,160},{224,256},{2... | collective-permute-start | bytes 73736 | tf_op jit(solution)/shard_map/ppermute | solution.py:195
  31.3 1.9 %collective-permute-start.2 = (f32[3,16,128]{2,1,0:T(8,128)S(1)}, f32[3,16,128]{2,1,0:T(8,128)S(1)}, u32[]{:S(2)}, u32[]{:S(2)}) collective-permute-start(f32[3,16,128]{2,1,0:T(8,128)S(1)} %pad_maximum_fusion), channel_id=1, source_target_pairs={{0,32},{32,0},{64,96},{96,64},{128,160},{160,128},{192,224},{224,1... | collective-permute-start | bytes 73736 | tf_op jit(solution)/shard_map/ppermute | solution.py:195
  33.3 0.0 copy-start.6
  33.3 0.0 copy-start.7
  33.3 0.8 %own_kernel.1 = (bf16[384,384]{1,0:T(8,128)(2,1)S(1)}, bf16[384,384]{1,0:T(8,128)(2,1)S(1)}, f32[16,384]{1,0:T(8,128)S(1)}, s32[8,8,128]{2,1,0:T(8,128)S(1)}, f32[6,8,128]{2,1,0:T(8,128)S(1)}) custom-call(f32[3,1,128]{2,1,0:T(1,128)S(1)} %bitcast.41, f32[1,128]{1,0:T(1,128)S(1)} %bitcast.49, s32[64,128]{1,0:T(8,128)S(1)} %bitcast.36, ...), custom_call_target="tpu_custom_call" | custom-call | flops 1048576 | bytes 731136 | tf_op jit(solution)/shard_map/own_kernel/pallas_call | solution.py:206
  34.1 5.0 %collective-permute-done.3.row_two = f32[3,16,128]{2,1,0:T(8,128)S(1)} collective-permute-done((f32[3,16,128]{2,1,0:T(8,128)S(1)}, f32[3,16,128]{2,1,0:T(8,128)S(1)}, u32[]{:S(2)}, u32[]{:S(2)}) %collective-permute-start.3) | collective-permute-done | bytes 24608 | tf_op jit(solution)/shard_map/ppermute | solution.py:195
  39.1 1.4 %first_kernel.1 = (f32[3,8,128]{2,1,0:T(8,128)}, f32[3,8,128]{2,1,0:T(8,128)}, f32[16,128]{1,0:T(8,128)S(1)}, bf16[1024,384]{1,0:T(8,128)(2,1)S(1)}, bf16[1024,3...) custom-call(f32[3,1,128]{2,1,0:T(1,128)S(1)} %bitcast.42, f32[1,128]{1,0:T(1,128)S(1)} %bitcast.50, s32[1,32]{1,0:T(1,128)S(1)} %bitcast.52, ...), custom_call_target="tpu_custom_call" | custom-call | flops 1048576 | bytes 1807488 | tf_op jit(solution)/shard_map/first_kernel/pallas_call | solution.py:206
  40.6 1.9 %collective-permute-start.5 = (f32[16,128]{1,0:T(8,128)S(1)}, f32[16,128]{1,0:T(8,128)S(1)}, u32[]{:S(2)}, u32[]{:S(2)}) collective-permute-start(f32[16,128]{1,0:T(8,128)S(1)} %get-tuple-element.27), channel_id=1, source_target_pairs={{1,2},{2,1},{3,4},{4,3},{5,6},{6,5},{7,8},{8,7},{9,10},{10,9},{11,... | collective-permute-start | bytes 24584 | tf_op jit(solution)/shard_map/ppermute | solution.py:195
  42.5 14.9 %collective-permute-start.4 = (f32[16,128]{1,0:T(8,128)S(1)}, f32[16,128]{1,0:T(8,128)S(1)}, u32[]{:S(2)}, u32[]{:S(2)}) collective-permute-start(f32[16,128]{1,0:T(8,128)S(1)} %get-tuple-element.27), channel_id=1, source_target_pairs={{0,1},{1,0},{2,3},{3,2},{4,5},{5,4},{6,7},{7,6},{8,9},{9,8},{10,11... | collective-permute-start | bytes 24584 | tf_op jit(solution)/shard_map/ppermute | solution.py:195
  57.4 1.6 %collective-permute-done.4.near_one = f32[16,128]{1,0:T(8,128)S(1)} collective-permute-done((f32[16,128]{1,0:T(8,128)S(1)}, f32[16,128]{1,0:T(8,128)S(1)}, u32[]{:S(2)}, u32[]{:S(2)}) %collective-permute-start.4) | collective-permute-done | bytes 8224 | tf_op jit(solution)/shard_map/ppermute | solution.py:195
  59.1 2.9 %collective-permute-start.7 = (f32[3,16,128]{2,1,0:T(8,128)S(1)}, f32[3,16,128]{2,1,0:T(8,128)S(1)}, u32[]{:S(2)}, u32[]{:S(2)}) collective-permute-start(f32[3,16,128]{2,1,0:T(8,128)S(1)} %pad_maximum_fusion.1), channel_id=1, source_target_pairs={{32,64},{64,32},{96,128},{128,96},{160,192},{192,160},{224,256},{2... | collective-permute-start | bytes 73736 | tf_op jit(solution)/shard_map/ppermute | solution.py:195
  62.0 1.9 %collective-permute-start.6 = (f32[3,16,128]{2,1,0:T(8,128)S(1)}, f32[3,16,128]{2,1,0:T(8,128)S(1)}, u32[]{:S(2)}, u32[]{:S(2)}) collective-permute-start(f32[3,16,128]{2,1,0:T(8,128)S(1)} %pad_maximum_fusion.1), channel_id=1, source_target_pairs={{0,32},{32,0},{64,96},{96,64},{128,160},{160,128},{192,224},{224,1... | collective-permute-start | bytes 73736 | tf_op jit(solution)/shard_map/ppermute | solution.py:195
  63.9 0.2 again_kernel.1.partial
  64.2 6.8 %collective-permute-done.7.row_two = f32[3,16,128]{2,1,0:T(8,128)S(1)} collective-permute-done((f32[3,16,128]{2,1,0:T(8,128)S(1)}, f32[3,16,128]{2,1,0:T(8,128)S(1)}, u32[]{:S(2)}, u32[]{:S(2)}) %collective-permute-start.7) | collective-permute-done | bytes 24608 | tf_op jit(solution)/shard_map/ppermute | solution.py:195
  70.9 0.9 %last_kernel.1 = (f32[3,8,128]{2,1,0:T(8,128)}, f32[3,8,128]{2,1,0:T(8,128)}) custom-call(bf16[1024,384]{1,0:T(8,128)(2,1)S(1)} %get-tuple-element.21.w_high, bf16[1024,384]{1,0:T(8,128)(2,1)S(1)} %get-tuple-element.22.w_low, f32[3,16,128]{2,1,0:T(8,128)S(1)} %again_kernel.1.partial, f32[16,128]{1,0:T(8,128)S(1)} %collective-permute-done.4.near_one, ...), custom_call_target="tpu_custom_call" | custom-call | flops 1048576 | bytes 1687552 | tf_op jit(solution)/shard_map/last_kernel/pallas_call | solution.py:206
  (23 shorter events, 0.0 us)
Async XLA Ops:
  0.6 0.7 copy-start.5
  0.6 0.7 copy-start.10
  0.7 0.7 copy-start.11
  1.3 0.7 copy-start
  2.0 0.7 copy-start.2
  2.7 30.5 %copy-start.4 = (s32[1,1,64,128]{3,2,1,0:T(8,128)S(1)}, s32[1,1,64,128]{3,2,1,0:T(8,128)}, u32[]{:S(2)}) copy-start(s32[1,1,64,128]{3,2,1,0:T(8,128)} %param.11) | copy-start | bytes 98308
  2.9 22.7 %collective-permute-start.1 = (f32[16,128]{1,0:T(8,128)S(1)}, f32[16,128]{1,0:T(8,128)S(1)}, u32[]{:S(2)}, u32[]{:S(2)}) collective-permute-start(f32[16,128]{1,0:T(8,128)S(1)} %pack_kernel.1), channel_id=1, source_target_pairs={{1,2},{2,1},{3,4},{4,3},{5,6},{6,5},{7,8},{8,7},{9,10},{10,9},{11,... | collective-permute-start | bytes 24584 | tf_op jit(solution)/shard_map/ppermute | solution.py:195
  6.4 20.9 %collective-permute-start = (f32[16,128]{1,0:T(8,128)S(1)}, f32[16,128]{1,0:T(8,128)S(1)}, u32[]{:S(2)}, u32[]{:S(2)}) collective-permute-start(f32[16,128]{1,0:T(8,128)S(1)} %pack_kernel.1), channel_id=1, source_target_pairs={{0,1},{1,0},{2,3},{3,2},{4,5},{5,4},{6,7},{7,6},{8,9},{9,8},{10,11... | collective-permute-start | bytes 24584 | tf_op jit(solution)/shard_map/ppermute | solution.py:195
  27.2 6.0 %copy-start.1 = (f32[3,8,1,1,128]{4,3,2,1,0:T(1,128)S(1)}, f32[3,8,1,1,128]{4,3,2,1,0:T(1,128)}, u32[]{:S(2)}) copy-start(f32[3,8,1,1,128]{4,3,2,1,0:T(1,128)} %param.13) | copy-start | bytes 36868
  27.2 6.0 %copy-start.3 = (f32[3,8,1,1,128]{4,3,2,1,0:T(1,128)S(1)}, f32[3,8,1,1,128]{4,3,2,1,0:T(1,128)}, u32[]{:S(2)}) copy-start(f32[3,8,1,1,128]{4,3,2,1,0:T(1,128)} %param.15) | copy-start | bytes 36868
  27.2 11.9 %collective-permute-start.3 = (f32[3,16,128]{2,1,0:T(8,128)S(1)}, f32[3,16,128]{2,1,0:T(8,128)S(1)}, u32[]{:S(2)}, u32[]{:S(2)}) collective-permute-start(f32[3,16,128]{2,1,0:T(8,128)S(1)} %pad_maximum_fusion), channel_id=1, source_target_pairs={{32,64},{64,32},{96,128},{128,96},{160,192},{192,160},{224,256},{2... | collective-permute-start | bytes 73736 | tf_op jit(solution)/shard_map/ppermute | solution.py:195
  31.3 7.8 %collective-permute-start.2 = (f32[3,16,128]{2,1,0:T(8,128)S(1)}, f32[3,16,128]{2,1,0:T(8,128)S(1)}, u32[]{:S(2)}, u32[]{:S(2)}) collective-permute-start(f32[3,16,128]{2,1,0:T(8,128)S(1)} %pad_maximum_fusion), channel_id=1, source_target_pairs={{0,32},{32,0},{64,96},{96,64},{128,160},{160,128},{192,224},{224,1... | collective-permute-start | bytes 73736 | tf_op jit(solution)/shard_map/ppermute | solution.py:195
  33.3 5.8 %copy-start.6 = (f32[3,8,1,1,128]{4,3,2,1,0:T(1,128)S(1)}, f32[3,8,1,1,128]{4,3,2,1,0:T(1,128)}, u32[]{:S(2)}) copy-start(f32[3,8,1,1,128]{4,3,2,1,0:T(1,128)} %param.12) | copy-start | bytes 36868
  33.3 5.8 %copy-start.7 = (f32[3,8,1,1,128]{4,3,2,1,0:T(1,128)S(1)}, f32[3,8,1,1,128]{4,3,2,1,0:T(1,128)}, u32[]{:S(2)}) copy-start(f32[3,8,1,1,128]{4,3,2,1,0:T(1,128)} %param.14) | copy-start | bytes 36868
  40.6 16.9 %collective-permute-start.5 = (f32[16,128]{1,0:T(8,128)S(1)}, f32[16,128]{1,0:T(8,128)S(1)}, u32[]{:S(2)}, u32[]{:S(2)}) collective-permute-start(f32[16,128]{1,0:T(8,128)S(1)} %get-tuple-element.27), channel_id=1, source_target_pairs={{1,2},{2,1},{3,4},{4,3},{5,6},{6,5},{7,8},{8,7},{9,10},{10,9},{11,... | collective-permute-start | bytes 24584 | tf_op jit(solution)/shard_map/ppermute | solution.py:195
  42.5 16.6 %collective-permute-start.4 = (f32[16,128]{1,0:T(8,128)S(1)}, f32[16,128]{1,0:T(8,128)S(1)}, u32[]{:S(2)}, u32[]{:S(2)}) collective-permute-start(f32[16,128]{1,0:T(8,128)S(1)} %get-tuple-element.27), channel_id=1, source_target_pairs={{0,1},{1,0},{2,3},{3,2},{4,5},{5,4},{6,7},{7,6},{8,9},{9,8},{10,11... | collective-permute-start | bytes 24584 | tf_op jit(solution)/shard_map/ppermute | solution.py:195
  59.1 4.9 %copy-start.8 = (f32[3,8,128]{2,1,0:T(8,128)S(1)}, f32[3,8,128]{2,1,0:T(8,128)}, u32[]{:S(2)}) copy-start(f32[3,8,128]{2,1,0:T(8,128)} %get-tuple-element.20.vec) | copy-start | bytes 36868
  59.1 4.9 %copy-start.9 = (f32[3,8,128]{2,1,0:T(8,128)S(1)}, f32[3,8,128]{2,1,0:T(8,128)}, u32[]{:S(2)}) copy-start(f32[3,8,128]{2,1,0:T(8,128)} %get-tuple-element.26.heat) | copy-start | bytes 36868
  59.1 11.9 %collective-permute-start.7 = (f32[3,16,128]{2,1,0:T(8,128)S(1)}, f32[3,16,128]{2,1,0:T(8,128)S(1)}, u32[]{:S(2)}, u32[]{:S(2)}) collective-permute-start(f32[3,16,128]{2,1,0:T(8,128)S(1)} %pad_maximum_fusion.1), channel_id=1, source_target_pairs={{32,64},{64,32},{96,128},{128,96},{160,192},{192,160},{224,256},{2... | collective-permute-start | bytes 73736 | tf_op jit(solution)/shard_map/ppermute | solution.py:195
  62.0 8.9 %collective-permute-start.6 = (f32[3,16,128]{2,1,0:T(8,128)S(1)}, f32[3,16,128]{2,1,0:T(8,128)S(1)}, u32[]{:S(2)}, u32[]{:S(2)}) collective-permute-start(f32[3,16,128]{2,1,0:T(8,128)S(1)} %pad_maximum_fusion.1), channel_id=1, source_target_pairs={{0,32},{32,0},{64,96},{96,64},{128,160},{160,128},{192,224},{224,1... | collective-permute-start | bytes 73736 | tf_op jit(solution)/shard_map/ppermute | solution.py:195

commit v2 on v1

v2 whole, which is shorter than its diff:
```python
import functools

import jax
import jax.numpy as jnp
from jax import lax
from jax.experimental import pallas as pl
from jax.experimental.pallas import tpu as pltpu
from jax.sharding import PartitionSpec as P

column_edge = 20.0
reach_sq = 64.0
A = 128
G = 32
NB = 64
F = 16
OWN = 3 * A
F32 = jnp.float32
BF16 = jnp.bfloat16
KEYS = ((0, 0), (0, 1), (0, 2), (1, 1), (1, 2), (2, 2))
RING = ((-1, -1), (-1, 0), (-1, 1), (0, -1), (0, 1), (1, -1), (1, 0), (1, 1))
WIDE = tuple((x, y) for x in range(-2, 3) for y in range(-2, 3))
KINDS = 3


def other(i, count):
    return (i + 1) % count if i % 2 else (i - 1) % count


def routes(nx, ny):
    def pair_x(x, y):
        return x ^ 1, y

    def pair_y(x, y):
        return x, y ^ 1

    def across_y(x, y):
        return (x, other(y, ny)) if y % 4 in (0, 3) else None

    def across_x(x, y):
        return (other(x, nx), y) if y % 4 in (1, 2) else None

    def beside(x, y):
        if y % 4 in (1, 2):
            return x, other(y, ny)
        if x in (0, nx - 1):
            return other(x, nx), other(y, ny)
        return other(x, nx), y

    return (
        (pair_y, -1),
        (pair_x, 0),
        (across_x, 1),
        (across_y, 0),
        (pair_x, 3),
        (beside, 4),
        (pair_x, 5),
        (pair_y, 6),
    )


def class_of(x, y, nx):
    return 4 * (0 if x == 0 else 3 if x == nx - 1 else 1 + (x + 1) % 2) + y % 4


@functools.lru_cache(None)
def make_plan(nx, ny):
    devices = [(x, y) for x in range(nx) for y in range(ny)]
    steps = routes(nx, ny)

    def wanted(x, y):
        return [
            (kind, (x + a) % nx, (y + b) % ny)
            for kind in range(KINDS)
            for a, b in (WIDE if kind == 0 else RING)
        ]

    known = [{d: {(k, *d) for k in range(KINDS)} for d in devices}]
    for target, base in steps:
        later = {d: set(known[-1][d]) for d in devices}
        for d in devices:
            if target(*d):
                later[target(*d)] |= known[base + 1][d]
        known.append(later)
    first = {d: {} for d in devices}
    for t, state in enumerate(known):
        for d in devices:
            for item in state[d]:
                first[d].setdefault(item, t)
    demand = {d: set(wanted(*d)) for d in devices}
    assert all(demand[d] <= known[-1][d] for d in devices)
    sent = [None] * len(steps)
    for i in reversed(range(len(steps))):
        target, base = steps[i]
        sent[i] = {}
        for d in devices:
            t = target(*d)
            if t is None:
                sent[i][d] = []
                continue
            items = {m for m in demand[t] if first[t][m] == i + 1 and m in known[base + 1][d]}
            near = lambda v, count: (v + count // 2) % count
            sent[i][d] = sorted(
                items, key=lambda m: (m[0], near(m[1] - t[0], nx), near(m[2] - t[1], ny))
            )
        for d in devices:
            demand[d] |= set(sent[i][d])
    sizes = [max(1, *(len(v) for v in s.values())) for s in sent]
    starts = [KINDS + sum(sizes[:i]) for i in range(len(sizes))]
    place = {d: {(k, *d): k for k in range(KINDS)} for d in devices}
    for i, (target, _) in enumerate(steps):
        for d in devices:
            for j, item in enumerate(sent[i][d]):
                place[target(*d)].setdefault(item, starts[i] + j)
    send_rows = [{} for _ in steps]
    last_rows = {}
    for d in devices:
        c = class_of(*d, nx)
        for i in range(len(steps)):
            row = tuple(place[d][item] for item in sent[i][d])
            assert send_rows[i].setdefault(c, row) == row
        row = tuple(place[d][item] for item in wanted(*d))
        assert last_rows.setdefault(c, row) == row
    links = [
        [(x * ny + y, t[0] * ny + t[1]) for x, y in devices for t in [f(x, y)] if t]
        for f, _ in steps
    ]
    return steps, sizes, starts, send_rows, last_rows, links


def for_each_row(rows, nx, body):
    x, y = lax.axis_index("gx"), lax.axis_index("gy")
    column = jnp.where(x == 0, 0, jnp.where(x == nx - 1, 3, 1 + lax.rem(x + 1, 2)))
    mine = 4 * column + lax.rem(y, 4)
    classes = {}
    for c, row in rows.items():
        classes.setdefault(row, []).append(c)
    for row, members in classes.items():
        hit = mine == members[0]
        for c in members[1:]:
            hit = hit | (mine == c)
        pl.when(hit)(functools.partial(body, row))


def block_at(refs, starts, place):
    if place < KINDS:
        return refs[0][place]
    i = max(j for j in range(len(starts)) if starts[j] <= place)
    return refs[i + 1][place - starts[i]]


def relay_kernel(rows, starts, nx, *refs):
    out = refs[-1]

    def body(row):
        for j, place in enumerate(row):
            out[j] = block_at(refs, starts, place)
        for j in range(len(row), out.shape[0]):
            out[j] = jnp.zeros((F, A), F32)

    for_each_row(rows, nx, body)


def split(x):
    high = x.astype(BF16)
    return high, (x - high.astype(F32)).astype(BF16)


def border_lanes(border, values):
    index = jnp.concatenate([border[...]] * (A // G), axis=1)
    return jnp.take_along_axis(values, jnp.broadcast_to(index, values.shape), axis=1)


def by_group(parts):
    group = lax.broadcasted_iota(jnp.int32, parts[0].shape, 1) // G
    out = parts[3]
    for q in range(3):
        out = jnp.where(group == q, parts[q], out)
    return out


def stacked(vec, heat):
    return [jnp.concatenate([vec[b], heat[b]], axis=0) for b in range(3)]


def count_slots(entries, groups):
    sub = lax.broadcasted_iota(jnp.int32, (8, A), 0)
    counters = [jnp.zeros((8, A), jnp.int32) for _ in groups]
    for n in range(NB):
        e = jnp.broadcast_to(entries[n : n + 1, :], (8, A))
        mark = jnp.where(sub == (e & 7), jnp.left_shift(jnp.int32(1), e & 24), 0)
        which = lax.shift_right_arithmetic(e, 5)
        for i, g in enumerate(groups):
            counters[i] += jnp.where(which == g, mark, 0)
    return counters


FAR_GROUPS = [4 * (3 * (x + 1) + y + 1) for x, y in RING]


def pair_terms(counter, source, home):
    tiles = [lax.shift_right_logical(counter, 8 * q) & 255 for q in range(4)]
    count = jnp.concatenate(tiles, axis=0).astype(F32)
    d = [source[a] - home[a] for a in range(3)]
    r2 = d[0] * d[0] + d[1] * d[1] + d[2] * d[2]
    near = r2 + 1.0
    inverse = (count * (home[3] * source[3])) / ((reach_sq + r2) * near)
    c = inverse * near * (reach_sq / NB)
    bend = inverse * (2.0 * reach_sq / NB)
    g = [bend * d[a] for a in range(3)]
    return {(a, b): (g[a] * d[b] + c if a == b else g[a] * d[b]) for a, b in KEYS}


def put_terms(w_high, w_low, sums, rows, terms):
    for (a, b), value in terms.items():
        part = value[0:8] + value[8:16] + value[16:24] + value[24:32]
        sums[(a, b)] = sums[(a, b)] + part if (a, b) in sums else part
        high, low = split(value)
        for p, q in sorted({(a, b), (b, a)}):
            w_high[rows[q] : rows[q] + G, p * A : (p + 1) * A] = high
            w_low[rows[q] : rows[q] + G, p * A : (p + 1) * A] = low


def total(sums):
    return {key: jnp.sum(value, axis=0, keepdims=True) for key, value in sums.items()}


def apply_weights(w_high, w_low, lhs):
    high, low = split(lhs)
    both = jnp.concatenate([high, low], axis=0)
    main = jnp.dot(both, w_high[...], preferred_element_type=F32)
    rest = jnp.dot(high, w_low[...], preferred_element_type=F32)
    return main[:F] + main[F:] + rest


def self_product(terms, fields, a):
    return sum(terms[(min(a, b), max(a, b))] * fields[b] for b in range(3))


def spread(rows):
    return [jnp.broadcast_to(r, (G, A)) for r in rows]


def own_kernel(pos, spring, border, entries, vec, heat, vec0, heat0,
               payload, w_high, w_low, partial, self_out, counts):
    counters = count_slots(entries[...], FAR_GROUPS + [16, 17, 18, 19])
    for i in range(8):
        counts[i] = counters[i]
    root = jnp.sqrt(spring[...])
    home = spread([pos[0], pos[1], pos[2], root])
    geo = jnp.concatenate([pos[0], pos[1], pos[2], root, jnp.zeros((4, A), F32)], axis=0).T
    sums = {}
    for t in range(4):
        source = spread([geo[t * G : (t + 1) * G, c : c + 1] for c in range(4)])
        terms = pair_terms(counters[8 + t], source, home)
        put_terms(w_high, w_low, sums, [b * A + t * G for b in range(3)], terms)
    own_terms = total(sums)
    for i, key in enumerate(KEYS):
        self_out[i : i + 1, :] = own_terms[key]
    current, previous = stacked(vec, heat), stacked(vec0, heat0)
    far = apply_weights(w_high, w_low, jnp.concatenate(current, axis=1))
    begun = []
    for a in range(3):
        inner = self_product(own_terms, current, a) - far[:, a * A : (a + 1) * A] - current[a]
        begun.append(2.0 * inner - previous[a])
        partial[a] = begun[a]
    geometry = jnp.concatenate(
        [pos[0], pos[1], pos[2], spring[...], jnp.zeros((F - 4, A), F32)], axis=0
    )
    picked = functools.partial(border_lanes, border)
    lists = [picked(entries[F * s : F * (s + 1), :].astype(F32)) for s in range(4)]
    payload[0] = by_group([picked(x) for x in (*current, geometry)])
    payload[1] = by_group([picked(x) for x in begun] + [lists[3]])
    payload[2] = by_group(lists[:3] + [jnp.zeros((F, A), F32)])


def moved(block, source, target):
    shift = (target - source) % 4 * G
    return pltpu.roll(block, shift, 1) if shift else block


def last_kernel(rows, starts, nx, n_in, pos, spring, vec, heat, partial, self_in, counts,
                own_high, own_low, *rest):
    received = rest[:n_in]
    v2, h2, v3, h3, pool, far_high, far_low, edge_high, edge_low = rest[n_in:]

    def body(row):
        for j, place in enumerate(row):
            pool[j] = block_at(received, starts, place)

    for_each_row(rows, nx, body)
    values = {s: pool[j] for j, s in enumerate(WIDE)}
    halves = {s: split(x) for s, x in values.items()}
    geo = jnp.concatenate(
        [values[s][0:4] for s in WIDE] + [jnp.zeros((A - 4 * len(WIDE), A), F32)], axis=0
    ).T[3 * G :]
    geo = {
        s: [
            jnp.sqrt(geo[:, 4 * j + c : 4 * j + c + 1]) if c == 3 else geo[:, 4 * j + c : 4 * j + c + 1]
            for c in range(4)
        ]
        for j, s in enumerate(WIDE)
    }
    wide_geo = {s: spread(x) for s, x in geo.items()}

    def shifted(cols, s):
        return [cols[0] + column_edge * s[0], cols[1] + column_edge * s[1], cols[2], cols[3]]

    quads = (RING[:4], RING[4:])
    sides = []
    for q, quad in enumerate(quads):
        blocks = [[pool[len(WIDE) + k * 8 + 4 * q + g] for g in range(4)] for k in range(2)]
        fields = [by_group([moved(values[s], b, g) for g, s in enumerate(quad)]) for b in range(3)]
        begun = [by_group([moved(x, b, g) for g, x in enumerate(blocks[0])]) for b in range(3)]
        sides.append((quad, fields, begun, blocks))

    home = spread([pos[0], pos[1], pos[2], jnp.sqrt(spring[...])])
    sums = {}
    for j, s in enumerate(RING):
        terms = pair_terms(counts[j], shifted(wide_geo[s], s), home)
        put_terms(far_high, far_low, sums, [b * 2 * A + j * G for b in range(3)], terms)
    far_terms = total(sums)

    def beside(first, second):
        return jnp.concatenate([x for b in range(3) for x in (first[b], second[b])], axis=1)

    current = stacked(vec, heat)
    far = apply_weights(far_high, far_low, beside(sides[0][1], sides[1][1]))
    second = []
    for a in range(3):
        inner = self_product(far_terms, current, a) - far[:, a * A : (a + 1) * A]
        second.append(partial[a] + 2.0 * inner)
        v2[a] = second[a][:8]
        h2[a] = second[a][8:]

    for j in range(len(RING)):
        edge_high[j * A + 3 * G : (j + 1) * A, :] = jnp.zeros((G, OWN), BF16)
        edge_low[j * A + 3 * G : (j + 1) * A, :] = jnp.zeros((G, OWN), BF16)
    edges = []
    for quad, fields, begun, blocks in sides:
        lists = [
            by_group([moved(blocks[1 if k < 3 else 0][g], k, g) for g in range(4)]) for k in range(4)
        ]
        counters = count_slots(jnp.concatenate(lists, axis=0).astype(jnp.int32), FAR_GROUPS)
        there = by_group([moved(values[s][0:8], 3, g) for g, s in enumerate(quad)])
        home = spread([there[0:1], there[1:2], there[2:3], jnp.sqrt(there[3:4])])
        sums = {}
        for j, s in enumerate(RING):
            around = [(t[0] + s[0], t[1] + s[1]) for t in quad]
            source = [by_group([wide_geo[t][c] for t in around]) for c in range(4)]
            terms = pair_terms(counters[j], shifted(source, s), home)
            put_terms(edge_high, edge_low, sums, [j * A + b * G for b in range(3)], terms)
        terms = total(sums)
        lhs = [
            jnp.concatenate(
                [
                    jnp.concatenate([halves[(t[0] + s[0], t[1] + s[1])][h] for s in RING], axis=1)
                    for t in quad
                ],
                axis=0,
            )
            for h in range(2)
        ]
        main = jnp.dot(jnp.concatenate(lhs, axis=0), edge_high[...], preferred_element_type=F32)
        small = jnp.dot(lhs[0], edge_low[...], preferred_element_type=F32)
        result = []
        for a in range(3):
            cut = slice(a * A, (a + 1) * A)
            sums_of = [
                main[g * F : (g + 1) * F, cut]
                + main[(4 + g) * F : (5 + g) * F, cut]
                + small[g * F : (g + 1) * F, cut]
                for g in range(4)
            ]
            inner = self_product(terms, fields, a) - by_group(sums_of)
            result.append(begun[a] + 2.0 * inner)
        edges.append(result)

    all_terms = {key: far_terms[key] + self_in[i : i + 1, :] for i, key in enumerate(KEYS)}
    far = apply_weights(far_high, far_low, beside(*edges))
    far += apply_weights(own_high, own_low, jnp.concatenate(second, axis=1))
    for a in range(3):
        inner = self_product(all_terms, second, a) - far[:, a * A : (a + 1) * A] - second[a]
        third = 2.0 * inner - current[a]
        v3[a] = third[:8]
        h3[a] = third[8:]


def call(kernel, out_shape, args, scratch=()):
    size = sum(x.size * x.dtype.itemsize for x in (*args, *out_shape))
    return pl.pallas_call(
        kernel,
        out_shape=out_shape,
        scratch_shapes=scratch,
        cost_estimate=pl.CostEstimate(flops=2**20, bytes_accessed=size, transcendentals=0),
        compiler_params=pltpu.CompilerParams(vmem_limit_bytes=24 * 2**20),
    )(*args)


def shards(positions, spring, border, neighbours, vec_prev, vec_now, heat_prev, heat_now):
    nx, ny = lax.axis_size("gx"), lax.axis_size("gy")
    steps, sizes, starts, send_rows, last_rows, links = make_plan(nx, ny)
    shape = jax.ShapeDtypeStruct
    vector = shape((3, 8, A), F32)
    pos = positions.reshape(3, 1, A)
    stiff = spring.reshape(1, A)
    entries = neighbours.reshape(NB, A)
    v0, v1, h0, h1 = (x.reshape(3, 8, A) for x in (vec_prev, vec_now, heat_prev, heat_now))
    payload, own_high, own_low, partial, self_terms, counts = call(
        own_kernel,
        (
            shape((KINDS, F, A), F32),
            shape((OWN, OWN), BF16),
            shape((OWN, OWN), BF16),
            shape((3, F, A), F32),
            shape((6, A), F32),
            shape((8, 8, A), jnp.int32),
        ),
        (pos, stiff, border.reshape(1, G), entries, v1, h1, v0, h0),
    )
    received = [payload]
    for i, (_, base) in enumerate(steps):
        known = received[: base + 2]
        if send_rows[i][0] == tuple(range(KINDS)) and len(set(send_rows[i].values())) == 1:
            outgoing = payload
        else:
            (outgoing,) = call(
                functools.partial(relay_kernel, send_rows[i], starts, nx),
                (shape((sizes[i], F, A), F32),),
                known,
            )
        received.append(lax.ppermute(outgoing, ("gx", "gy"), links[i]))
    v2, h2, v3, h3 = call(
        functools.partial(last_kernel, last_rows, starts, nx, len(received)),
        (vector,) * 4,
        (pos, stiff, v1, h1, partial, self_terms, counts, own_high, own_low, *received),
        (
            pltpu.VMEM((len(WIDE) + 16, F, A), F32),
            pltpu.VMEM((6 * A, OWN), BF16),
            pltpu.VMEM((6 * A, OWN), BF16),
            pltpu.VMEM((8 * A, OWN), BF16),
            pltpu.VMEM((8 * A, OWN), BF16),
        ),
    )
    whole = vec_prev.shape
    return v2.reshape(whole), v3.reshape(whole), h2.reshape(whole), h3.reshape(whole)


def solution(mesh):
    wide = P(None, None, "gx", "gy", None)
    return jax.shard_map(
        shards,
        mesh=mesh,
        in_specs=(
            P(None, "gx", "gy", None),
            P("gx", "gy", None),
            P("gx", "gy", None),
            P("gx", "gy", None, None),
            wide, wide, wide, wide,
        ),
        out_specs=(wide, wide, wide, wide),
        check_vma=False,
    )
```

time: 72.4 us -> 68.4 us (0.945)
  the two profiles are of different devices: /device:TPU:8 before, /device:TPU:1 now
where the time goes in v2:
time: 68.4 us; the launch traced here: 67.8 us
  starting transfers between devices  45.5 us (67%)
  waiting for transfers between devices  13.6 us (20%)
  Pallas kernels  4.43 us (6%)
  local copies, waits for them, and re-layouts  3.56 us (5%)
  between operations  0.76 us (1%)
    ppermute x8, starting transfers between devices, shards(): received.append(lax.ppermute(outgoing, ('gx', 'gy'), links[i]))  45.5 us
    ppermute x8, waiting for transfers between devices, shards(): received.append(lax.ppermute(outgoing, ('gx', 'gy'), links[i]))  13.6 us
    pallas_call x9, Pallas kernels, call(): pl.pallas_call(kernel, out_shape=out_shape, scratch_shapes=scratch, cost_...  4.43 us
    unnamed x18, local copies, waits for them, and re-layouts  3.56 us
  transfers between devices with their start and end apart: 8, of which 7 were waited for; matrix products, arithmetic and copies ran while one was open for 0% of the time, Pallas kernels for 0%

profile of v2, /device:TPU:1, one launch (start us, length us, event | category | flops | bytes accessed | tf_op | source)
XLA Modules:
  0.0 67.8 jit_solution(17532840057885517132)
XLA Ops:
  0.6 0.0 copy-start
  0.7 0.7 copy-done
  1.4 0.7 %copy-done.1 = f32[3,8,1,1,128]{4,3,2,1,0:T(1,128)S(1)} copy-done((f32[3,8,1,1,128]{4,3,2,1,0:T(1,128)S(1)}, f32[3,8,1,1,128]{4,3,2,1,0:T(1,128)}, u32[]{:S(2)}) %copy-start.1) | copy-done | bytes 12312
  2.1 0.8 %copy-done.3 = s32[1,1,64,128]{3,2,1,0:T(8,128)S(1)} copy-done((s32[1,1,64,128]{3,2,1,0:T(8,128)S(1)}, s32[1,1,64,128]{3,2,1,0:T(8,128)}, u32[]{:S(2)}) %copy-start.3) | copy-done | bytes 32792
  2.8 0.7 %copy-done.4 = f32[3,8,1,1,128]{4,3,2,1,0:T(1,128)S(1)} copy-done((f32[3,8,1,1,128]{4,3,2,1,0:T(1,128)S(1)}, f32[3,8,1,1,128]{4,3,2,1,0:T(1,128)}, u32[]{:S(2)}) %copy-start.4) | copy-done | bytes 12312
  3.5 0.7 %copy-done.5 = f32[3,8,1,1,128]{4,3,2,1,0:T(1,128)S(1)} copy-done((f32[3,8,1,1,128]{4,3,2,1,0:T(1,128)S(1)}, f32[3,8,1,1,128]{4,3,2,1,0:T(1,128)}, u32[]{:S(2)}) %copy-start.5) | copy-done | bytes 12312
  4.2 0.8 %shard_map.111 = (f32[3,16,128]{2,1,0:T(8,128)S(1)}, bf16[384,384]{1,0:T(8,128)(2,1)S(1)}, bf16[384,384]{1,0:T(8,128)(2,1)S(1)}, f32[3,16,128]{2,1,0:T(8,128)S(1...) custom-call(f32[3,1,128]{2,1,0:T(1,128)S(1)} %bitcast.27, f32[1,128]{1,0:T(1,128)S(1)} %bitcast.29, ...), custom_call_target="tpu_custom_call" | custom-call | flops 1048576 | bytes 758912 | tf_op jit(solution)/shard_map/pallas_call | solution.py:390
  5.1 4.0 %collective-permute-start = (f32[3,16,128]{2,1,0:T(8,128)S(1)}, f32[3,16,128]{2,1,0:T(8,128)S(1)}, u32[]{:S(2)}, u32[]{:S(2)}) collective-permute-start(f32[3,16,128]{2,1,0:T(8,128)S(1)} %get-tuple-element.19.refs_0_.rest_0_), channel_id=1, source_target_pairs={{0,1},{1,0},{2,3},{3,2},{4,5},{5,4},{6,7},{7,6},{8,9},{9,8},{10,11... | collective-permute-start | bytes 73736 | tf_op jit(solution)/shard_map/ppermute | solution.py:431
  9.1 1.2 %collective-permute-done.refs_1_.rest_1_ = f32[3,16,128]{2,1,0:T(8,128)S(1)} collective-permute-done((f32[3,16,128]{2,1,0:T(8,128)S(1)}, f32[3,16,128]{2,1,0:T(8,128)S(1)}, u32[]{:S(2)}, u32[]{:S(2)}) %collective-permute-start) | collective-permute-done | bytes 24608 | tf_op jit(solution)/shard_map/ppermute | solution.py:431
  10.3 9.2 %collective-permute-start.1 = (f32[6,16,128]{2,1,0:T(8,128)S(1)}, f32[6,16,128]{2,1,0:T(8,128)S(1)}, u32[]{:S(2)}, u32[]{:S(2)}) collective-permute-start(f32[6,16,128]{2,1,0:T(8,128)S(1)} %shard_map.112), channel_id=1, source_target_pairs={{0,32},{1,33},{2,34},{3,35},{4,36},{5,37},{6,38},{7,39},{8,40},{9,... | collective-permute-start | bytes 147464 | tf_op jit(solution)/shard_map/ppermute | solution.py:431
  19.5 0.9 %collective-permute-done.1.refs_2_.rest_2_ = f32[6,16,128]{2,1,0:T(8,128)S(1)} collective-permute-done((f32[6,16,128]{2,1,0:T(8,128)S(1)}, f32[6,16,128]{2,1,0:T(8,128)S(1)}, u32[]{:S(2)}, u32[]{:S(2)}) %collective-permute-start.1) | collective-permute-done | bytes 49184 | tf_op jit(solution)/shard_map/ppermute | solution.py:431
  20.4 0.7 collective-permute-start.2
  21.1 14.7 %collective-permute-start.3 = (f32[6,16,128]{2,1,0:T(8,128)S(1)}, f32[6,16,128]{2,1,0:T(8,128)S(1)}, u32[]{:S(2)}, u32[]{:S(2)}) collective-permute-start(f32[6,16,128]{2,1,0:T(8,128)S(1)} %shard_map.114), channel_id=1, source_target_pairs={{0,31},{3,4},{4,3},{7,8},{8,7},{11,12},{12,11},{15,16},{16,15},{19... | collective-permute-start | bytes 147464 | tf_op jit(solution)/shard_map/ppermute | solution.py:431
  35.9 3.0 %collective-permute-done.3.refs_4_.rest_4_ = f32[6,16,128]{2,1,0:T(8,128)S(1)} collective-permute-done((f32[6,16,128]{2,1,0:T(8,128)S(1)}, f32[6,16,128]{2,1,0:T(8,128)S(1)}, u32[]{:S(2)}, u32[]{:S(2)}) %collective-permute-start.3) | collective-permute-done | bytes 49184 | tf_op jit(solution)/shard_map/ppermute | solution.py:431
  38.9 0.0 collective-permute-done.2.refs_3_.rest_3_
  38.9 3.4 %collective-permute-start.4 = (f32[4,16,128]{2,1,0:T(8,128)S(1)}, f32[4,16,128]{2,1,0:T(8,128)S(1)}, u32[]{:S(2)}, u32[]{:S(2)}) collective-permute-start(f32[4,16,128]{2,1,0:T(8,128)S(1)} %shard_map.115), channel_id=1, source_target_pairs={{0,32},{1,33},{2,34},{3,35},{4,36},{5,37},{6,38},{7,39},{8,40},{9,... | collective-permute-start | bytes 98312 | tf_op jit(solution)/shard_map/ppermute | solution.py:431
  42.3 0.8 %collective-permute-done.4.refs_5_.rest_5_ = f32[4,16,128]{2,1,0:T(8,128)S(1)} collective-permute-done((f32[4,16,128]{2,1,0:T(8,128)S(1)}, f32[4,16,128]{2,1,0:T(8,128)S(1)}, u32[]{:S(2)}, u32[]{:S(2)}) %collective-permute-start.4) | collective-permute-done | bytes 32800 | tf_op jit(solution)/shard_map/ppermute | solution.py:431
  43.2 2.2 %collective-permute-start.5 = (f32[16,16,128]{2,1,0:T(8,128)S(1)}, f32[16,16,128]{2,1,0:T(8,128)S(1)}, u32[]{:S(2)}, u32[]{:S(2)}) collective-permute-start(f32[16,16,128]{2,1,0:T(8,128)S(1)} %shard_map.116), channel_id=1, source_target_pairs={{0,511},{1,2},{2,1},{3,484},{4,483},{5,6},{6,5},{7,488},{8,487},{9... | collective-permute-start | bytes 393224 | tf_op jit(solution)/shard_map/ppermute | solution.py:431
  45.4 4.1 %collective-permute-done.5.refs_6_.rest_6_ = f32[16,16,128]{2,1,0:T(8,128)S(1)} collective-permute-done((f32[16,16,128]{2,1,0:T(8,128)S(1)}, f32[16,16,128]{2,1,0:T(8,128)S(1)}, u32[]{:S(2)}, u32[]{:S(2)}) %collective-permute-start.5) | collective-permute-done | bytes 131104 | tf_op jit(solution)/shard_map/ppermute | solution.py:431
  49.5 9.2 %collective-permute-start.6 = (f32[4,16,128]{2,1,0:T(8,128)S(1)}, f32[4,16,128]{2,1,0:T(8,128)S(1)}, u32[]{:S(2)}, u32[]{:S(2)}) collective-permute-start(f32[4,16,128]{2,1,0:T(8,128)S(1)} %shard_map.117), channel_id=1, source_target_pairs={{0,32},{1,33},{2,34},{3,35},{4,36},{5,37},{6,38},{7,39},{8,40},{9,... | collective-permute-start | bytes 98312 | tf_op jit(solution)/shard_map/ppermute | solution.py:431
  58.6 0.8 %collective-permute-done.6.refs_7_.rest_7_ = f32[4,16,128]{2,1,0:T(8,128)S(1)} collective-permute-done((f32[4,16,128]{2,1,0:T(8,128)S(1)}, f32[4,16,128]{2,1,0:T(8,128)S(1)}, u32[]{:S(2)}, u32[]{:S(2)}) %collective-permute-start.6) | collective-permute-done | bytes 32800 | tf_op jit(solution)/shard_map/ppermute | solution.py:431
  59.5 2.0 %collective-permute-start.7 = (f32[5,16,128]{2,1,0:T(8,128)S(1)}, f32[5,16,128]{2,1,0:T(8,128)S(1)}, u32[]{:S(2)}, u32[]{:S(2)}) collective-permute-start(f32[5,16,128]{2,1,0:T(8,128)S(1)} %shard_map.118), channel_id=1, source_target_pairs={{0,1},{1,0},{2,3},{3,2},{4,5},{5,4},{6,7},{7,6},{8,9},{9,8},{10,11... | collective-permute-start | bytes 122888 | tf_op jit(solution)/shard_map/ppermute | solution.py:431
  61.5 2.8 %collective-permute-done.7.rest_8_ = f32[5,16,128]{2,1,0:T(8,128)S(1)} collective-permute-done((f32[5,16,128]{2,1,0:T(8,128)S(1)}, f32[5,16,128]{2,1,0:T(8,128)S(1)}, u32[]{:S(2)}, u32[]{:S(2)}) %collective-permute-start.7) | collective-permute-done | bytes 40992 | tf_op jit(solution)/shard_map/ppermute | solution.py:431
  64.3 3.5 %shard_map.119 = (f32[3,8,128]{2,1,0:T(8,128)}, f32[3,8,128]{2,1,0:T(8,128)}, f32[3,8,128]{2,1,0:T(8,128)}, f32[3,8,128]{2,1,0:T(8,128)}) custom-call(f32[3,1,128]{2,1,0:T(1,128)S(1)} %bitcast.28, f32[1,128]{1,0:T(1,128)S(1)} %bitcast.30, f32[3,8,128]{2,1,0:T(8,128)S(1)} %bitcast.21, f32[3,8,128]{2,1,0:T(8,128)S(1)} %bitcast.23, ...), custom_call_target="tpu_custom_call" | custom-call | flops 1048576 | bytes 1176576 | tf_op jit(solution)/shard_map/pallas_call | solution.py:390
  (19 shorter events, 0.1 us)
Async XLA Ops:
  0.6 0.7 %copy-start = (f32[3,8,1,1,128]{4,3,2,1,0:T(1,128)S(1)}, f32[3,8,1,1,128]{4,3,2,1,0:T(1,128)}, u32[]{:S(2)}) copy-start(f32[3,8,1,1,128]{4,3,2,1,0:T(1,128)} %param.13) | copy-start | bytes 36868
  0.6 0.7 %copy-start.6 = (f32[3,1,1,128]{3,2,1,0:T(1,128)S(1)}, f32[3,1,1,128]{3,2,1,0:T(1,128)}, u32[]{:S(2)}) copy-start(f32[3,1,1,128]{3,2,1,0:T(1,128)} %param.8) | copy-start | bytes 4612
  0.7 0.7 %copy-start.7 = (f32[1,1,128]{2,1,0:T(1,128)S(1)}, f32[1,1,128]{2,1,0:T(1,128)}, u32[]{:S(2)}) copy-start(f32[1,1,128]{2,1,0:T(1,128)} %param.9) | copy-start | bytes 1540
  0.7 0.7 %copy-start.8 = (s32[1,1,32]{2,1,0:T(1,128)S(1)}, s32[1,1,32]{2,1,0:T(1,128)}, u32[]{:S(2)}) copy-start(s32[1,1,32]{2,1,0:T(1,128)} %param.10) | copy-start | bytes 388
  1.3 0.7 %copy-start.1 = (f32[3,8,1,1,128]{4,3,2,1,0:T(1,128)S(1)}, f32[3,8,1,1,128]{4,3,2,1,0:T(1,128)}, u32[]{:S(2)}) copy-start(f32[3,8,1,1,128]{4,3,2,1,0:T(1,128)} %param.15) | copy-start | bytes 36868
  2.1 0.8 %copy-start.3 = (s32[1,1,64,128]{3,2,1,0:T(8,128)S(1)}, s32[1,1,64,128]{3,2,1,0:T(8,128)}, u32[]{:S(2)}) copy-start(s32[1,1,64,128]{3,2,1,0:T(8,128)} %param.11) | copy-start | bytes 98308
  2.8 0.7 %copy-start.4 = (f32[3,8,1,1,128]{4,3,2,1,0:T(1,128)S(1)}, f32[3,8,1,1,128]{4,3,2,1,0:T(1,128)}, u32[]{:S(2)}) copy-start(f32[3,8,1,1,128]{4,3,2,1,0:T(1,128)} %param.12) | copy-start | bytes 36868
  3.5 0.7 %copy-start.5 = (f32[3,8,1,1,128]{4,3,2,1,0:T(1,128)S(1)}, f32[3,8,1,1,128]{4,3,2,1,0:T(1,128)}, u32[]{:S(2)}) copy-start(f32[3,8,1,1,128]{4,3,2,1,0:T(1,128)} %param.14) | copy-start | bytes 36868
  5.1 5.2 %collective-permute-start = (f32[3,16,128]{2,1,0:T(8,128)S(1)}, f32[3,16,128]{2,1,0:T(8,128)S(1)}, u32[]{:S(2)}, u32[]{:S(2)}) collective-permute-start(f32[3,16,128]{2,1,0:T(8,128)S(1)} %get-tuple-element.19.refs_0_.rest_0_), channel_id=1, source_target_pairs={{0,1},{1,0},{2,3},{3,2},{4,5},{5,4},{6,7},{7,6},{8,9},{9,8},{10,11... | collective-permute-start | bytes 73736 | tf_op jit(solution)/shard_map/ppermute | solution.py:431
  10.3 10.1 %collective-permute-start.1 = (f32[6,16,128]{2,1,0:T(8,128)S(1)}, f32[6,16,128]{2,1,0:T(8,128)S(1)}, u32[]{:S(2)}, u32[]{:S(2)}) collective-permute-start(f32[6,16,128]{2,1,0:T(8,128)S(1)} %shard_map.112), channel_id=1, source_target_pairs={{0,32},{1,33},{2,34},{3,35},{4,36},{5,37},{6,38},{7,39},{8,40},{9,... | collective-permute-start | bytes 147464 | tf_op jit(solution)/shard_map/ppermute | solution.py:431
  20.4 18.5 %collective-permute-start.2 = (f32[8,16,128]{2,1,0:T(8,128)S(1)}, f32[8,16,128]{2,1,0:T(8,128)S(1)}, u32[]{:S(2)}, u32[]{:S(2)}) collective-permute-start(f32[8,16,128]{2,1,0:T(8,128)S(1)} %shard_map.113), channel_id=1, source_target_pairs={{1,481},{2,482},{5,485},{6,486},{9,489},{10,490},{13,493},{14,494}... | collective-permute-start | bytes 196616 | tf_op jit(solution)/shard_map/ppermute | solution.py:431
  21.1 17.8 %collective-permute-start.3 = (f32[6,16,128]{2,1,0:T(8,128)S(1)}, f32[6,16,128]{2,1,0:T(8,128)S(1)}, u32[]{:S(2)}, u32[]{:S(2)}) collective-permute-start(f32[6,16,128]{2,1,0:T(8,128)S(1)} %shard_map.114), channel_id=1, source_target_pairs={{0,31},{3,4},{4,3},{7,8},{8,7},{11,12},{12,11},{15,16},{16,15},{19... | collective-permute-start | bytes 147464 | tf_op jit(solution)/shard_map/ppermute | solution.py:431
  38.9 4.2 %collective-permute-start.4 = (f32[4,16,128]{2,1,0:T(8,128)S(1)}, f32[4,16,128]{2,1,0:T(8,128)S(1)}, u32[]{:S(2)}, u32[]{:S(2)}) collective-permute-start(f32[4,16,128]{2,1,0:T(8,128)S(1)} %shard_map.115), channel_id=1, source_target_pairs={{0,32},{1,33},{2,34},{3,35},{4,36},{5,37},{6,38},{7,39},{8,40},{9,... | collective-permute-start | bytes 98312 | tf_op jit(solution)/shard_map/ppermute | solution.py:431
  43.2 6.3 %collective-permute-start.5 = (f32[16,16,128]{2,1,0:T(8,128)S(1)}, f32[16,16,128]{2,1,0:T(8,128)S(1)}, u32[]{:S(2)}, u32[]{:S(2)}) collective-permute-start(f32[16,16,128]{2,1,0:T(8,128)S(1)} %shard_map.116), channel_id=1, source_target_pairs={{0,511},{1,2},{2,1},{3,484},{4,483},{5,6},{6,5},{7,488},{8,487},{9... | collective-permute-start | bytes 393224 | tf_op jit(solution)/shard_map/ppermute | solution.py:431
  49.5 10.0 %collective-permute-start.6 = (f32[4,16,128]{2,1,0:T(8,128)S(1)}, f32[4,16,128]{2,1,0:T(8,128)S(1)}, u32[]{:S(2)}, u32[]{:S(2)}) collective-permute-start(f32[4,16,128]{2,1,0:T(8,128)S(1)} %shard_map.117), channel_id=1, source_target_pairs={{0,32},{1,33},{2,34},{3,35},{4,36},{5,37},{6,38},{7,39},{8,40},{9,... | collective-permute-start | bytes 98312 | tf_op jit(solution)/shard_map/ppermute | solution.py:431
  59.5 4.9 %copy-start.2 = (f32[3,8,1,1,128]{4,3,2,1,0:T(1,128)S(1)}, f32[3,8,1,1,128]{4,3,2,1,0:T(1,128)}, u32[]{:S(2)}) copy-start(f32[3,8,1,1,128]{4,3,2,1,0:T(1,128)} %param.15) | copy-start | bytes 36868
  59.5 4.9 %collective-permute-start.7 = (f32[5,16,128]{2,1,0:T(8,128)S(1)}, f32[5,16,128]{2,1,0:T(8,128)S(1)}, u32[]{:S(2)}, u32[]{:S(2)}) collective-permute-start(f32[5,16,128]{2,1,0:T(8,128)S(1)} %shard_map.118), channel_id=1, source_target_pairs={{0,1},{1,0},{2,3},{3,2},{4,5},{5,4},{6,7},{7,6},{8,9},{9,8},{10,11... | collective-permute-start | bytes 122888 | tf_op jit(solution)/shard_map/ppermute | solution.py:431

commit v3 on v2

--- a/solution.py
+++ b/solution.py
@@ -33,39 +33,33 @@
     def pair_y(x, y):
         return x, y ^ 1
 
-    def across_y(x, y):
-        return (x, other(y, ny)) if y % 4 in (0, 3) else None
-
-    def across_x(x, y):
-        return (other(x, nx), y) if y % 4 in (1, 2) else None
+    def across(x, y):
+        if x in (0, nx - 1):
+            return other(x, nx), y
+        return x, other(y, ny)
 
     def beside(x, y):
-        if y % 4 in (1, 2):
-            return x, other(y, ny)
-        if x in (0, nx - 1):
-            return other(x, nx), other(y, ny)
-        return other(x, nx), y
-
-    return (
-        (pair_y, -1),
-        (pair_x, 0),
-        (across_x, 1),
-        (across_y, 0),
-        (pair_x, 3),
-        (beside, 4),
-        (pair_x, 5),
-        (pair_y, 6),
-    )
+        if x not in (0, nx - 1):
+            return other(x, nx), y
+        return (x if y % 4 in (1, 2) else other(x, nx)), other(y, ny)
+
+    return pair_x, pair_y, across, beside, pair_x, pair_y
 
 
 def class_of(x, y, nx):
-    return 4 * (0 if x == 0 else 3 if x == nx - 1 else 1 + (x + 1) % 2) + y % 4
+    ends = {0: 0, 1: 1, nx - 2: 4, nx - 1: 5}
+    return 4 * ends.get(x, 2 + x % 2) + y % 4
 
 
 @functools.lru_cache(None)
 def make_plan(nx, ny):
     devices = [(x, y) for x in range(nx) for y in range(ny)]
     steps = routes(nx, ny)
+    source = [{f(*d): d for d in devices} for f in steps]
+    known, brought = {d: {d} for d in devices}, []
+    for i in range(len(steps)):
+        brought.append({d: known[source[i][d]] for d in devices})
+        known = {d: known[d] | brought[i][d] for d in devices}
 
     def wanted(x, y):
         return [
@@ -74,62 +68,55 @@
             for a, b in (WIDE if kind == 0 else RING)
         ]
 
-    known = [{d: {(k, *d) for k in range(KINDS)} for d in devices}]
-    for target, base in steps:
-        later = {d: set(known[-1][d]) for d in devices}
+    def route_of(item, d, before):
+        found = [i for i in range(before) if item[1:] in brought[i][d]]
+        late = item[0] and item[1] != d[0] and item[2] != d[1]
+        return found[-1 if late else 0]
+
+    sent = [{d: set() for d in devices} for _ in steps]
+
+    def ask(items, d, before):
+        for item in items:
+            if item[1:] != d:
+                i = route_of(item, d, before)
+                sent[i][d].add(item)
+
+    for d in devices:
+        ask(wanted(*d), d, len(steps))
+    for i in reversed(range(len(steps))):
         for d in devices:
-            if target(*d):
-                later[target(*d)] |= known[base + 1][d]
-        known.append(later)
-    first = {d: {} for d in devices}
-    for t, state in enumerate(known):
-        for d in devices:
-            for item in state[d]:
-                first[d].setdefault(item, t)
-    demand = {d: set(wanted(*d)) for d in devices}
-    assert all(demand[d] <= known[-1][d] for d in devices)
-    sent = [None] * len(steps)
-    for i in reversed(range(len(steps))):
-        target, base = steps[i]
-        sent[i] = {}
-        for d in devices:
-            t = target(*d)
-            if t is None:
-                sent[i][d] = []
-                continue
-            items = {m for m in demand[t] if first[t][m] == i + 1 and m in known[base + 1][d]}
-            near = lambda v, count: (v + count // 2) % count
-            sent[i][d] = sorted(
-                items, key=lambda m: (m[0], near(m[1] - t[0], nx), near(m[2] - t[1], ny))
-            )
-        for d in devices:
-            demand[d] |= set(sent[i][d])
-    sizes = [max(1, *(len(v) for v in s.values())) for s in sent]
+            ask(sent[i][d], source[i][d], i)
+
+    def order(d):
+        near = lambda v, count: (v + count // 2) % count
+        return lambda m: (m[0], near(m[1] - d[0], nx), near(m[2] - d[1], ny))
+
+    lists = [{d: sorted(s[d], key=order(d)) for d in devices} for s in sent]
+    sizes = [max(1, *map(len, s.values())) for s in lists]
     starts = [KINDS + sum(sizes[:i]) for i in range(len(sizes))]
-    place = {d: {(k, *d): k for k in range(KINDS)} for d in devices}
-    for i, (target, _) in enumerate(steps):
-        for d in devices:
-            for j, item in enumerate(sent[i][d]):
-                place[target(*d)].setdefault(item, starts[i] + j)
+
+    def place(item, d, before):
+        if item[1:] == d:
+            return item[0]
+        i = route_of(item, d, before)
+        return starts[i] + lists[i][d].index(item)
+
     send_rows = [{} for _ in steps]
     last_rows = {}
     for d in devices:
         c = class_of(*d, nx)
-        for i in range(len(steps)):
-            row = tuple(place[d][item] for item in sent[i][d])
+        for i, f in enumerate(steps):
+            row = tuple(place(item, d, i) for item in lists[i][f(*d)])
             assert send_rows[i].setdefault(c, row) == row
-        row = tuple(place[d][item] for item in wanted(*d))
+        row = tuple(place(item, d, len(steps)) for item in wanted(*d))
         assert last_rows.setdefault(c, row) == row
-    links = [
-        [(x * ny + y, t[0] * ny + t[1]) for x, y in devices for t in [f(x, y)] if t]
-        for f, _ in steps
-    ]
+    links = [[(x * ny + y, f(x, y)[0] * ny + f(x, y)[1]) for x, y in devices] for f in steps]
     return steps, sizes, starts, send_rows, last_rows, links
 
 
 def for_each_row(rows, nx, body):
     x, y = lax.axis_index("gx"), lax.axis_index("gy")
-    column = jnp.where(x == 0, 0, jnp.where(x == nx - 1, 3, 1 + lax.rem(x + 1, 2)))
+    column = jnp.where(x < 2, x, jnp.where(x < nx - 2, 2 + lax.rem(x, 2), x + 6 - nx))
     mine = 4 * column + lax.rem(y, 4)
     classes = {}
     for c, row in rows.items():
@@ -240,14 +227,26 @@
     return [jnp.broadcast_to(r, (G, A)) for r in rows]
 
 
-def own_kernel(pos, spring, border, entries, vec, heat, vec0, heat0,
-               payload, w_high, w_low, partial, self_out, counts):
+def own_kernel(*refs):
+    inputs, outputs, buffers, arrived = refs[:8], refs[8:16], refs[16:24], refs[24]
+    payload, w_high, w_low, partial, self_out, counts, state, place = outputs
+    copies = [
+        pltpu.make_async_copy(source, target, arrived.at[i])
+        for i, (source, target) in enumerate(zip(inputs, buffers))
+    ]
+    for copy in copies:
+        copy.start()
+    entries, pos, spring, border, vec, heat, vec0, heat0 = buffers
+    copies[0].wait()
     counters = count_slots(entries[...], FAR_GROUPS + [16, 17, 18, 19])
     for i in range(8):
         counts[i] = counters[i]
+    for copy in copies[1:]:
+        copy.wait()
     root = jnp.sqrt(spring[...])
     home = spread([pos[0], pos[1], pos[2], root])
-    geo = jnp.concatenate([pos[0], pos[1], pos[2], root, jnp.zeros((4, A), F32)], axis=0).T
+    place[...] = jnp.concatenate([pos[0], pos[1], pos[2], root, jnp.zeros((4, A), F32)], axis=0)
+    geo = place[...].T
     sums = {}
     for t in range(4):
         source = spread([geo[t * G : (t + 1) * G, c : c + 1] for c in range(4)])
@@ -263,6 +262,7 @@
         inner = self_product(own_terms, current, a) - far[:, a * A : (a + 1) * A] - current[a]
         begun.append(2.0 * inner - previous[a])
         partial[a] = begun[a]
+        state[a] = current[a]
     geometry = jnp.concatenate(
         [pos[0], pos[1], pos[2], spring[...], jnp.zeros((F - 4, A), F32)], axis=0
     )
@@ -278,7 +278,7 @@
     return pltpu.roll(block, shift, 1) if shift else block
 
 
-def last_kernel(rows, starts, nx, n_in, pos, spring, vec, heat, partial, self_in, counts,
+def last_kernel(rows, starts, nx, n_in, place, state, partial, self_in, counts,
                 own_high, own_low, *rest):
     received = rest[:n_in]
     v2, h2, v3, h3, pool, far_high, far_low, edge_high, edge_low = rest[n_in:]
@@ -313,7 +313,7 @@
         begun = [by_group([moved(x, b, g) for g, x in enumerate(blocks[0])]) for b in range(3)]
         sides.append((quad, fields, begun, blocks))
 
-    home = spread([pos[0], pos[1], pos[2], jnp.sqrt(spring[...])])
+    home = spread([place[c : c + 1, :] for c in range(4)])
     sums = {}
     for j, s in enumerate(RING):
         terms = pair_terms(counts[j], shifted(wide_geo[s], s), home)
@@ -323,7 +323,7 @@
     def beside(first, second):
         return jnp.concatenate([x for b in range(3) for x in (first[b], second[b])], axis=1)
 
-    current = stacked(vec, heat)
+    current = [state[b] for b in range(3)]
     far = apply_weights(far_high, far_low, beside(sides[0][1], sides[1][1]))
     second = []
     for a in range(3):
@@ -385,12 +385,14 @@
         h3[a] = third[8:]
 
 
-def call(kernel, out_shape, args, scratch=()):
+def call(kernel, name, out_shape, args, scratch=(), space=pltpu.VMEM):
     size = sum(x.size * x.dtype.itemsize for x in (*args, *out_shape))
     return pl.pallas_call(
         kernel,
         out_shape=out_shape,
+        in_specs=[pl.BlockSpec(memory_space=space)] * len(args),
         scratch_shapes=scratch,
+        name=name,
         cost_estimate=pl.CostEstimate(flops=2**20, bytes_accessed=size, transcendentals=0),
         compiler_params=pltpu.CompilerParams(vmem_limit_bytes=24 * 2**20),
     )(*args)
@@ -405,8 +407,13 @@
     stiff = spring.reshape(1, A)
     entries = neighbours.reshape(NB, A)
     v0, v1, h0, h1 = (x.reshape(3, 8, A) for x in (vec_prev, vec_now, heat_prev, heat_now))
-    payload, own_high, own_low, partial, self_terms, counts = call(
+    first = [
+        pltpu.with_memory_space_constraint(x, pltpu.HBM)
+        for x in (entries, pos, stiff, border.reshape(1, G), v1, h1, v0, h0)
+    ]
+    payload, own_high, own_low, partial, self_terms, counts, state, place = call(
         own_kernel,
+        "own_kernel",
         (
             shape((KINDS, F, A), F32),
             shape((OWN, OWN), BF16),
@@ -414,25 +421,30 @@
             shape((3, F, A), F32),
             shape((6, A), F32),
             shape((8, 8, A), jnp.int32),
+            shape((3, F, A), F32),
+            shape((8, A), F32),
         ),
-        (pos, stiff, border.reshape(1, G), entries, v1, h1, v0, h0),
+        first,
+        [pltpu.VMEM(x.shape, x.dtype) for x in first] + [pltpu.SemaphoreType.DMA((8,))],
+        pltpu.HBM,
     )
     received = [payload]
-    for i, (_, base) in enumerate(steps):
-        known = received[: base + 2]
+    for i in range(len(steps)):
         if send_rows[i][0] == tuple(range(KINDS)) and len(set(send_rows[i].values())) == 1:
             outgoing = payload
         else:
             (outgoing,) = call(
                 functools.partial(relay_kernel, send_rows[i], starts, nx),
+                f"relay_{i}",
                 (shape((sizes[i], F, A), F32),),
-                known,
+                received,
             )
         received.append(lax.ppermute(outgoing, ("gx", "gy"), links[i]))
     v2, h2, v3, h3 = call(
         functools.partial(last_kernel, last_rows, starts, nx, len(received)),
+        "last_kernel",
         (vector,) * 4,
-        (pos, stiff, v1, h1, partial, self_terms, counts, own_high, own_low, *received),
+        (place, state, partial, self_terms, counts, own_high, own_low, *received),
         (
             pltpu.VMEM((len(WIDE) + 16, F, A), F32),
             pltpu.VMEM((6 * A, OWN), BF16),

time: 68.4 us -> 53.5 us (0.78)
  starting transfers between devices: 45.5 us -> 33.7 us
  local copies, waits for them, and re-layouts: 3.56 us -> 0 us
  Pallas kernels: 4.43 us -> 5.36 us
    ppermute x8 -> x6, starting transfers between devices: 45.5 us -> 33.7 us  [shards(): received.append(lax.ppermute(outgoing, ('gx', 'gy'), links[i]))]
    unnamed x18 -> x0, local copies, waits for them, and re-layouts: 3.56 us -> none
    pallas_call x9 -> x7, Pallas kernels: 4.43 us -> 5.36 us  [call(): pl.pallas_call(kernel, out_shape=out_shape, in_specs=[pl.BlockSpec(memory...]
    ppermute x8 -> x6, waiting for transfers between devices: 13.6 us -> 13.4 us  [shards(): received.append(lax.ppermute(outgoing, ('gx', 'gy'), links[i]))]
  transfers between devices with their start and end apart: 8 -> 6, of which waited for: 7 -> 6; matrix products, arithmetic and copies ran while one was open for 0% -> 0% of each run, Pallas kernels for 0% -> 0%
where the time goes in v3:
time: 53.5 us; the launch traced here: 53.2 us
  starting transfers between devices  33.7 us (63%)
  waiting for transfers between devices  13.4 us (25%)
  Pallas kernels  5.36 us (10%)
  between operations  0.7 us (1%)
    ppermute x6, starting transfers between devices, shards(): received.append(lax.ppermute(outgoing, ('gx', 'gy'), links[i]))  33.7 us
    ppermute x6, waiting for transfers between devices, shards(): received.append(lax.ppermute(outgoing, ('gx', 'gy'), links[i]))  13.4 us
    pallas_call x7, Pallas kernels, call(): pl.pallas_call(kernel, out_shape=out_shape, in_specs=[pl.BlockSpec(memory...  5.36 us
  transfers between devices with their start and end apart: 6, of which 6 were waited for; matrix products, arithmetic and copies ran while one was open for 0% of the time, Pallas kernels for 0%

profile of v3, /device:TPU:1, one launch (start us, length us, event | category | flops | bytes accessed | tf_op | source)
XLA Modules:
  0.0 53.2 jit_solution(6346759291324724656)
XLA Ops:
  0.6 1.8 %own_kernel.1 = (f32[3,16,128]{2,1,0:T(8,128)S(1)}, bf16[384,384]{1,0:T(8,128)(2,1)S(1)}, bf16[384,384]{1,0:T(8,128)(2,1)S(1)}, f32[3,16,128]{2,1,0:T(8,128)S(1)...) custom-call(s32[64,128]{1,0:T(8,128)} %bitcast.20, ...), custom_call_target="tpu_custom_call" | custom-call | flops 1048576 | bytes 787584 | tf_op jit(solution)/shard_map/own_kernel/pallas_call | solution.py:390
  2.5 8.7 %collective-permute-start = (f32[3,16,128]{2,1,0:T(8,128)S(1)}, f32[3,16,128]{2,1,0:T(8,128)S(1)}, u32[]{:S(2)}, u32[]{:S(2)}) collective-permute-start(f32[3,16,128]{2,1,0:T(8,128)S(1)} %get-tuple-element.23.refs_0_.rest_0_), channel_id=1, source_target_pairs={{0,32},{1,33},{2,34},{3,35},{4,36},{5,37},{6,38},{7,39},{8,40},{9,... | collective-permute-start | bytes 73736 | tf_op jit(solution)/shard_map/ppermute | solution.py:442
  11.2 0.8 %collective-permute-done.refs_1_.rest_1_ = f32[3,16,128]{2,1,0:T(8,128)S(1)} collective-permute-done((f32[3,16,128]{2,1,0:T(8,128)S(1)}, f32[3,16,128]{2,1,0:T(8,128)S(1)}, u32[]{:S(2)}, u32[]{:S(2)}) %collective-permute-start) | collective-permute-done | bytes 24608 | tf_op jit(solution)/shard_map/ppermute | solution.py:442
  12.1 1.9 %collective-permute-start.1 = (f32[4,16,128]{2,1,0:T(8,128)S(1)}, f32[4,16,128]{2,1,0:T(8,128)S(1)}, u32[]{:S(2)}, u32[]{:S(2)}) collective-permute-start(f32[4,16,128]{2,1,0:T(8,128)S(1)} %relay_1.1), channel_id=1, source_target_pairs={{0,1},{1,0},{2,3},{3,2},{4,5},{5,4},{6,7},{7,6},{8,9},{9,8},{10,11... | collective-permute-start | bytes 98312 | tf_op jit(solution)/shard_map/ppermute | solution.py:442
  14.0 2.7 %collective-permute-done.1.refs_2_.rest_2_ = f32[4,16,128]{2,1,0:T(8,128)S(1)} collective-permute-done((f32[4,16,128]{2,1,0:T(8,128)S(1)}, f32[4,16,128]{2,1,0:T(8,128)S(1)}, u32[]{:S(2)}, u32[]{:S(2)}) %collective-permute-start.1) | collective-permute-done | bytes 32800 | tf_op jit(solution)/shard_map/ppermute | solution.py:442
  16.7 14.7 %collective-permute-start.2 = (f32[6,16,128]{2,1,0:T(8,128)S(1)}, f32[6,16,128]{2,1,0:T(8,128)S(1)}, u32[]{:S(2)}, u32[]{:S(2)}) collective-permute-start(f32[6,16,128]{2,1,0:T(8,128)S(1)} %relay_2.1), channel_id=1, source_target_pairs={{0,480},{1,481},{2,482},{3,483},{4,484},{5,485},{6,486},{7,487},{8... | collective-permute-start | bytes 147464 | tf_op jit(solution)/shard_map/ppermute | solution.py:442
  31.5 3.0 %collective-permute-done.2.refs_3_.rest_3_ = f32[6,16,128]{2,1,0:T(8,128)S(1)} collective-permute-done((f32[6,16,128]{2,1,0:T(8,128)S(1)}, f32[6,16,128]{2,1,0:T(8,128)S(1)}, u32[]{:S(2)}, u32[]{:S(2)}) %collective-permute-start.2) | collective-permute-done | bytes 49184 | tf_op jit(solution)/shard_map/ppermute | solution.py:442
  34.5 3.4 %collective-permute-start.3 = (f32[12,16,128]{2,1,0:T(8,128)S(1)}, f32[12,16,128]{2,1,0:T(8,128)S(1)}, u32[]{:S(2)}, u32[]{:S(2)}) collective-permute-start(f32[12,16,128]{2,1,0:T(8,128)S(1)} %relay_3.1), channel_id=1, source_target_pairs={{0,511},{1,2},{2,1},{3,484},{4,483},{5,6},{6,5},{7,488},{8,487},{9... | collective-permute-start | bytes 294920 | tf_op jit(solution)/shard_map/ppermute | solution.py:442
  37.9 2.8 %collective-permute-done.3.refs_4_.rest_4_ = f32[12,16,128]{2,1,0:T(8,128)S(1)} collective-permute-done((f32[12,16,128]{2,1,0:T(8,128)S(1)}, f32[12,16,128]{2,1,0:T(8,128)S(1)}, u32[]{:S(2)}, u32[]{:S(2)}) %collective-permute-start.3) | collective-permute-done | bytes 98336 | tf_op jit(solution)/shard_map/ppermute | solution.py:442
  40.7 3.0 %collective-permute-start.4 = (f32[6,16,128]{2,1,0:T(8,128)S(1)}, f32[6,16,128]{2,1,0:T(8,128)S(1)}, u32[]{:S(2)}, u32[]{:S(2)}) collective-permute-start(f32[6,16,128]{2,1,0:T(8,128)S(1)} %relay_4.1), channel_id=1, source_target_pairs={{0,32},{1,33},{2,34},{3,35},{4,36},{5,37},{6,38},{7,39},{8,40},{9,... | collective-permute-start | bytes 147464 | tf_op jit(solution)/shard_map/ppermute | solution.py:442
  43.8 0.9 %collective-permute-done.4.refs_5_.rest_5_ = f32[6,16,128]{2,1,0:T(8,128)S(1)} collective-permute-done((f32[6,16,128]{2,1,0:T(8,128)S(1)}, f32[6,16,128]{2,1,0:T(8,128)S(1)}, u32[]{:S(2)}, u32[]{:S(2)}) %collective-permute-start.4) | collective-permute-done | bytes 49184 | tf_op jit(solution)/shard_map/ppermute | solution.py:442
  44.6 1.9 %collective-permute-start.5 = (f32[9,16,128]{2,1,0:T(8,128)S(1)}, f32[9,16,128]{2,1,0:T(8,128)S(1)}, u32[]{:S(2)}, u32[]{:S(2)}) collective-permute-start(f32[9,16,128]{2,1,0:T(8,128)S(1)} %relay_5.1), channel_id=1, source_target_pairs={{0,1},{1,0},{2,3},{3,2},{4,5},{5,4},{6,7},{7,6},{8,9},{9,8},{10,11... | collective-permute-start | bytes 221192 | tf_op jit(solution)/shard_map/ppermute | solution.py:442
  46.5 3.2 %collective-permute-done.5.rest_6_ = f32[9,16,128]{2,1,0:T(8,128)S(1)} collective-permute-done((f32[9,16,128]{2,1,0:T(8,128)S(1)}, f32[9,16,128]{2,1,0:T(8,128)S(1)}, u32[]{:S(2)}, u32[]{:S(2)}) %collective-permute-start.5) | collective-permute-done | bytes 73760 | tf_op jit(solution)/shard_map/ppermute | solution.py:442
  49.7 3.5 %last_kernel.1 = (f32[3,8,128]{2,1,0:T(8,128)}, f32[3,8,128]{2,1,0:T(8,128)}, f32[3,8,128]{2,1,0:T(8,128)}, f32[3,8,128]{2,1,0:T(8,128)}) custom-call(f32[8,128]{1,0:T(8,128)S(1)} %get-tuple-element.16.place, f32[3,16,128]{2,1,0:T(8,128)S(1)} %get-tuple-element.17.state, f32[3,16,128]{2,1,0:T(8,128)S(1)} %get-tuple-element.18.partial, ...), custom_call_target="tpu_custom_call" | custom-call | flops 1048576 | bytes 1080320 | tf_op jit(solution)/shard_map/last_kernel/pallas_call | solution.py:390
  (5 shorter events, 0.0 us)
Async XLA Ops:
  2.5 9.6 %collective-permute-start = (f32[3,16,128]{2,1,0:T(8,128)S(1)}, f32[3,16,128]{2,1,0:T(8,128)S(1)}, u32[]{:S(2)}, u32[]{:S(2)}) collective-permute-start(f32[3,16,128]{2,1,0:T(8,128)S(1)} %get-tuple-element.23.refs_0_.rest_0_), channel_id=1, source_target_pairs={{0,32},{1,33},{2,34},{3,35},{4,36},{5,37},{6,38},{7,39},{8,40},{9,... | collective-permute-start | bytes 73736 | tf_op jit(solution)/shard_map/ppermute | solution.py:442
  12.1 4.6 %collective-permute-start.1 = (f32[4,16,128]{2,1,0:T(8,128)S(1)}, f32[4,16,128]{2,1,0:T(8,128)S(1)}, u32[]{:S(2)}, u32[]{:S(2)}) collective-permute-start(f32[4,16,128]{2,1,0:T(8,128)S(1)} %relay_1.1), channel_id=1, source_target_pairs={{0,1},{1,0},{2,3},{3,2},{4,5},{5,4},{6,7},{7,6},{8,9},{9,8},{10,11... | collective-permute-start | bytes 98312 | tf_op jit(solution)/shard_map/ppermute | solution.py:442
  16.7 17.8 %collective-permute-start.2 = (f32[6,16,128]{2,1,0:T(8,128)S(1)}, f32[6,16,128]{2,1,0:T(8,128)S(1)}, u32[]{:S(2)}, u32[]{:S(2)}) collective-permute-start(f32[6,16,128]{2,1,0:T(8,128)S(1)} %relay_2.1), channel_id=1, source_target_pairs={{0,480},{1,481},{2,482},{3,483},{4,484},{5,485},{6,486},{7,487},{8... | collective-permute-start | bytes 147464 | tf_op jit(solution)/shard_map/ppermute | solution.py:442
  34.5 6.2 %collective-permute-start.3 = (f32[12,16,128]{2,1,0:T(8,128)S(1)}, f32[12,16,128]{2,1,0:T(8,128)S(1)}, u32[]{:S(2)}, u32[]{:S(2)}) collective-permute-start(f32[12,16,128]{2,1,0:T(8,128)S(1)} %relay_3.1), channel_id=1, source_target_pairs={{0,511},{1,2},{2,1},{3,484},{4,483},{5,6},{6,5},{7,488},{8,487},{9... | collective-permute-start | bytes 294920 | tf_op jit(solution)/shard_map/ppermute | solution.py:442
  40.7 3.9 %collective-permute-start.4 = (f32[6,16,128]{2,1,0:T(8,128)S(1)}, f32[6,16,128]{2,1,0:T(8,128)S(1)}, u32[]{:S(2)}, u32[]{:S(2)}) collective-permute-start(f32[6,16,128]{2,1,0:T(8,128)S(1)} %relay_4.1), channel_id=1, source_target_pairs={{0,32},{1,33},{2,34},{3,35},{4,36},{5,37},{6,38},{7,39},{8,40},{9,... | collective-permute-start | bytes 147464 | tf_op jit(solution)/shard_map/ppermute | solution.py:442
  44.6 5.1 %collective-permute-start.5 = (f32[9,16,128]{2,1,0:T(8,128)S(1)}, f32[9,16,128]{2,1,0:T(8,128)S(1)}, u32[]{:S(2)}, u32[]{:S(2)}) collective-permute-start(f32[9,16,128]{2,1,0:T(8,128)S(1)} %relay_5.1), channel_id=1, source_target_pairs={{0,1},{1,0},{2,3},{3,2},{4,5},{5,4},{6,7},{7,6},{8,9},{9,8},{10,11... | collective-permute-start | bytes 221192 | tf_op jit(solution)/shard_map/ppermute | solution.py:442

commit v4 on v3

--- a/solution.py
+++ b/solution.py
@@ -102,7 +102,7 @@
         return starts[i] + lists[i][d].index(item)
 
     send_rows = [{} for _ in steps]
-    last_rows = {}
+    last_rows, next_rows = {}, {}
     for d in devices:
         c = class_of(*d, nx)
         for i, f in enumerate(steps):
@@ -110,8 +110,10 @@
             assert send_rows[i].setdefault(c, row) == row
         row = tuple(place(item, d, len(steps)) for item in wanted(*d))
         assert last_rows.setdefault(c, row) == row
+        row = tuple(row[WIDE.index(s)] for s in RING)
+        assert max(row) < starts[-1] and next_rows.setdefault(c, row) == row
     links = [[(x * ny + y, f(x, y)[0] * ny + f(x, y)[1]) for x, y in devices] for f in steps]
-    return steps, sizes, starts, send_rows, last_rows, links
+    return steps, sizes, starts, send_rows, next_rows, last_rows, links
 
 
 def for_each_row(rows, nx, body):
@@ -278,65 +280,83 @@
     return pltpu.roll(block, shift, 1) if shift else block
 
 
-def last_kernel(rows, starts, nx, n_in, place, state, partial, self_in, counts,
-                own_high, own_low, *rest):
-    received = rest[:n_in]
-    v2, h2, v3, h3, pool, far_high, far_low, edge_high, edge_low = rest[n_in:]
-
+def geometry_of(values):
+    rows = [v[0:4] for v in values.values()]
+    rows.append(jnp.zeros((A - 4 * len(values), A), F32))
+    geo = jnp.concatenate(rows, axis=0).T[3 * G :]
+    out = {}
+    for j, s in enumerate(values):
+        cols = [geo[:, 4 * j + c : 4 * j + c + 1] for c in range(4)]
+        out[s] = spread(cols[:3] + [jnp.sqrt(cols[3])])
+    return out
+
+
+def shifted(cols, s):
+    return [cols[0] + column_edge * s[0], cols[1] + column_edge * s[1], cols[2], cols[3]]
+
+
+def fill_pool(rows, starts, nx, received, pool):
     def body(row):
         for j, place in enumerate(row):
             pool[j] = block_at(received, starts, place)
 
     for_each_row(rows, nx, body)
-    values = {s: pool[j] for j, s in enumerate(WIDE)}
-    halves = {s: split(x) for s, x in values.items()}
-    geo = jnp.concatenate(
-        [values[s][0:4] for s in WIDE] + [jnp.zeros((A - 4 * len(WIDE), A), F32)], axis=0
-    ).T[3 * G :]
-    geo = {
-        s: [
-            jnp.sqrt(geo[:, 4 * j + c : 4 * j + c + 1]) if c == 3 else geo[:, 4 * j + c : 4 * j + c + 1]
-            for c in range(4)
-        ]
-        for j, s in enumerate(WIDE)
-    }
-    wide_geo = {s: spread(x) for s, x in geo.items()}
-
-    def shifted(cols, s):
-        return [cols[0] + column_edge * s[0], cols[1] + column_edge * s[1], cols[2], cols[3]]
-
-    quads = (RING[:4], RING[4:])
-    sides = []
-    for q, quad in enumerate(quads):
-        blocks = [[pool[len(WIDE) + k * 8 + 4 * q + g] for g in range(4)] for k in range(2)]
-        fields = [by_group([moved(values[s], b, g) for g, s in enumerate(quad)]) for b in range(3)]
-        begun = [by_group([moved(x, b, g) for g, x in enumerate(blocks[0])]) for b in range(3)]
-        sides.append((quad, fields, begun, blocks))
-
+
+
+QUADS = (RING[:4], RING[4:])
+
+
+def side_fields(values):
+    return [
+        [by_group([moved(values[s], b, g) for g, s in enumerate(quad)]) for b in range(3)]
+        for quad in QUADS
+    ]
+
+
+def woven(first, second):
+    return jnp.concatenate([x for b in range(3) for x in (first[b], second[b])], axis=1)
+
+
+def next_kernel(rows, starts, nx, n_in, place, state, partial, self_in, counts,
+                own_high, own_low, *rest):
+    v2, h2, begun, far_high, far_low, pool = rest[n_in:]
+    fill_pool(rows, starts, nx, rest[:n_in], pool)
+    values = {s: pool[j] for j, s in enumerate(RING)}
+    geo = geometry_of(values)
     home = spread([place[c : c + 1, :] for c in range(4)])
     sums = {}
     for j, s in enumerate(RING):
-        terms = pair_terms(counts[j], shifted(wide_geo[s], s), home)
+        terms = pair_terms(counts[j], shifted(geo[s], s), home)
         put_terms(far_high, far_low, sums, [b * 2 * A + j * G for b in range(3)], terms)
     far_terms = total(sums)
-
-    def beside(first, second):
-        return jnp.concatenate([x for b in range(3) for x in (first[b], second[b])], axis=1)
-
     current = [state[b] for b in range(3)]
-    far = apply_weights(far_high, far_low, beside(sides[0][1], sides[1][1]))
+    far = apply_weights(far_high, far_low, woven(*side_fields(values)))
     second = []
     for a in range(3):
         inner = self_product(far_terms, current, a) - far[:, a * A : (a + 1) * A]
         second.append(partial[a] + 2.0 * inner)
         v2[a] = second[a][:8]
         h2[a] = second[a][8:]
-
+    all_terms = {key: far_terms[key] + self_in[i : i + 1, :] for i, key in enumerate(KEYS)}
+    far = apply_weights(own_high, own_low, jnp.concatenate(second, axis=1))
+    for a in range(3):
+        inner = self_product(all_terms, second, a) - far[:, a * A : (a + 1) * A] - second[a]
+        begun[a] = 2.0 * inner - current[a]
+
+
+def last_kernel(rows, starts, nx, n_in, third, far_high, far_low, *rest):
+    v3, h3, pool, edge_high, edge_low = rest[n_in:]
+    fill_pool(rows, starts, nx, rest[:n_in], pool)
+    values = {s: pool[j] for j, s in enumerate(WIDE)}
+    halves = {s: split(x) for s, x in values.items()}
+    geo = geometry_of(values)
     for j in range(len(RING)):
         edge_high[j * A + 3 * G : (j + 1) * A, :] = jnp.zeros((G, OWN), BF16)
         edge_low[j * A + 3 * G : (j + 1) * A, :] = jnp.zeros((G, OWN), BF16)
     edges = []
-    for quad, fields, begun, blocks in sides:
+    for q, (quad, fields) in enumerate(zip(QUADS, side_fields(values))):
+        blocks = [[pool[len(WIDE) + k * 8 + 4 * q + g] for g in range(4)] for k in range(2)]
+        begun = [by_group([moved(x, b, g) for g, x in enumerate(blocks[0])]) for b in range(3)]
         lists = [
             by_group([moved(blocks[1 if k < 3 else 0][g], k, g) for g in range(4)]) for k in range(4)
         ]
@@ -346,7 +366,7 @@
         sums = {}
         for j, s in enumerate(RING):
             around = [(t[0] + s[0], t[1] + s[1]) for t in quad]
-            source = [by_group([wide_geo[t][c] for t in around]) for c in range(4)]
+            source = [by_group([geo[t][c] for t in around]) for c in range(4)]
             terms = pair_terms(counters[j], shifted(source, s), home)
             put_terms(edge_high, edge_low, sums, [j * A + b * G for b in range(3)], terms)
         terms = total(sums)
@@ -374,15 +394,11 @@
             inner = self_product(terms, fields, a) - by_group(sums_of)
             result.append(begun[a] + 2.0 * inner)
         edges.append(result)
-
-    all_terms = {key: far_terms[key] + self_in[i : i + 1, :] for i, key in enumerate(KEYS)}
-    far = apply_weights(far_high, far_low, beside(*edges))
-    far += apply_weights(own_high, own_low, jnp.concatenate(second, axis=1))
+    far = apply_weights(far_high, far_low, woven(*edges))
     for a in range(3):
-        inner = self_product(all_terms, second, a) - far[:, a * A : (a + 1) * A] - second[a]
-        third = 2.0 * inner - current[a]
-        v3[a] = third[:8]
-        h3[a] = third[8:]
+        result = third[a] - 2.0 * far[:, a * A : (a + 1) * A]
+        v3[a] = result[:8]
+        h3[a] = result[8:]
 
 
 def call(kernel, name, out_shape, args, scratch=(), space=pltpu.VMEM):
@@ -400,7 +416,7 @@
 
 def shards(positions, spring, border, neighbours, vec_prev, vec_now, heat_prev, heat_now):
     nx, ny = lax.axis_size("gx"), lax.axis_size("gy")
-    steps, sizes, starts, send_rows, last_rows, links = make_plan(nx, ny)
+    steps, sizes, starts, send_rows, next_rows, last_rows, links = make_plan(nx, ny)
     shape = jax.ShapeDtypeStruct
     vector = shape((3, 8, A), F32)
     pos = positions.reshape(3, 1, A)
@@ -440,15 +456,27 @@
                 received,
             )
         received.append(lax.ppermute(outgoing, ("gx", "gy"), links[i]))
-    v2, h2, v3, h3 = call(
+    early = received[:-1]
+    v2, h2, third, far_high, far_low = call(
+        functools.partial(next_kernel, next_rows, starts, nx, len(early)),
+        "next_kernel",
+        (
+            vector,
+            vector,
+            shape((3, F, A), F32),
+            shape((6 * A, OWN), BF16),
+            shape((6 * A, OWN), BF16),
+        ),
+        (place, state, partial, self_terms, counts, own_high, own_low, *early),
+        (pltpu.VMEM((len(RING), F, A), F32),),
+    )
+    v3, h3 = call(
         functools.partial(last_kernel, last_rows, starts, nx, len(received)),
         "last_kernel",
-        (vector,) * 4,
-        (place, state, partial, self_terms, counts, own_high, own_low, *received),
+        (vector, vector),
+        (third, far_high, far_low, *received),
         (
             pltpu.VMEM((len(WIDE) + 16, F, A), F32),
-            pltpu.VMEM((6 * A, OWN), BF16),
-            pltpu.VMEM((6 * A, OWN), BF16),
             pltpu.VMEM((8 * A, OWN), BF16),
             pltpu.VMEM((8 * A, OWN), BF16),
         ),

time: 53.5 us -> 53.1 us (level)
  waiting for transfers between devices: 13.4 us -> 11.8 us
  Pallas kernels: 5.36 us -> 6.55 us
    ppermute x6, waiting for transfers between devices: 13.4 us -> 11.8 us  [shards(): received.append(lax.ppermute(outgoing, ('gx', 'gy'), links[i]))]
    pallas_call x7 -> x8, Pallas kernels: 5.36 us -> 6.55 us  [call(): pl.pallas_call(kernel, out_shape=out_shape, in_specs=[pl.BlockSpec(memory...]
  transfers between devices with their start and end apart: 6 -> 6, of which waited for: 6 -> 6; matrix products, arithmetic and copies ran while one was open for 0% -> 0% of each run, Pallas kernels for 0% -> 3%
where the time goes in v4:
time: 53.1 us; the launch traced here: 52.8 us
  starting transfers between devices  33.7 us (63%)
  waiting for transfers between devices  11.8 us (22%)
  Pallas kernels  6.55 us (12%)
  between operations  0.7 us (1%)
    ppermute x6, starting transfers between devices, shards(): received.append(lax.ppermute(outgoing, ('gx', 'gy'), links[i]))  33.7 us
    ppermute x6, waiting for transfers between devices, shards(): received.append(lax.ppermute(outgoing, ('gx', 'gy'), links[i]))  11.8 us
    pallas_call x8, Pallas kernels, call(): pl.pallas_call(kernel, out_shape=out_shape, in_specs=[pl.BlockSpec(memory...  6.55 us
  transfers between devices with their start and end apart: 6, of which 6 were waited for; matrix products, arithmetic and copies ran while one was open for 0% of the time, Pallas kernels for 3%

profile of v4, /device:TPU:1, one launch (start us, length us, event | category | flops | bytes accessed | tf_op | source)
XLA Modules:
  0.0 52.8 jit_solution(16692410950953187533)
XLA Ops:
  0.6 1.8 %own_kernel.1 = (f32[3,16,128]{2,1,0:T(8,128)S(1)}, bf16[384,384]{1,0:T(8,128)(2,1)S(1)}, bf16[384,384]{1,0:T(8,128)(2,1)S(1)}, f32[3,16,128]{2,1,0:T(8,128)S(1)...) custom-call(s32[64,128]{1,0:T(8,128)} %bitcast.20, ...), custom_call_target="tpu_custom_call" | custom-call | flops 1048576 | bytes 787584 | tf_op jit(solution)/shard_map/own_kernel/pallas_call | solution.py:406
  2.5 8.7 %collective-permute-start = (f32[3,16,128]{2,1,0:T(8,128)S(1)}, f32[3,16,128]{2,1,0:T(8,128)S(1)}, u32[]{:S(2)}, u32[]{:S(2)}) collective-permute-start(f32[3,16,128]{2,1,0:T(8,128)S(1)} %get-tuple-element.26.refs_0_.rest_0_), channel_id=1, source_target_pairs={{0,32},{1,33},{2,34},{3,35},{4,36},{5,37},{6,38},{7,39},{8,40},{9,... | collective-permute-start | bytes 73736 | tf_op jit(solution)/shard_map/ppermute | solution.py:458
  11.2 0.8 %collective-permute-done.refs_1_.rest_1_ = f32[3,16,128]{2,1,0:T(8,128)S(1)} collective-permute-done((f32[3,16,128]{2,1,0:T(8,128)S(1)}, f32[3,16,128]{2,1,0:T(8,128)S(1)}, u32[]{:S(2)}, u32[]{:S(2)}) %collective-permute-start) | collective-permute-done | bytes 24608 | tf_op jit(solution)/shard_map/ppermute | solution.py:458
  12.1 1.9 %collective-permute-start.1 = (f32[4,16,128]{2,1,0:T(8,128)S(1)}, f32[4,16,128]{2,1,0:T(8,128)S(1)}, u32[]{:S(2)}, u32[]{:S(2)}) collective-permute-start(f32[4,16,128]{2,1,0:T(8,128)S(1)} %relay_1.1), channel_id=1, source_target_pairs={{0,1},{1,0},{2,3},{3,2},{4,5},{5,4},{6,7},{7,6},{8,9},{9,8},{10,11... | collective-permute-start | bytes 98312 | tf_op jit(solution)/shard_map/ppermute | solution.py:458
  14.0 2.7 %collective-permute-done.1.refs_2_.rest_2_ = f32[4,16,128]{2,1,0:T(8,128)S(1)} collective-permute-done((f32[4,16,128]{2,1,0:T(8,128)S(1)}, f32[4,16,128]{2,1,0:T(8,128)S(1)}, u32[]{:S(2)}, u32[]{:S(2)}) %collective-permute-start.1) | collective-permute-done | bytes 32800 | tf_op jit(solution)/shard_map/ppermute | solution.py:458
  16.7 14.7 %collective-permute-start.2 = (f32[6,16,128]{2,1,0:T(8,128)S(1)}, f32[6,16,128]{2,1,0:T(8,128)S(1)}, u32[]{:S(2)}, u32[]{:S(2)}) collective-permute-start(f32[6,16,128]{2,1,0:T(8,128)S(1)} %relay_2.1), channel_id=1, source_target_pairs={{0,480},{1,481},{2,482},{3,483},{4,484},{5,485},{6,486},{7,487},{8... | collective-permute-start | bytes 147464 | tf_op jit(solution)/shard_map/ppermute | solution.py:458
  31.5 3.0 %collective-permute-done.2.refs_3_.rest_3_ = f32[6,16,128]{2,1,0:T(8,128)S(1)} collective-permute-done((f32[6,16,128]{2,1,0:T(8,128)S(1)}, f32[6,16,128]{2,1,0:T(8,128)S(1)}, u32[]{:S(2)}, u32[]{:S(2)}) %collective-permute-start.2) | collective-permute-done | bytes 49184 | tf_op jit(solution)/shard_map/ppermute | solution.py:458
  34.5 3.4 %collective-permute-start.3 = (f32[12,16,128]{2,1,0:T(8,128)S(1)}, f32[12,16,128]{2,1,0:T(8,128)S(1)}, u32[]{:S(2)}, u32[]{:S(2)}) collective-permute-start(f32[12,16,128]{2,1,0:T(8,128)S(1)} %relay_3.1), channel_id=1, source_target_pairs={{0,511},{1,2},{2,1},{3,484},{4,483},{5,6},{6,5},{7,488},{8,487},{9... | collective-permute-start | bytes 294920 | tf_op jit(solution)/shard_map/ppermute | solution.py:458
  37.9 2.8 %collective-permute-done.3.refs_4_.rest_4_ = f32[12,16,128]{2,1,0:T(8,128)S(1)} collective-permute-done((f32[12,16,128]{2,1,0:T(8,128)S(1)}, f32[12,16,128]{2,1,0:T(8,128)S(1)}, u32[]{:S(2)}, u32[]{:S(2)}) %collective-permute-start.3) | collective-permute-done | bytes 98336 | tf_op jit(solution)/shard_map/ppermute | solution.py:458
  40.7 3.0 %collective-permute-start.4 = (f32[6,16,128]{2,1,0:T(8,128)S(1)}, f32[6,16,128]{2,1,0:T(8,128)S(1)}, u32[]{:S(2)}, u32[]{:S(2)}) collective-permute-start(f32[6,16,128]{2,1,0:T(8,128)S(1)} %relay_4.1), channel_id=1, source_target_pairs={{0,32},{1,33},{2,34},{3,35},{4,36},{5,37},{6,38},{7,39},{8,40},{9,... | collective-permute-start | bytes 147464 | tf_op jit(solution)/shard_map/ppermute | solution.py:458
  43.8 0.9 %collective-permute-done.4.rest_5_.refs_5_ = f32[6,16,128]{2,1,0:T(8,128)S(1)} collective-permute-done((f32[6,16,128]{2,1,0:T(8,128)S(1)}, f32[6,16,128]{2,1,0:T(8,128)S(1)}, u32[]{:S(2)}, u32[]{:S(2)}) %collective-permute-start.4) | collective-permute-done | bytes 49184 | tf_op jit(solution)/shard_map/ppermute | solution.py:458
  44.6 1.9 %collective-permute-start.5 = (f32[9,16,128]{2,1,0:T(8,128)S(1)}, f32[9,16,128]{2,1,0:T(8,128)S(1)}, u32[]{:S(2)}, u32[]{:S(2)}) collective-permute-start(f32[9,16,128]{2,1,0:T(8,128)S(1)} %relay_5.1), channel_id=1, source_target_pairs={{0,1},{1,0},{2,3},{3,2},{4,5},{5,4},{6,7},{7,6},{8,9},{9,8},{10,11... | collective-permute-start | bytes 221192 | tf_op jit(solution)/shard_map/ppermute | solution.py:458
  46.5 1.6 %next_kernel.1 = (f32[3,8,128]{2,1,0:T(8,128)}, f32[3,8,128]{2,1,0:T(8,128)}, f32[3,16,128]{2,1,0:T(8,128)S(1)}, bf16[768,384]{1,0:T(8,128)(2,1)S(1)}, bf16[768,384]{1,0:T(8,128)(2,1)S(1)}) custom-call(f32[8,128]{1,0:T(8,128)S(1)} %get-tuple-element.19.place, f32[3,16,128]{2,1,0:T(8,128)S(1)} %get-tuple-element.20.state, ...), custom_call_target="tpu_custom_call" | custom-call | flops 1048576 | bytes 2186240 | tf_op jit(solution)/shard_map/next_kernel/pallas_call | solution.py:406
  48.2 1.6 %collective-permute-done.5.rest_6_ = f32[9,16,128]{2,1,0:T(8,128)S(1)} collective-permute-done((f32[9,16,128]{2,1,0:T(8,128)S(1)}, f32[9,16,128]{2,1,0:T(8,128)S(1)}, u32[]{:S(2)}, u32[]{:S(2)}) %collective-permute-start.5) | collective-permute-done | bytes 73760 | tf_op jit(solution)/shard_map/ppermute | solution.py:458
  49.7 3.1 %last_kernel.1 = (f32[3,8,128]{2,1,0:T(8,128)}, f32[3,8,128]{2,1,0:T(8,128)}) custom-call(f32[3,16,128]{2,1,0:T(8,128)S(1)} %get-tuple-element.28.third, bf16[768,384]{1,0:T(8,128)(2,1)S(1)} %get-tuple-element.29.far_high, bf16[768,384]{1,0:T(8,128)(2,1)S(1)} %get-tuple-element.30.far_low, f32[3,16,128]{2,1,0:T(8,128)S(1)} %get-tuple-element.26.refs_0_.rest_0_, ...), custom_call_target="tpu_custom_call" | custom-call | flops 1048576 | bytes 1581056 | tf_op jit(solution)/shard_map/last_kernel/pallas_call | solution.py:406
  (5 shorter events, 0.0 us)
Async XLA Ops:
  2.5 9.6 %collective-permute-start = (f32[3,16,128]{2,1,0:T(8,128)S(1)}, f32[3,16,128]{2,1,0:T(8,128)S(1)}, u32[]{:S(2)}, u32[]{:S(2)}) collective-permute-start(f32[3,16,128]{2,1,0:T(8,128)S(1)} %get-tuple-element.26.refs_0_.rest_0_), channel_id=1, source_target_pairs={{0,32},{1,33},{2,34},{3,35},{4,36},{5,37},{6,38},{7,39},{8,40},{9,... | collective-permute-start | bytes 73736 | tf_op jit(solution)/shard_map/ppermute | solution.py:458
  12.1 4.6 %collective-permute-start.1 = (f32[4,16,128]{2,1,0:T(8,128)S(1)}, f32[4,16,128]{2,1,0:T(8,128)S(1)}, u32[]{:S(2)}, u32[]{:S(2)}) collective-permute-start(f32[4,16,128]{2,1,0:T(8,128)S(1)} %relay_1.1), channel_id=1, source_target_pairs={{0,1},{1,0},{2,3},{3,2},{4,5},{5,4},{6,7},{7,6},{8,9},{9,8},{10,11... | collective-permute-start | bytes 98312 | tf_op jit(solution)/shard_map/ppermute | solution.py:458
  16.7 17.8 %collective-permute-start.2 = (f32[6,16,128]{2,1,0:T(8,128)S(1)}, f32[6,16,128]{2,1,0:T(8,128)S(1)}, u32[]{:S(2)}, u32[]{:S(2)}) collective-permute-start(f32[6,16,128]{2,1,0:T(8,128)S(1)} %relay_2.1), channel_id=1, source_target_pairs={{0,480},{1,481},{2,482},{3,483},{4,484},{5,485},{6,486},{7,487},{8... | collective-permute-start | bytes 147464 | tf_op jit(solution)/shard_map/ppermute | solution.py:458
  34.5 6.2 %collective-permute-start.3 = (f32[12,16,128]{2,1,0:T(8,128)S(1)}, f32[12,16,128]{2,1,0:T(8,128)S(1)}, u32[]{:S(2)}, u32[]{:S(2)}) collective-permute-start(f32[12,16,128]{2,1,0:T(8,128)S(1)} %relay_3.1), channel_id=1, source_target_pairs={{0,511},{1,2},{2,1},{3,484},{4,483},{5,6},{6,5},{7,488},{8,487},{9... | collective-permute-start | bytes 294920 | tf_op jit(solution)/shard_map/ppermute | solution.py:458
  40.7 3.9 %collective-permute-start.4 = (f32[6,16,128]{2,1,0:T(8,128)S(1)}, f32[6,16,128]{2,1,0:T(8,128)S(1)}, u32[]{:S(2)}, u32[]{:S(2)}) collective-permute-start(f32[6,16,128]{2,1,0:T(8,128)S(1)} %relay_4.1), channel_id=1, source_target_pairs={{0,32},{1,33},{2,34},{3,35},{4,36},{5,37},{6,38},{7,39},{8,40},{9,... | collective-permute-start | bytes 147464 | tf_op jit(solution)/shard_map/ppermute | solution.py:458
  44.6 5.1 %collective-permute-start.5 = (f32[9,16,128]{2,1,0:T(8,128)S(1)}, f32[9,16,128]{2,1,0:T(8,128)S(1)}, u32[]{:S(2)}, u32[]{:S(2)}) collective-permute-start(f32[9,16,128]{2,1,0:T(8,128)S(1)} %relay_5.1), channel_id=1, source_target_pairs={{0,1},{1,0},{2,3},{3,2},{4,5},{5,4},{6,7},{7,6},{8,9},{9,8},{10,11... | collective-permute-start | bytes 221192 | tf_op jit(solution)/shard_map/ppermute | solution.py:458

commit v5 on v4

--- a/solution.py
+++ b/solution.py
@@ -17,8 +17,11 @@
 F32 = jnp.float32
 BF16 = jnp.bfloat16
 KEYS = ((0, 0), (0, 1), (0, 2), (1, 1), (1, 2), (2, 2))
-RING = ((-1, -1), (-1, 0), (-1, 1), (0, -1), (0, 1), (1, -1), (1, 0), (1, 1))
+EARLY = ((-1, -1), (0, -1), (-1, 0), (1, 0))
+LATE = ((1, -1), (-1, 1), (0, 1), (1, 1))
+RING = EARLY + LATE
 WIDE = tuple((x, y) for x in range(-2, 3) for y in range(-2, 3))
+KNOWN = tuple(s for s in WIDE if s[1] < 2)
 KINDS = 3
 
 
@@ -61,15 +64,19 @@
         brought.append({d: known[source[i][d]] for d in devices})
         known = {d: known[d] | brought[i][d] for d in devices}
 
-    def wanted(x, y):
-        return [
-            (kind, (x + a) % nx, (y + b) % ny)
-            for kind in range(KINDS)
-            for a, b in (WIDE if kind == 0 else RING)
-        ]
+    def at(kind, d, steps_to):
+        up = 1 - d[1] % 2 * 2
+        return [(kind, (d[0] + a) % nx, (d[1] + up * b) % ny) for a, b in steps_to]
+
+    def wanted(d, wide, quad):
+        return at(0, d, wide) + at(1, d, quad) + at(2, d, quad)
+
+    soon = {d: at(1, d, EARLY) + at(2, d, EARLY) for d in devices}
 
     def route_of(item, d, before):
         found = [i for i in range(before) if item[1:] in brought[i][d]]
+        if item in soon[d]:
+            found = [i for i in found if i < len(steps) - 1]
         late = item[0] and item[1] != d[0] and item[2] != d[1]
         return found[-1 if late else 0]
 
@@ -82,7 +89,7 @@
                 sent[i][d].add(item)
 
     for d in devices:
-        ask(wanted(*d), d, len(steps))
+        ask(wanted(d, WIDE, RING), d, len(steps))
     for i in reversed(range(len(steps))):
         for d in devices:
             ask(sent[i][d], source[i][d], i)
@@ -108,9 +115,9 @@
         for i, f in enumerate(steps):
             row = tuple(place(item, d, i) for item in lists[i][f(*d)])
             assert send_rows[i].setdefault(c, row) == row
-        row = tuple(place(item, d, len(steps)) for item in wanted(*d))
+        row = tuple(place(item, d, len(steps)) for item in wanted(d, WIDE, LATE))
         assert last_rows.setdefault(c, row) == row
-        row = tuple(row[WIDE.index(s)] for s in RING)
+        row = tuple(place(item, d, len(steps)) for item in wanted(d, KNOWN, EARLY))
         assert max(row) < starts[-1] and next_rows.setdefault(c, row) == row
     links = [[(x * ny + y, f(x, y)[0] * ny + f(x, y)[1]) for x, y in devices] for f in steps]
     return steps, sizes, starts, send_rows, next_rows, last_rows, links
@@ -183,7 +190,13 @@
     return counters
 
 
-FAR_GROUPS = [4 * (3 * (x + 1) + y + 1) for x, y in RING]
+def upward():
+    return 1 - 2 * lax.rem(lax.axis_index("gy"), 2)
+
+
+def far_groups():
+    up = upward()
+    return [4 * (3 * (x + 1) + up * y + 1) for x, y in RING]
 
 
 def pair_terms(counter, source, home):
@@ -240,7 +253,7 @@
         copy.start()
     entries, pos, spring, border, vec, heat, vec0, heat0 = buffers
     copies[0].wait()
-    counters = count_slots(entries[...], FAR_GROUPS + [16, 17, 18, 19])
+    counters = count_slots(entries[...], far_groups() + [16, 17, 18, 19])
     for i in range(8):
         counts[i] = counters[i]
     for copy in copies[1:]:
@@ -292,7 +305,8 @@
 
 
 def shifted(cols, s):
-    return [cols[0] + column_edge * s[0], cols[1] + column_edge * s[1], cols[2], cols[3]]
+    rise = column_edge * s[1] * upward().astype(F32)
+    return [cols[0] + column_edge * s[0], cols[1] + rise, cols[2], cols[3]]
 
 
 def fill_pool(rows, starts, nx, received, pool):
@@ -303,14 +317,60 @@
     for_each_row(rows, nx, body)
 
 
-QUADS = (RING[:4], RING[4:])
-
-
-def side_fields(values):
-    return [
-        [by_group([moved(values[s], b, g) for g, s in enumerate(quad)]) for b in range(3)]
-        for quad in QUADS
+def side_fields(values, quad):
+    return [by_group([moved(values[s], b, g) for g, s in enumerate(quad)]) for b in range(3)]
+
+
+def edge_state(quad, values, geo, blocks, edge_high, edge_low):
+    for j in range(len(RING)):
+        edge_high[j * A + 3 * G : (j + 1) * A, :] = jnp.zeros((G, OWN), BF16)
+        edge_low[j * A + 3 * G : (j + 1) * A, :] = jnp.zeros((G, OWN), BF16)
+    halves = {s: split(x) for s, x in values.items()}
+    fields = side_fields(values, quad)
+    begun = [by_group([moved(x, b, g) for g, x in enumerate(blocks[0])]) for b in range(3)]
+    lists = [
+        by_group([moved(blocks[1 if k < 3 else 0][g], k, g) for g in range(4)]) for k in range(4)
     ]
+    counters = count_slots(jnp.concatenate(lists, axis=0).astype(jnp.int32), far_groups())
+    there = by_group([moved(values[s][0:8], 3, g) for g, s in enumerate(quad)])
+    home = spread([there[0:1], there[1:2], there[2:3], jnp.sqrt(there[3:4])])
+    sums = {}
+    for j, s in enumerate(RING):
+        around = [(t[0] + s[0], t[1] + s[1]) for t in quad]
+        source = [by_group([geo[t][c] for t in around]) for c in range(4)]
+        terms = pair_terms(counters[j], shifted(source, s), home)
+        put_terms(edge_high, edge_low, sums, [j * A + b * G for b in range(3)], terms)
+    terms = total(sums)
+    lhs = [
+        jnp.concatenate(
+            [
+                jnp.concatenate([halves[(t[0] + s[0], t[1] + s[1])][h] for s in RING], axis=1)
+                for t in quad
+            ],
+            axis=0,
+        )
+        for h in range(2)
+    ]
+    main = jnp.dot(jnp.concatenate(lhs, axis=0), edge_high[...], preferred_element_type=F32)
+    small = jnp.dot(lhs[0], edge_low[...], preferred_element_type=F32)
+    result = []
+    for a in range(3):
+        cut = slice(a * A, (a + 1) * A)
+        sums_of = [
+            main[g * F : (g + 1) * F, cut]
+            + main[(4 + g) * F : (5 + g) * F, cut]
+            + small[g * F : (g + 1) * F, cut]
+            for g in range(4)
+        ]
+        inner = self_product(terms, fields, a) - by_group(sums_of)
+        result.append(begun[a] + 2.0 * inner)
+    return result
+
+
+def pool_blocks(pool, wide):
+    values = {s: pool[j] for j, s in enumerate(wide)}
+    blocks = [[pool[len(wide) + 4 * k + g] for g in range(4)] for k in range(2)]
+    return values, blocks
 
 
 def woven(first, second):
@@ -319,9 +379,9 @@
 
 def next_kernel(rows, starts, nx, n_in, place, state, partial, self_in, counts,
                 own_high, own_low, *rest):
-    v2, h2, begun, far_high, far_low, pool = rest[n_in:]
+    v2, h2, begun, early, far_high, far_low, pool, edge_high, edge_low = rest[n_in:]
     fill_pool(rows, starts, nx, rest[:n_in], pool)
-    values = {s: pool[j] for j, s in enumerate(RING)}
+    values, blocks = pool_blocks(pool, KNOWN)
     geo = geometry_of(values)
     home = spread([place[c : c + 1, :] for c in range(4)])
     sums = {}
@@ -330,7 +390,8 @@
         put_terms(far_high, far_low, sums, [b * 2 * A + j * G for b in range(3)], terms)
     far_terms = total(sums)
     current = [state[b] for b in range(3)]
-    far = apply_weights(far_high, far_low, woven(*side_fields(values)))
+    sides = woven(side_fields(values, EARLY), side_fields(values, LATE))
+    far = apply_weights(far_high, far_low, sides)
     second = []
     for a in range(3):
         inner = self_product(far_terms, current, a) - far[:, a * A : (a + 1) * A]
@@ -342,59 +403,17 @@
     for a in range(3):
         inner = self_product(all_terms, second, a) - far[:, a * A : (a + 1) * A] - second[a]
         begun[a] = 2.0 * inner - current[a]
-
-
-def last_kernel(rows, starts, nx, n_in, third, far_high, far_low, *rest):
+    edges = edge_state(EARLY, values, geo, blocks, edge_high, edge_low)
+    for a in range(3):
+        early[a] = edges[a]
+
+
+def last_kernel(rows, starts, nx, n_in, third, early, far_high, far_low, *rest):
     v3, h3, pool, edge_high, edge_low = rest[n_in:]
     fill_pool(rows, starts, nx, rest[:n_in], pool)
-    values = {s: pool[j] for j, s in enumerate(WIDE)}
-    halves = {s: split(x) for s, x in values.items()}
-    geo = geometry_of(values)
-    for j in range(len(RING)):
-        edge_high[j * A + 3 * G : (j + 1) * A, :] = jnp.zeros((G, OWN), BF16)
-        edge_low[j * A + 3 * G : (j + 1) * A, :] = jnp.zeros((G, OWN), BF16)
-    edges = []
-    for q, (quad, fields) in enumerate(zip(QUADS, side_fields(values))):
-        blocks = [[pool[len(WIDE) + k * 8 + 4 * q + g] for g in range(4)] for k in range(2)]
-        begun = [by_group([moved(x, b, g) for g, x in enumerate(blocks[0])]) for b in range(3)]
-        lists = [
-            by_group([moved(blocks[1 if k < 3 else 0][g], k, g) for g in range(4)]) for k in range(4)
-        ]
-        counters = count_slots(jnp.concatenate(lists, axis=0).astype(jnp.int32), FAR_GROUPS)
-        there = by_group([moved(values[s][0:8], 3, g) for g, s in enumerate(quad)])
-        home = spread([there[0:1], there[1:2], there[2:3], jnp.sqrt(there[3:4])])
-        sums = {}
-        for j, s in enumerate(RING):
-            around = [(t[0] + s[0], t[1] + s[1]) for t in quad]
-            source = [by_group([geo[t][c] for t in around]) for c in range(4)]
-            terms = pair_terms(counters[j], shifted(source, s), home)
-            put_terms(edge_high, edge_low, sums, [j * A + b * G for b in range(3)], terms)
-        terms = total(sums)
-        lhs = [
-            jnp.concatenate(
-                [
-                    jnp.concatenate([halves[(t[0] + s[0], t[1] + s[1])][h] for s in RING], axis=1)
-                    for t in quad
-                ],
-                axis=0,
-            )
-            for h in range(2)
-        ]
-        main = jnp.dot(jnp.concatenate(lhs, axis=0), edge_high[...], preferred_element_type=F32)
-        small = jnp.dot(lhs[0], edge_low[...], preferred_element_type=F32)
-        result = []
-        for a in range(3):
-            cut = slice(a * A, (a + 1) * A)
-            sums_of = [
-                main[g * F : (g + 1) * F, cut]
-                + main[(4 + g) * F : (5 + g) * F, cut]
-                + small[g * F : (g + 1) * F, cut]
-                for g in range(4)
-            ]
-            inner = self_product(terms, fields, a) - by_group(sums_of)
-            result.append(begun[a] + 2.0 * inner)
-        edges.append(result)
-    far = apply_weights(far_high, far_low, woven(*edges))
+    values, blocks = pool_blocks(pool, WIDE)
+    late = edge_state(LATE, values, geometry_of(values), blocks, edge_high, edge_low)
+    far = apply_weights(far_high, far_low, woven([early[b] for b in range(3)], late))
     for a in range(3):
         result = third[a] - 2.0 * far[:, a * A : (a + 1) * A]
         v3[a] = result[:8]
@@ -456,30 +475,28 @@
                 received,
             )
         received.append(lax.ppermute(outgoing, ("gx", "gy"), links[i]))
-    early = received[:-1]
-    v2, h2, third, far_high, far_low = call(
-        functools.partial(next_kernel, next_rows, starts, nx, len(early)),
+    edge = [pltpu.VMEM((8 * A, OWN), BF16)] * 2
+    before = received[:-1]
+    v2, h2, third, early, far_high, far_low = call(
+        functools.partial(next_kernel, next_rows, starts, nx, len(before)),
         "next_kernel",
         (
             vector,
             vector,
             shape((3, F, A), F32),
+            shape((3, F, A), F32),
             shape((6 * A, OWN), BF16),
             shape((6 * A, OWN), BF16),
         ),
-        (place, state, partial, self_terms, counts, own_high, own_low, *early),
-        (pltpu.VMEM((len(RING), F, A), F32),),
+        (place, state, partial, self_terms, counts, own_high, own_low, *before),
+        [pltpu.VMEM((len(KNOWN) + 8, F, A), F32)] + edge,
     )
     v3, h3 = call(
         functools.partial(last_kernel, last_rows, starts, nx, len(received)),
         "last_kernel",
         (vector, vector),
-        (third, far_high, far_low, *received),
-        (
-            pltpu.VMEM((len(WIDE) + 16, F, A), F32),
-            pltpu.VMEM((8 * A, OWN), BF16),
-            pltpu.VMEM((8 * A, OWN), BF16),
-        ),
+        (third, early, far_high, far_low, *received),
+        [pltpu.VMEM((len(WIDE) + 8, F, A), F32)] + edge,
     )
     whole = vec_prev.shape
     return v2.reshape(whole), v3.reshape(whole), h2.reshape(whole), h3.reshape(whole)

time: 53.1 us -> 52.3 us (0.985)
  transfers between devices with their start and end apart: 6 -> 6, of which waited for: 6 -> 6; matrix products, arithmetic and copies ran while one was open for 0% -> 0% of each run, Pallas kernels for 3% -> 4%
where the time goes in v5:
time: 52.3 us; the launch traced here: 52 us
  starting transfers between devices  33.7 us (64%)
  waiting for transfers between devices  11.3 us (22%)
  Pallas kernels  6.25 us (12%)
  between operations  0.7 us (1%)
    ppermute x6, starting transfers between devices, shards(): received.append(lax.ppermute(outgoing, ('gx', 'gy'), links[i]))  33.7 us
    ppermute x6, waiting for transfers between devices, shards(): received.append(lax.ppermute(outgoing, ('gx', 'gy'), links[i]))  11.3 us
    pallas_call x8, Pallas kernels, call(): pl.pallas_call(kernel, out_shape=out_shape, in_specs=[pl.BlockSpec(memory...  6.25 us
  transfers between devices with their start and end apart: 6, of which 6 were waited for; matrix products, arithmetic and copies ran while one was open for 0% of the time, Pallas kernels for 4%

profile of v5, /device:TPU:1, one launch (start us, length us, event | category | flops | bytes accessed | tf_op | source)
XLA Modules:
  0.0 52.0 jit_solution(2696407800206326763)
XLA Ops:
  0.6 1.8 %own_kernel.1 = (f32[3,16,128]{2,1,0:T(8,128)S(1)}, bf16[384,384]{1,0:T(8,128)(2,1)S(1)}, bf16[384,384]{1,0:T(8,128)(2,1)S(1)}, f32[3,16,128]{2,1,0:T(8,128)S(1)...) custom-call(s32[64,128]{1,0:T(8,128)} %bitcast.20, ...), custom_call_target="tpu_custom_call" | custom-call | flops 1048576 | bytes 787584 | tf_op jit(solution)/shard_map/own_kernel/pallas_call | solution.py:425
  2.5 8.7 %collective-permute-start = (f32[3,16,128]{2,1,0:T(8,128)S(1)}, f32[3,16,128]{2,1,0:T(8,128)S(1)}, u32[]{:S(2)}, u32[]{:S(2)}) collective-permute-start(f32[3,16,128]{2,1,0:T(8,128)S(1)} %get-tuple-element.27.refs_0_.rest_0_), channel_id=1, source_target_pairs={{0,32},{1,33},{2,34},{3,35},{4,36},{5,37},{6,38},{7,39},{8,40},{9,... | collective-permute-start | bytes 73736 | tf_op jit(solution)/shard_map/ppermute | solution.py:477
  11.2 0.8 %collective-permute-done.refs_1_.rest_1_ = f32[3,16,128]{2,1,0:T(8,128)S(1)} collective-permute-done((f32[3,16,128]{2,1,0:T(8,128)S(1)}, f32[3,16,128]{2,1,0:T(8,128)S(1)}, u32[]{:S(2)}, u32[]{:S(2)}) %collective-permute-start) | collective-permute-done | bytes 24608 | tf_op jit(solution)/shard_map/ppermute | solution.py:477
  12.1 1.9 %collective-permute-start.1 = (f32[4,16,128]{2,1,0:T(8,128)S(1)}, f32[4,16,128]{2,1,0:T(8,128)S(1)}, u32[]{:S(2)}, u32[]{:S(2)}) collective-permute-start(f32[4,16,128]{2,1,0:T(8,128)S(1)} %relay_1.1), channel_id=1, source_target_pairs={{0,1},{1,0},{2,3},{3,2},{4,5},{5,4},{6,7},{7,6},{8,9},{9,8},{10,11... | collective-permute-start | bytes 98312 | tf_op jit(solution)/shard_map/ppermute | solution.py:477
  14.0 2.7 %collective-permute-done.1.refs_2_.rest_2_ = f32[4,16,128]{2,1,0:T(8,128)S(1)} collective-permute-done((f32[4,16,128]{2,1,0:T(8,128)S(1)}, f32[4,16,128]{2,1,0:T(8,128)S(1)}, u32[]{:S(2)}, u32[]{:S(2)}) %collective-permute-start.1) | collective-permute-done | bytes 32800 | tf_op jit(solution)/shard_map/ppermute | solution.py:477
  16.7 14.7 %collective-permute-start.2 = (f32[6,16,128]{2,1,0:T(8,128)S(1)}, f32[6,16,128]{2,1,0:T(8,128)S(1)}, u32[]{:S(2)}, u32[]{:S(2)}) collective-permute-start(f32[6,16,128]{2,1,0:T(8,128)S(1)} %relay_2.1), channel_id=1, source_target_pairs={{0,480},{1,481},{2,482},{3,483},{4,484},{5,485},{6,486},{7,487},{8... | collective-permute-start | bytes 147464 | tf_op jit(solution)/shard_map/ppermute | solution.py:477
  31.5 3.0 %collective-permute-done.2.refs_3_.rest_3_ = f32[6,16,128]{2,1,0:T(8,128)S(1)} collective-permute-done((f32[6,16,128]{2,1,0:T(8,128)S(1)}, f32[6,16,128]{2,1,0:T(8,128)S(1)}, u32[]{:S(2)}, u32[]{:S(2)}) %collective-permute-start.2) | collective-permute-done | bytes 49184 | tf_op jit(solution)/shard_map/ppermute | solution.py:477
  34.5 3.4 %collective-permute-start.3 = (f32[12,16,128]{2,1,0:T(8,128)S(1)}, f32[12,16,128]{2,1,0:T(8,128)S(1)}, u32[]{:S(2)}, u32[]{:S(2)}) collective-permute-start(f32[12,16,128]{2,1,0:T(8,128)S(1)} %relay_3.1), channel_id=1, source_target_pairs={{0,511},{1,2},{2,1},{3,484},{4,483},{5,6},{6,5},{7,488},{8,487},{9... | collective-permute-start | bytes 294920 | tf_op jit(solution)/shard_map/ppermute | solution.py:477
  37.9 2.8 %collective-permute-done.3.refs_4_.rest_4_ = f32[12,16,128]{2,1,0:T(8,128)S(1)} collective-permute-done((f32[12,16,128]{2,1,0:T(8,128)S(1)}, f32[12,16,128]{2,1,0:T(8,128)S(1)}, u32[]{:S(2)}, u32[]{:S(2)}) %collective-permute-start.3) | collective-permute-done | bytes 98336 | tf_op jit(solution)/shard_map/ppermute | solution.py:477
  40.7 3.0 %collective-permute-start.4 = (f32[6,16,128]{2,1,0:T(8,128)S(1)}, f32[6,16,128]{2,1,0:T(8,128)S(1)}, u32[]{:S(2)}, u32[]{:S(2)}) collective-permute-start(f32[6,16,128]{2,1,0:T(8,128)S(1)} %relay_4.1), channel_id=1, source_target_pairs={{0,32},{1,33},{2,34},{3,35},{4,36},{5,37},{6,38},{7,39},{8,40},{9,... | collective-permute-start | bytes 147464 | tf_op jit(solution)/shard_map/ppermute | solution.py:477
  43.8 0.9 %collective-permute-done.4.rest_5_.refs_5_ = f32[6,16,128]{2,1,0:T(8,128)S(1)} collective-permute-done((f32[6,16,128]{2,1,0:T(8,128)S(1)}, f32[6,16,128]{2,1,0:T(8,128)S(1)}, u32[]{:S(2)}, u32[]{:S(2)}) %collective-permute-start.4) | collective-permute-done | bytes 49184 | tf_op jit(solution)/shard_map/ppermute | solution.py:477
  44.6 1.9 %collective-permute-start.5 = (f32[9,16,128]{2,1,0:T(8,128)S(1)}, f32[9,16,128]{2,1,0:T(8,128)S(1)}, u32[]{:S(2)}, u32[]{:S(2)}) collective-permute-start(f32[9,16,128]{2,1,0:T(8,128)S(1)} %relay_5.1), channel_id=1, source_target_pairs={{0,1},{1,0},{2,3},{3,2},{4,5},{5,4},{6,7},{7,6},{8,9},{9,8},{10,11... | collective-permute-start | bytes 221192 | tf_op jit(solution)/shard_map/ppermute | solution.py:477
  46.5 2.1 %next_kernel.1 = (f32[3,8,128]{2,1,0:T(8,128)}, f32[3,8,128]{2,1,0:T(8,128)}, f32[3,16,128]{2,1,0:T(8,128)S(1)}, f32[3,16,128]{2,1,0:T(8,128)S(1)}, bf16[768,384...) custom-call(f32[8,128]{1,0:T(8,128)S(1)} %get-tuple-element.20.place, f32[3,16,128]{2,1,0:T(8,128)S(1)} %get-tuple-element.21.state, ...), custom_call_target="tpu_custom_call" | custom-call | flops 1048576 | bytes 2210816 | tf_op jit(solution)/shard_map/next_kernel/pallas_call | solution.py:425
  48.6 1.1 %collective-permute-done.5.rest_6_ = f32[9,16,128]{2,1,0:T(8,128)S(1)} collective-permute-done((f32[9,16,128]{2,1,0:T(8,128)S(1)}, f32[9,16,128]{2,1,0:T(8,128)S(1)}, u32[]{:S(2)}, u32[]{:S(2)}) %collective-permute-start.5) | collective-permute-done | bytes 73760 | tf_op jit(solution)/shard_map/ppermute | solution.py:477
  49.7 2.3 %last_kernel.1 = (f32[3,8,128]{2,1,0:T(8,128)}, f32[3,8,128]{2,1,0:T(8,128)}) custom-call(f32[3,16,128]{2,1,0:T(8,128)S(1)} %get-tuple-element.29.third, f32[3,16,128]{2,1,0:T(8,128)S(1)} %get-tuple-element.30.early, bf16[768,384]{1,0:T(8,128)(2,1)S(1)} %get-tuple-element.31.far_high, bf16[768,384]{1,0:T(8,128)(2,1)S(1)} %get-tuple-element.32.far_low, ...), custom_call_target="tpu_custom_call" | custom-call | flops 1048576 | bytes 1605632 | tf_op jit(solution)/shard_map/last_kernel/pallas_call | solution.py:425
  (5 shorter events, 0.0 us)
Async XLA Ops:
  2.5 9.6 %collective-permute-start = (f32[3,16,128]{2,1,0:T(8,128)S(1)}, f32[3,16,128]{2,1,0:T(8,128)S(1)}, u32[]{:S(2)}, u32[]{:S(2)}) collective-permute-start(f32[3,16,128]{2,1,0:T(8,128)S(1)} %get-tuple-element.27.refs_0_.rest_0_), channel_id=1, source_target_pairs={{0,32},{1,33},{2,34},{3,35},{4,36},{5,37},{6,38},{7,39},{8,40},{9,... | collective-permute-start | bytes 73736 | tf_op jit(solution)/shard_map/ppermute | solution.py:477
  12.1 4.6 %collective-permute-start.1 = (f32[4,16,128]{2,1,0:T(8,128)S(1)}, f32[4,16,128]{2,1,0:T(8,128)S(1)}, u32[]{:S(2)}, u32[]{:S(2)}) collective-permute-start(f32[4,16,128]{2,1,0:T(8,128)S(1)} %relay_1.1), channel_id=1, source_target_pairs={{0,1},{1,0},{2,3},{3,2},{4,5},{5,4},{6,7},{7,6},{8,9},{9,8},{10,11... | collective-permute-start | bytes 98312 | tf_op jit(solution)/shard_map/ppermute | solution.py:477
  16.7 17.8 %collective-permute-start.2 = (f32[6,16,128]{2,1,0:T(8,128)S(1)}, f32[6,16,128]{2,1,0:T(8,128)S(1)}, u32[]{:S(2)}, u32[]{:S(2)}) collective-permute-start(f32[6,16,128]{2,1,0:T(8,128)S(1)} %relay_2.1), channel_id=1, source_target_pairs={{0,480},{1,481},{2,482},{3,483},{4,484},{5,485},{6,486},{7,487},{8... | collective-permute-start | bytes 147464 | tf_op jit(solution)/shard_map/ppermute | solution.py:477
  34.5 6.2 %collective-permute-start.3 = (f32[12,16,128]{2,1,0:T(8,128)S(1)}, f32[12,16,128]{2,1,0:T(8,128)S(1)}, u32[]{:S(2)}, u32[]{:S(2)}) collective-permute-start(f32[12,16,128]{2,1,0:T(8,128)S(1)} %relay_3.1), channel_id=1, source_target_pairs={{0,511},{1,2},{2,1},{3,484},{4,483},{5,6},{6,5},{7,488},{8,487},{9... | collective-permute-start | bytes 294920 | tf_op jit(solution)/shard_map/ppermute | solution.py:477
  40.7 3.9 %collective-permute-start.4 = (f32[6,16,128]{2,1,0:T(8,128)S(1)}, f32[6,16,128]{2,1,0:T(8,128)S(1)}, u32[]{:S(2)}, u32[]{:S(2)}) collective-permute-start(f32[6,16,128]{2,1,0:T(8,128)S(1)} %relay_4.1), channel_id=1, source_target_pairs={{0,32},{1,33},{2,34},{3,35},{4,36},{5,37},{6,38},{7,39},{8,40},{9,... | collective-permute-start | bytes 147464 | tf_op jit(solution)/shard_map/ppermute | solution.py:477
  44.6 5.1 %collective-permute-start.5 = (f32[9,16,128]{2,1,0:T(8,128)S(1)}, f32[9,16,128]{2,1,0:T(8,128)S(1)}, u32[]{:S(2)}, u32[]{:S(2)}) collective-permute-start(f32[9,16,128]{2,1,0:T(8,128)S(1)} %relay_5.1), channel_id=1, source_target_pairs={{0,1},{1,0},{2,3},{3,2},{4,5},{5,4},{6,7},{7,6},{8,9},{9,8},{10,11... | collective-permute-start | bytes 221192 | tf_op jit(solution)/shard_map/ppermute | solution.py:477

commit v6 on v5

--- a/solution.py
+++ b/solution.py
@@ -77,7 +77,7 @@
         found = [i for i in range(before) if item[1:] in brought[i][d]]
         if item in soon[d]:
             found = [i for i in found if i < len(steps) - 1]
-        late = item[0] and item[1] != d[0] and item[2] != d[1]
+        late = item[0] and item[1] != d[0] and (item[2] != d[1] or item[1] == d[0] ^ 1)
         return found[-1 if late else 0]
 
     sent = [{d: set() for d in devices} for _ in steps]
@@ -139,9 +139,9 @@
 
 def block_at(refs, starts, place):
     if place < KINDS:
-        return refs[0][place]
+        return refs[min(place, 1)][max(place - 1, 0)]
     i = max(j for j in range(len(starts)) if starts[j] <= place)
-    return refs[i + 1][place - starts[i]]
+    return refs[i + 2][place - starts[i]]
 
 
 def relay_kernel(rows, starts, nx, *refs):
@@ -227,10 +227,10 @@
 
 
 def apply_weights(w_high, w_low, lhs):
-    high, low = split(lhs)
+    high, low = split(jnp.concatenate(lhs, axis=1))
     both = jnp.concatenate([high, low], axis=0)
-    main = jnp.dot(both, w_high[...], preferred_element_type=F32)
-    rest = jnp.dot(high, w_low[...], preferred_element_type=F32)
+    main = jnp.dot(both, w_high, preferred_element_type=F32)
+    rest = jnp.dot(high, w_low, preferred_element_type=F32)
     return main[:F] + main[F:] + rest
 
 
@@ -242,22 +242,30 @@
     return [jnp.broadcast_to(r, (G, A)) for r in rows]
 
 
-def own_kernel(*refs):
-    inputs, outputs, buffers, arrived = refs[:8], refs[8:16], refs[16:24], refs[24]
-    payload, w_high, w_low, partial, self_out, counts, state, place = outputs
+def pack_kernel(*refs):
+    inputs, payload, buffers, arrived = refs[:8], refs[8], refs[9:17], refs[17]
     copies = [
         pltpu.make_async_copy(source, target, arrived.at[i])
         for i, (source, target) in enumerate(zip(inputs, buffers))
     ]
     for copy in copies:
         copy.start()
-    entries, pos, spring, border, vec, heat, vec0, heat0 = buffers
-    copies[0].wait()
+    for copy in copies[:5]:
+        copy.wait()
+    pos, spring, border, vec, heat = buffers[:5]
+    geometry = jnp.concatenate(
+        [pos[0], pos[1], pos[2], spring[...], jnp.zeros((F - 4, A), F32)], axis=0
+    )
+    payload[0] = by_group([border_lanes(border, x) for x in (*stacked(vec, heat), geometry)])
+    for copy in copies[5:]:
+        copy.wait()
+
+
+def own_kernel(pos, spring, border, vec, heat, entries, vec0, heat0,
+               payload, w_high, w_low, partial, self_out, counts, state, place):
     counters = count_slots(entries[...], far_groups() + [16, 17, 18, 19])
     for i in range(8):
         counts[i] = counters[i]
-    for copy in copies[1:]:
-        copy.wait()
     root = jnp.sqrt(spring[...])
     home = spread([pos[0], pos[1], pos[2], root])
     place[...] = jnp.concatenate([pos[0], pos[1], pos[2], root, jnp.zeros((4, A), F32)], axis=0)
@@ -271,21 +279,17 @@
     for i, key in enumerate(KEYS):
         self_out[i : i + 1, :] = own_terms[key]
     current, previous = stacked(vec, heat), stacked(vec0, heat0)
-    far = apply_weights(w_high, w_low, jnp.concatenate(current, axis=1))
+    far = apply_weights(w_high[...], w_low[...], current)
     begun = []
     for a in range(3):
         inner = self_product(own_terms, current, a) - far[:, a * A : (a + 1) * A] - current[a]
         begun.append(2.0 * inner - previous[a])
         partial[a] = begun[a]
         state[a] = current[a]
-    geometry = jnp.concatenate(
-        [pos[0], pos[1], pos[2], spring[...], jnp.zeros((F - 4, A), F32)], axis=0
-    )
     picked = functools.partial(border_lanes, border)
     lists = [picked(entries[F * s : F * (s + 1), :].astype(F32)) for s in range(4)]
-    payload[0] = by_group([picked(x) for x in (*current, geometry)])
-    payload[1] = by_group([picked(x) for x in begun] + [lists[3]])
-    payload[2] = by_group(lists[:3] + [jnp.zeros((F, A), F32)])
+    payload[0] = by_group([picked(x) for x in begun] + [lists[3]])
+    payload[1] = by_group(lists[:3] + [jnp.zeros((F, A), F32)])
 
 
 def moved(block, source, target):
@@ -373,13 +377,9 @@
     return values, blocks
 
 
-def woven(first, second):
-    return jnp.concatenate([x for b in range(3) for x in (first[b], second[b])], axis=1)
-
-
 def next_kernel(rows, starts, nx, n_in, place, state, partial, self_in, counts,
                 own_high, own_low, *rest):
-    v2, h2, begun, early, far_high, far_low, pool, edge_high, edge_low = rest[n_in:]
+    v2, h2, begun, far_high, far_low, pool, edge_high, edge_low = rest[n_in:]
     fill_pool(rows, starts, nx, rest[:n_in], pool)
     values, blocks = pool_blocks(pool, KNOWN)
     geo = geometry_of(values)
@@ -387,11 +387,11 @@
     sums = {}
     for j, s in enumerate(RING):
         terms = pair_terms(counts[j], shifted(geo[s], s), home)
-        put_terms(far_high, far_low, sums, [b * 2 * A + j * G for b in range(3)], terms)
+        put_terms(far_high, far_low, sums, [(j // 4 * 3 + b) * A + j % 4 * G for b in range(3)], terms)
     far_terms = total(sums)
     current = [state[b] for b in range(3)]
-    sides = woven(side_fields(values, EARLY), side_fields(values, LATE))
-    far = apply_weights(far_high, far_low, sides)
+    sides = side_fields(values, EARLY) + side_fields(values, LATE)
+    far = apply_weights(far_high[...], far_low[...], sides)
     second = []
     for a in range(3):
         inner = self_product(far_terms, current, a) - far[:, a * A : (a + 1) * A]
@@ -399,21 +399,20 @@
         v2[a] = second[a][:8]
         h2[a] = second[a][8:]
     all_terms = {key: far_terms[key] + self_in[i : i + 1, :] for i, key in enumerate(KEYS)}
-    far = apply_weights(own_high, own_low, jnp.concatenate(second, axis=1))
+    far = apply_weights(own_high[...], own_low[...], second)
+    early = edge_state(EARLY, values, geo, blocks, edge_high, edge_low)
+    far += apply_weights(far_high[:OWN, :], far_low[:OWN, :], early)
     for a in range(3):
         inner = self_product(all_terms, second, a) - far[:, a * A : (a + 1) * A] - second[a]
         begun[a] = 2.0 * inner - current[a]
-    edges = edge_state(EARLY, values, geo, blocks, edge_high, edge_low)
-    for a in range(3):
-        early[a] = edges[a]
-
-
-def last_kernel(rows, starts, nx, n_in, third, early, far_high, far_low, *rest):
+
+
+def last_kernel(rows, starts, nx, n_in, third, far_high, far_low, *rest):
     v3, h3, pool, edge_high, edge_low = rest[n_in:]
     fill_pool(rows, starts, nx, rest[:n_in], pool)
     values, blocks = pool_blocks(pool, WIDE)
     late = edge_state(LATE, values, geometry_of(values), blocks, edge_high, edge_low)
-    far = apply_weights(far_high, far_low, woven([early[b] for b in range(3)], late))
+    far = apply_weights(far_high[OWN:, :], far_low[OWN:, :], late)
     for a in range(3):
         result = third[a] - 2.0 * far[:, a * A : (a + 1) * A]
         v3[a] = result[:8]
@@ -426,6 +425,7 @@
         kernel,
         out_shape=out_shape,
         in_specs=[pl.BlockSpec(memory_space=space)] * len(args),
+        out_specs=[pl.BlockSpec(memory_space=pltpu.VMEM)] * len(out_shape),
         scratch_shapes=scratch,
         name=name,
         cost_estimate=pl.CostEstimate(flops=2**20, bytes_accessed=size, transcendentals=0),
@@ -442,15 +442,24 @@
     stiff = spring.reshape(1, A)
     entries = neighbours.reshape(NB, A)
     v0, v1, h0, h1 = (x.reshape(3, 8, A) for x in (vec_prev, vec_now, heat_prev, heat_now))
+    index = border.reshape(1, G)
     first = [
         pltpu.with_memory_space_constraint(x, pltpu.HBM)
-        for x in (entries, pos, stiff, border.reshape(1, G), v1, h1, v0, h0)
+        for x in (pos, stiff, index, v1, h1, entries, v0, h0)
     ]
-    payload, own_high, own_low, partial, self_terms, counts, state, place = call(
+    fields, *first = call(
+        pack_kernel,
+        "pack_kernel",
+        (shape((1, F, A), F32), *(shape(x.shape, x.dtype) for x in first)),
+        first,
+        [pltpu.SemaphoreType.DMA((8,))],
+        pltpu.HBM,
+    )
+    lists, own_high, own_low, partial, self_terms, counts, state, place = call(
         own_kernel,
         "own_kernel",
         (
-            shape((KINDS, F, A), F32),
+            shape((2, F, A), F32),
             shape((OWN, OWN), BF16),
             shape((OWN, OWN), BF16),
             shape((3, F, A), F32),
@@ -460,13 +469,11 @@
             shape((8, A), F32),
         ),
         first,
-        [pltpu.VMEM(x.shape, x.dtype) for x in first] + [pltpu.SemaphoreType.DMA((8,))],
-        pltpu.HBM,
     )
-    received = [payload]
+    received = [fields, lists]
     for i in range(len(steps)):
-        if send_rows[i][0] == tuple(range(KINDS)) and len(set(send_rows[i].values())) == 1:
-            outgoing = payload
+        if i == 0 and set(send_rows[0].values()) == {(0,)}:
+            outgoing = fields
         else:
             (outgoing,) = call(
                 functools.partial(relay_kernel, send_rows[i], starts, nx),
@@ -477,13 +484,12 @@
         received.append(lax.ppermute(outgoing, ("gx", "gy"), links[i]))
     edge = [pltpu.VMEM((8 * A, OWN), BF16)] * 2
     before = received[:-1]
-    v2, h2, third, early, far_high, far_low = call(
+    v2, h2, third, far_high, far_low = call(
         functools.partial(next_kernel, next_rows, starts, nx, len(before)),
         "next_kernel",
         (
             vector,
             vector,
-            shape((3, F, A), F32),
             shape((3, F, A), F32),
             shape((6 * A, OWN), BF16),
             shape((6 * A, OWN), BF16),
@@ -495,7 +501,7 @@
         functools.partial(last_kernel, last_rows, starts, nx, len(received)),
         "last_kernel",
         (vector, vector),
-        (third, early, far_high, far_low, *received),
+        (third, far_high, far_low, *received),
         [pltpu.VMEM((len(WIDE) + 8, F, A), F32)] + edge,
     )
     whole = vec_prev.shape

time: 52.3 us -> 51.4 us (0.983)
  waiting for transfers between devices: 11.3 us -> 10.4 us
    ppermute x6, waiting for transfers between devices: 11.3 us -> 10.4 us  [shards(): received.append(lax.ppermute(outgoing, ('gx', 'gy'), links[i]))]
    pallas_call x8 -> x9, Pallas kernels: 6.25 us -> 6.4 us  [call(): pl.pallas_call(kernel, out_shape=out_shape, in_specs=[pl.BlockSpec(memory...]
  transfers between devices with their start and end apart: 6 -> 6, of which waited for: 6 -> 5; matrix products, arithmetic and copies ran while one was open for 0% -> 0% of each run, Pallas kernels for 4% -> 6%
where the time goes in v6:
time: 51.4 us; the launch traced here: 51.1 us
  starting transfers between devices  33.6 us (65%)
  waiting for transfers between devices  10.4 us (20%)
  Pallas kernels  6.4 us (12%)
  between operations  0.71 us (1%)
    ppermute x6, starting transfers between devices, shards(): received.append(lax.ppermute(outgoing, ('gx', 'gy'), links[i]))  33.6 us
    ppermute x6, waiting for transfers between devices, shards(): received.append(lax.ppermute(outgoing, ('gx', 'gy'), links[i]))  10.4 us
    pallas_call x9, Pallas kernels, call(): pl.pallas_call(kernel, out_shape=out_shape, in_specs=[pl.BlockSpec(memory...  6.4 us
  transfers between devices with their start and end apart: 6, of which 5 were waited for; matrix products, arithmetic and copies ran while one was open for 0% of the time, Pallas kernels for 6%

profile of v6, /device:TPU:1, one launch (start us, length us, event | category | flops | bytes accessed | tf_op | source)
XLA Modules:
  0.0 51.1 jit_solution(17746973488585608046)
XLA Ops:
  0.6 1.0 %pack_kernel.1 = (f32[1,16,128]{2,1,0:T(8,128)S(1)}, f32[3,1,128]{2,1,0:T(1,128)S(1)}, f32[1,128]{1,0:T(1,128)S(1)}, s32[1,32]{1,0:T(1,128)S(1)}, f32[3,8,128]{2...) custom-call(f32[3,1,128]{2,1,0:T(1,128)} %bitcast.25, ...), custom_call_target="tpu_custom_call" | custom-call | flops 1048576 | bytes 176384 | tf_op jit(solution)/shard_map/pack_kernel/pallas_call | solution.py:424
  1.6 8.7 %collective-permute-start = (f32[1,16,128]{2,1,0:T(8,128)S(1)}, f32[1,16,128]{2,1,0:T(8,128)S(1)}, u32[]{:S(2)}, u32[]{:S(2)}) collective-permute-start(f32[1,16,128]{2,1,0:T(8,128)S(1)} %get-tuple-element.43.refs_0_.rest_0_), channel_id=1, source_target_pairs={{0,32},{1,33},{2,34},{3,35},{4,36},{5,37},{6,38},{7,39},{8,40},{9,... | collective-permute-start | bytes 24584 | tf_op jit(solution)/shard_map/ppermute | solution.py:484
  10.4 0.8 %own_kernel.1 = (f32[2,16,128]{2,1,0:T(8,128)S(1)}, bf16[384,384]{1,0:T(8,128)(2,1)S(1)}, bf16[384,384]{1,0:T(8,128)(2,1)S(1)}, f32[3,16,128]{2,1,0:T(8,128)S(1)...) custom-call(f32[3,1,128]{2,1,0:T(1,128)S(1)} %get-tuple-element.28.pos, ...), custom_call_target="tpu_custom_call" | custom-call | flops 1048576 | bytes 779392 | tf_op jit(solution)/shard_map/own_kernel/pallas_call | solution.py:424
  11.2 0.0 collective-permute-done.refs_2_.rest_2_
  11.3 1.9 %collective-permute-start.1 = (f32[4,16,128]{2,1,0:T(8,128)S(1)}, f32[4,16,128]{2,1,0:T(8,128)S(1)}, u32[]{:S(2)}, u32[]{:S(2)}) collective-permute-start(f32[4,16,128]{2,1,0:T(8,128)S(1)} %relay_1.1), channel_id=1, source_target_pairs={{0,1},{1,0},{2,3},{3,2},{4,5},{5,4},{6,7},{7,6},{8,9},{9,8},{10,11... | collective-permute-start | bytes 98312 | tf_op jit(solution)/shard_map/ppermute | solution.py:484
  13.2 2.7 %collective-permute-done.1.refs_3_.rest_3_ = f32[4,16,128]{2,1,0:T(8,128)S(1)} collective-permute-done((f32[4,16,128]{2,1,0:T(8,128)S(1)}, f32[4,16,128]{2,1,0:T(8,128)S(1)}, u32[]{:S(2)}, u32[]{:S(2)}) %collective-permute-start.1) | collective-permute-done | bytes 32800 | tf_op jit(solution)/shard_map/ppermute | solution.py:484
  16.0 14.7 %collective-permute-start.2 = (f32[6,16,128]{2,1,0:T(8,128)S(1)}, f32[6,16,128]{2,1,0:T(8,128)S(1)}, u32[]{:S(2)}, u32[]{:S(2)}) collective-permute-start(f32[6,16,128]{2,1,0:T(8,128)S(1)} %relay_2.1), channel_id=1, source_target_pairs={{0,480},{1,481},{2,482},{3,483},{4,484},{5,485},{6,486},{7,487},{8... | collective-permute-start | bytes 147464 | tf_op jit(solution)/shard_map/ppermute | solution.py:484
  30.7 3.0 %collective-permute-done.2.refs_4_.rest_4_ = f32[6,16,128]{2,1,0:T(8,128)S(1)} collective-permute-done((f32[6,16,128]{2,1,0:T(8,128)S(1)}, f32[6,16,128]{2,1,0:T(8,128)S(1)}, u32[]{:S(2)}, u32[]{:S(2)}) %collective-permute-start.2) | collective-permute-done | bytes 49184 | tf_op jit(solution)/shard_map/ppermute | solution.py:484
  33.7 3.3 %collective-permute-start.3 = (f32[12,16,128]{2,1,0:T(8,128)S(1)}, f32[12,16,128]{2,1,0:T(8,128)S(1)}, u32[]{:S(2)}, u32[]{:S(2)}) collective-permute-start(f32[12,16,128]{2,1,0:T(8,128)S(1)} %relay_3.1), channel_id=1, source_target_pairs={{0,511},{1,2},{2,1},{3,484},{4,483},{5,6},{6,5},{7,488},{8,487},{9... | collective-permute-start | bytes 294920 | tf_op jit(solution)/shard_map/ppermute | solution.py:484
  37.0 2.9 %collective-permute-done.3.refs_5_.rest_5_ = f32[12,16,128]{2,1,0:T(8,128)S(1)} collective-permute-done((f32[12,16,128]{2,1,0:T(8,128)S(1)}, f32[12,16,128]{2,1,0:T(8,128)S(1)}, u32[]{:S(2)}, u32[]{:S(2)}) %collective-permute-start.3) | collective-permute-done | bytes 98336 | tf_op jit(solution)/shard_map/ppermute | solution.py:484
  40.0 3.0 %collective-permute-start.4 = (f32[8,16,128]{2,1,0:T(8,128)S(1)}, f32[8,16,128]{2,1,0:T(8,128)S(1)}, u32[]{:S(2)}, u32[]{:S(2)}) collective-permute-start(f32[8,16,128]{2,1,0:T(8,128)S(1)} %relay_4.1), channel_id=1, source_target_pairs={{0,32},{1,33},{2,34},{3,35},{4,36},{5,37},{6,38},{7,39},{8,40},{9,... | collective-permute-start | bytes 196616 | tf_op jit(solution)/shard_map/ppermute | solution.py:484
  43.0 0.9 %collective-permute-done.4.rest_6_.refs_6_ = f32[8,16,128]{2,1,0:T(8,128)S(1)} collective-permute-done((f32[8,16,128]{2,1,0:T(8,128)S(1)}, f32[8,16,128]{2,1,0:T(8,128)S(1)}, u32[]{:S(2)}, u32[]{:S(2)}) %collective-permute-start.4) | collective-permute-done | bytes 65568 | tf_op jit(solution)/shard_map/ppermute | solution.py:484
  43.9 1.9 %collective-permute-start.5 = (f32[9,16,128]{2,1,0:T(8,128)S(1)}, f32[9,16,128]{2,1,0:T(8,128)S(1)}, u32[]{:S(2)}, u32[]{:S(2)}) collective-permute-start(f32[9,16,128]{2,1,0:T(8,128)S(1)} %relay_5.1), channel_id=1, source_target_pairs={{0,1},{1,0},{2,3},{3,2},{4,5},{5,4},{6,7},{7,6},{8,9},{9,8},{10,11... | collective-permute-start | bytes 221192 | tf_op jit(solution)/shard_map/ppermute | solution.py:484
  45.8 2.4 %next_kernel.1 = (f32[3,8,128]{2,1,0:T(8,128)}, f32[3,8,128]{2,1,0:T(8,128)}, f32[3,16,128]{2,1,0:T(8,128)S(1)}, bf16[768,384]{1,0:T(8,128)(2,1)S(1)}, bf16[768,384]{1,0:T(8,128)(2,1)S(1)}) custom-call(f32[8,128]{1,0:T(8,128)S(1)} %get-tuple-element.36.place, f32[3,16,128]{2,1,0:T(8,128)S(1)} %get-tuple-element.37.state, ...), custom_call_target="tpu_custom_call" | custom-call | flops 1048576 | bytes 2186240 | tf_op jit(solution)/shard_map/next_kernel/pallas_call | solution.py:424
  48.2 0.8 %collective-permute-done.5.rest_7_ = f32[9,16,128]{2,1,0:T(8,128)S(1)} collective-permute-done((f32[9,16,128]{2,1,0:T(8,128)S(1)}, f32[9,16,128]{2,1,0:T(8,128)S(1)}, u32[]{:S(2)}, u32[]{:S(2)}) %collective-permute-start.5) | collective-permute-done | bytes 73760 | tf_op jit(solution)/shard_map/ppermute | solution.py:484
  49.0 2.1 %last_kernel.1 = (f32[3,8,128]{2,1,0:T(8,128)}, f32[3,8,128]{2,1,0:T(8,128)}) custom-call(f32[3,16,128]{2,1,0:T(8,128)S(1)} %get-tuple-element.46.third, bf16[768,384]{1,0:T(8,128)(2,1)S(1)} %get-tuple-element.47.far_high, bf16[768,384]{1,0:T(8,128)(2,1)S(1)} %get-tuple-element.48.far_low, f32[1,16,128]{2,1,0:T(8,128)S(1)} %get-tuple-element.43.refs_0_.rest_0_, ...), custom_call_target="tpu_custom_call" | custom-call | flops 1048576 | bytes 1581056 | tf_op jit(solution)/shard_map/last_kernel/pallas_call | solution.py:424
  (5 shorter events, 0.1 us)
Async XLA Ops:
  1.6 9.6 %collective-permute-start = (f32[1,16,128]{2,1,0:T(8,128)S(1)}, f32[1,16,128]{2,1,0:T(8,128)S(1)}, u32[]{:S(2)}, u32[]{:S(2)}) collective-permute-start(f32[1,16,128]{2,1,0:T(8,128)S(1)} %get-tuple-element.43.refs_0_.rest_0_), channel_id=1, source_target_pairs={{0,32},{1,33},{2,34},{3,35},{4,36},{5,37},{6,38},{7,39},{8,40},{9,... | collective-permute-start | bytes 24584 | tf_op jit(solution)/shard_map/ppermute | solution.py:484
  11.3 4.7 %collective-permute-start.1 = (f32[4,16,128]{2,1,0:T(8,128)S(1)}, f32[4,16,128]{2,1,0:T(8,128)S(1)}, u32[]{:S(2)}, u32[]{:S(2)}) collective-permute-start(f32[4,16,128]{2,1,0:T(8,128)S(1)} %relay_1.1), channel_id=1, source_target_pairs={{0,1},{1,0},{2,3},{3,2},{4,5},{5,4},{6,7},{7,6},{8,9},{9,8},{10,11... | collective-permute-start | bytes 98312 | tf_op jit(solution)/shard_map/ppermute | solution.py:484
  16.0 17.8 %collective-permute-start.2 = (f32[6,16,128]{2,1,0:T(8,128)S(1)}, f32[6,16,128]{2,1,0:T(8,128)S(1)}, u32[]{:S(2)}, u32[]{:S(2)}) collective-permute-start(f32[6,16,128]{2,1,0:T(8,128)S(1)} %relay_2.1), channel_id=1, source_target_pairs={{0,480},{1,481},{2,482},{3,483},{4,484},{5,485},{6,486},{7,487},{8... | collective-permute-start | bytes 147464 | tf_op jit(solution)/shard_map/ppermute | solution.py:484
  33.7 6.2 %collective-permute-start.3 = (f32[12,16,128]{2,1,0:T(8,128)S(1)}, f32[12,16,128]{2,1,0:T(8,128)S(1)}, u32[]{:S(2)}, u32[]{:S(2)}) collective-permute-start(f32[12,16,128]{2,1,0:T(8,128)S(1)} %relay_3.1), channel_id=1, source_target_pairs={{0,511},{1,2},{2,1},{3,484},{4,483},{5,6},{6,5},{7,488},{8,487},{9... | collective-permute-start | bytes 294920 | tf_op jit(solution)/shard_map/ppermute | solution.py:484
  40.0 3.9 %collective-permute-start.4 = (f32[8,16,128]{2,1,0:T(8,128)S(1)}, f32[8,16,128]{2,1,0:T(8,128)S(1)}, u32[]{:S(2)}, u32[]{:S(2)}) collective-permute-start(f32[8,16,128]{2,1,0:T(8,128)S(1)} %relay_4.1), channel_id=1, source_target_pairs={{0,32},{1,33},{2,34},{3,35},{4,36},{5,37},{6,38},{7,39},{8,40},{9,... | collective-permute-start | bytes 196616 | tf_op jit(solution)/shard_map/ppermute | solution.py:484
  43.9 5.1 %collective-permute-start.5 = (f32[9,16,128]{2,1,0:T(8,128)S(1)}, f32[9,16,128]{2,1,0:T(8,128)S(1)}, u32[]{:S(2)}, u32[]{:S(2)}) collective-permute-start(f32[9,16,128]{2,1,0:T(8,128)S(1)} %relay_5.1), channel_id=1, source_target_pairs={{0,1},{1,0},{2,3},{3,2},{4,5},{5,4},{6,7},{7,6},{8,9},{9,8},{10,11... | collective-permute-start | bytes 221192 | tf_op jit(solution)/shard_map/ppermute | solution.py:484

commit v7 on v6

--- a/solution.py
+++ b/solution.py
@@ -37,14 +37,12 @@
         return x, y ^ 1
 
     def across(x, y):
-        if x in (0, nx - 1):
-            return other(x, nx), y
-        return x, other(y, ny)
+        return other(x, nx), other(y, ny)
 
     def beside(x, y):
-        if x not in (0, nx - 1):
-            return other(x, nx), y
-        return (x if y % 4 in (1, 2) else other(x, nx)), other(y, ny)
+        if x in (0, nx - 1) and y % 4 in (1, 2):
+            return x, other(y, ny)
+        return other(x, nx), y
 
     return pair_x, pair_y, across, beside, pair_x, pair_y
 

time: 51.4 us -> 52.8 us (1.027)
  waiting for transfers between devices: 10.4 us -> 13.4 us
  starting transfers between devices: 33.6 us -> 32 us
    ppermute x6, waiting for transfers between devices: 10.4 us -> 13.4 us  [shards(): received.append(lax.ppermute(outgoing, ('gx', 'gy'), links[i]))]
    ppermute x6, starting transfers between devices: 33.6 us -> 32 us  [shards(): received.append(lax.ppermute(outgoing, ('gx', 'gy'), links[i]))]
where the time goes in v7:
time: 52.8 us; the launch traced here: 52.4 us
  starting transfers between devices  32 us (61%)
  waiting for transfers between devices  13.4 us (25%)
  Pallas kernels  6.37 us (12%)
  between operations  0.71 us (1%)
    ppermute x6, starting transfers between devices, shards(): received.append(lax.ppermute(outgoing, ('gx', 'gy'), links[i]))  32 us
    ppermute x6, waiting for transfers between devices, shards(): received.append(lax.ppermute(outgoing, ('gx', 'gy'), links[i]))  13.4 us
    pallas_call x9, Pallas kernels, call(): pl.pallas_call(kernel, out_shape=out_shape, in_specs=[pl.BlockSpec(memory...  6.37 us
  transfers between devices with their start and end apart: 6, of which 5 were waited for; matrix products, arithmetic and copies ran while one was open for 0% of the time, Pallas kernels for 6%

profile of v7, /device:TPU:1, one launch (start us, length us, event | category | flops | bytes accessed | tf_op | source)
XLA Modules:
  0.0 52.4 jit_solution(11601522566984311669)
XLA Ops:
  0.6 1.0 %pack_kernel.1 = (f32[1,16,128]{2,1,0:T(8,128)S(1)}, f32[3,1,128]{2,1,0:T(1,128)S(1)}, f32[1,128]{1,0:T(1,128)S(1)}, s32[1,32]{1,0:T(1,128)S(1)}, f32[3,8,128]{2...) custom-call(f32[3,1,128]{2,1,0:T(1,128)} %bitcast.25, ...), custom_call_target="tpu_custom_call" | custom-call | flops 1048576 | bytes 176384 | tf_op jit(solution)/shard_map/pack_kernel/pallas_call | solution.py:422
  1.6 8.7 %collective-permute-start = (f32[1,16,128]{2,1,0:T(8,128)S(1)}, f32[1,16,128]{2,1,0:T(8,128)S(1)}, u32[]{:S(2)}, u32[]{:S(2)}) collective-permute-start(f32[1,16,128]{2,1,0:T(8,128)S(1)} %get-tuple-element.43.refs_0_.rest_0_), channel_id=1, source_target_pairs={{0,32},{1,33},{2,34},{3,35},{4,36},{5,37},{6,38},{7,39},{8,40},{9,... | collective-permute-start | bytes 24584 | tf_op jit(solution)/shard_map/ppermute | solution.py:482
  10.4 0.8 %own_kernel.1 = (f32[2,16,128]{2,1,0:T(8,128)S(1)}, bf16[384,384]{1,0:T(8,128)(2,1)S(1)}, bf16[384,384]{1,0:T(8,128)(2,1)S(1)}, f32[3,16,128]{2,1,0:T(8,128)S(1)...) custom-call(f32[3,1,128]{2,1,0:T(1,128)S(1)} %get-tuple-element.28.pos, ...), custom_call_target="tpu_custom_call" | custom-call | flops 1048576 | bytes 779392 | tf_op jit(solution)/shard_map/own_kernel/pallas_call | solution.py:422
  11.2 0.0 collective-permute-done.refs_2_.rest_2_
  11.3 1.9 %collective-permute-start.1 = (f32[4,16,128]{2,1,0:T(8,128)S(1)}, f32[4,16,128]{2,1,0:T(8,128)S(1)}, u32[]{:S(2)}, u32[]{:S(2)}) collective-permute-start(f32[4,16,128]{2,1,0:T(8,128)S(1)} %relay_1.1), channel_id=1, source_target_pairs={{0,1},{1,0},{2,3},{3,2},{4,5},{5,4},{6,7},{7,6},{8,9},{9,8},{10,11... | collective-permute-start | bytes 98312 | tf_op jit(solution)/shard_map/ppermute | solution.py:482
  13.2 2.7 %collective-permute-done.1.refs_3_.rest_3_ = f32[4,16,128]{2,1,0:T(8,128)S(1)} collective-permute-done((f32[4,16,128]{2,1,0:T(8,128)S(1)}, f32[4,16,128]{2,1,0:T(8,128)S(1)}, u32[]{:S(2)}, u32[]{:S(2)}) %collective-permute-start.1) | collective-permute-done | bytes 32800 | tf_op jit(solution)/shard_map/ppermute | solution.py:482
  16.0 15.6 %collective-permute-start.2 = (f32[6,16,128]{2,1,0:T(8,128)S(1)}, f32[6,16,128]{2,1,0:T(8,128)S(1)}, u32[]{:S(2)}, u32[]{:S(2)}) collective-permute-start(f32[6,16,128]{2,1,0:T(8,128)S(1)} %relay_2.1), channel_id=1, source_target_pairs={{0,511},{1,482},{2,481},{3,484},{4,483},{5,486},{6,485},{7,488},{8... | collective-permute-start | bytes 147464 | tf_op jit(solution)/shard_map/ppermute | solution.py:482
  31.5 4.2 %collective-permute-done.2.refs_4_.rest_4_ = f32[6,16,128]{2,1,0:T(8,128)S(1)} collective-permute-done((f32[6,16,128]{2,1,0:T(8,128)S(1)}, f32[6,16,128]{2,1,0:T(8,128)S(1)}, u32[]{:S(2)}, u32[]{:S(2)}) %collective-permute-start.2) | collective-permute-done | bytes 49184 | tf_op jit(solution)/shard_map/ppermute | solution.py:482
  35.7 1.9 %collective-permute-start.3 = (f32[12,16,128]{2,1,0:T(8,128)S(1)}, f32[12,16,128]{2,1,0:T(8,128)S(1)}, u32[]{:S(2)}, u32[]{:S(2)}) collective-permute-start(f32[12,16,128]{2,1,0:T(8,128)S(1)} %relay_3.1), channel_id=1, source_target_pairs={{0,480},{1,2},{2,1},{3,483},{4,484},{5,6},{6,5},{7,487},{8,488},{9... | collective-permute-start | bytes 294920 | tf_op jit(solution)/shard_map/ppermute | solution.py:482
  37.6 4.0 %collective-permute-done.3.refs_5_.rest_5_ = f32[12,16,128]{2,1,0:T(8,128)S(1)} collective-permute-done((f32[12,16,128]{2,1,0:T(8,128)S(1)}, f32[12,16,128]{2,1,0:T(8,128)S(1)}, u32[]{:S(2)}, u32[]{:S(2)}) %collective-permute-start.3) | collective-permute-done | bytes 98336 | tf_op jit(solution)/shard_map/ppermute | solution.py:482
  41.6 1.9 %collective-permute-start.4 = (f32[8,16,128]{2,1,0:T(8,128)S(1)}, f32[8,16,128]{2,1,0:T(8,128)S(1)}, u32[]{:S(2)}, u32[]{:S(2)}) collective-permute-start(f32[8,16,128]{2,1,0:T(8,128)S(1)} %relay_4.1), channel_id=1, source_target_pairs={{0,32},{1,33},{2,34},{3,35},{4,36},{5,37},{6,38},{7,39},{8,40},{9,... | collective-permute-start | bytes 196616 | tf_op jit(solution)/shard_map/ppermute | solution.py:482
  43.6 1.2 %collective-permute-done.4.rest_6_.refs_6_ = f32[8,16,128]{2,1,0:T(8,128)S(1)} collective-permute-done((f32[8,16,128]{2,1,0:T(8,128)S(1)}, f32[8,16,128]{2,1,0:T(8,128)S(1)}, u32[]{:S(2)}, u32[]{:S(2)}) %collective-permute-start.4) | collective-permute-done | bytes 65568 | tf_op jit(solution)/shard_map/ppermute | solution.py:482
  44.8 1.9 %collective-permute-start.5 = (f32[9,16,128]{2,1,0:T(8,128)S(1)}, f32[9,16,128]{2,1,0:T(8,128)S(1)}, u32[]{:S(2)}, u32[]{:S(2)}) collective-permute-start(f32[9,16,128]{2,1,0:T(8,128)S(1)} %relay_5.1), channel_id=1, source_target_pairs={{0,1},{1,0},{2,3},{3,2},{4,5},{5,4},{6,7},{7,6},{8,9},{9,8},{10,11... | collective-permute-start | bytes 221192 | tf_op jit(solution)/shard_map/ppermute | solution.py:482
  46.7 2.4 %next_kernel.1 = (f32[3,8,128]{2,1,0:T(8,128)}, f32[3,8,128]{2,1,0:T(8,128)}, f32[3,16,128]{2,1,0:T(8,128)S(1)}, bf16[768,384]{1,0:T(8,128)(2,1)S(1)}, bf16[768,384]{1,0:T(8,128)(2,1)S(1)}) custom-call(f32[8,128]{1,0:T(8,128)S(1)} %get-tuple-element.36.place, f32[3,16,128]{2,1,0:T(8,128)S(1)} %get-tuple-element.37.state, ...), custom_call_target="tpu_custom_call" | custom-call | flops 1048576 | bytes 2186240 | tf_op jit(solution)/shard_map/next_kernel/pallas_call | solution.py:422
  49.1 1.3 %collective-permute-done.5.rest_7_ = f32[9,16,128]{2,1,0:T(8,128)S(1)} collective-permute-done((f32[9,16,128]{2,1,0:T(8,128)S(1)}, f32[9,16,128]{2,1,0:T(8,128)S(1)}, u32[]{:S(2)}, u32[]{:S(2)}) %collective-permute-start.5) | collective-permute-done | bytes 73760 | tf_op jit(solution)/shard_map/ppermute | solution.py:482
  50.3 2.1 %last_kernel.1 = (f32[3,8,128]{2,1,0:T(8,128)}, f32[3,8,128]{2,1,0:T(8,128)}) custom-call(f32[3,16,128]{2,1,0:T(8,128)S(1)} %get-tuple-element.46.third, bf16[768,384]{1,0:T(8,128)(2,1)S(1)} %get-tuple-element.47.far_high, bf16[768,384]{1,0:T(8,128)(2,1)S(1)} %get-tuple-element.48.far_low, f32[1,16,128]{2,1,0:T(8,128)S(1)} %get-tuple-element.43.refs_0_.rest_0_, ...), custom_call_target="tpu_custom_call" | custom-call | flops 1048576 | bytes 1581056 | tf_op jit(solution)/shard_map/last_kernel/pallas_call | solution.py:422
  (5 shorter events, 0.1 us)
Async XLA Ops:
  1.6 9.6 %collective-permute-start = (f32[1,16,128]{2,1,0:T(8,128)S(1)}, f32[1,16,128]{2,1,0:T(8,128)S(1)}, u32[]{:S(2)}, u32[]{:S(2)}) collective-permute-start(f32[1,16,128]{2,1,0:T(8,128)S(1)} %get-tuple-element.43.refs_0_.rest_0_), channel_id=1, source_target_pairs={{0,32},{1,33},{2,34},{3,35},{4,36},{5,37},{6,38},{7,39},{8,40},{9,... | collective-permute-start | bytes 24584 | tf_op jit(solution)/shard_map/ppermute | solution.py:482
  11.3 4.7 %collective-permute-start.1 = (f32[4,16,128]{2,1,0:T(8,128)S(1)}, f32[4,16,128]{2,1,0:T(8,128)S(1)}, u32[]{:S(2)}, u32[]{:S(2)}) collective-permute-start(f32[4,16,128]{2,1,0:T(8,128)S(1)} %relay_1.1), channel_id=1, source_target_pairs={{0,1},{1,0},{2,3},{3,2},{4,5},{5,4},{6,7},{7,6},{8,9},{9,8},{10,11... | collective-permute-start | bytes 98312 | tf_op jit(solution)/shard_map/ppermute | solution.py:482
  16.0 19.7 %collective-permute-start.2 = (f32[6,16,128]{2,1,0:T(8,128)S(1)}, f32[6,16,128]{2,1,0:T(8,128)S(1)}, u32[]{:S(2)}, u32[]{:S(2)}) collective-permute-start(f32[6,16,128]{2,1,0:T(8,128)S(1)} %relay_2.1), channel_id=1, source_target_pairs={{0,511},{1,482},{2,481},{3,484},{4,483},{5,486},{6,485},{7,488},{8... | collective-permute-start | bytes 147464 | tf_op jit(solution)/shard_map/ppermute | solution.py:482
  35.7 5.9 %collective-permute-start.3 = (f32[12,16,128]{2,1,0:T(8,128)S(1)}, f32[12,16,128]{2,1,0:T(8,128)S(1)}, u32[]{:S(2)}, u32[]{:S(2)}) collective-permute-start(f32[12,16,128]{2,1,0:T(8,128)S(1)} %relay_3.1), channel_id=1, source_target_pairs={{0,480},{1,2},{2,1},{3,483},{4,484},{5,6},{6,5},{7,487},{8,488},{9... | collective-permute-start | bytes 294920 | tf_op jit(solution)/shard_map/ppermute | solution.py:482
  41.6 3.1 %collective-permute-start.4 = (f32[8,16,128]{2,1,0:T(8,128)S(1)}, f32[8,16,128]{2,1,0:T(8,128)S(1)}, u32[]{:S(2)}, u32[]{:S(2)}) collective-permute-start(f32[8,16,128]{2,1,0:T(8,128)S(1)} %relay_4.1), channel_id=1, source_target_pairs={{0,32},{1,33},{2,34},{3,35},{4,36},{5,37},{6,38},{7,39},{8,40},{9,... | collective-permute-start | bytes 196616 | tf_op jit(solution)/shard_map/ppermute | solution.py:482
  44.8 5.6 %collective-permute-start.5 = (f32[9,16,128]{2,1,0:T(8,128)S(1)}, f32[9,16,128]{2,1,0:T(8,128)S(1)}, u32[]{:S(2)}, u32[]{:S(2)}) collective-permute-start(f32[9,16,128]{2,1,0:T(8,128)S(1)} %relay_5.1), channel_id=1, source_target_pairs={{0,1},{1,0},{2,3},{3,2},{4,5},{5,4},{6,7},{7,6},{8,9},{9,8},{10,11... | collective-permute-start | bytes 221192 | tf_op jit(solution)/shard_map/ppermute | solution.py:482
